TPU v7x, 32 devices: a whole 2x2x4 slice. The times are simulated.
32 devices in a mesh: tower: 2 (over x), dp: 16 (over z, y, core).
Axes of the slice: x: 2, y: 2, z: 4, core: 2. Of those that a mesh axis runs over, the one named last changes fastest.
Arguments:
- tokens: bfloat16 [2, 16384, 768], P('tower', 'dp'), may hold values from -6 to 6
- segments: int32 [2, 128, 128], P('tower', 'dp'), may hold values from 0 to 7, as said below
- pairs: int32 [1024], replicated, may hold values from 0 to 1023, as said below
- scores: float32 [1024], replicated, may hold values from -0.5 to 1
- w_qkv: bfloat16 [768, 2304], replicated, may hold values from -0.21875 to 0.21875
- b_query: float32 [768], replicated, may hold values from -1.75 to 1.75
- b_value: float32 [768], replicated, may hold values from -3 to 3
- w_out: bfloat16 [768, 768], replicated, may hold values from -0.4375 to 0.4375
- b_out: float32 [768], replicated, may hold values from -3 to 3
- gain_one: float32 [768], replicated, may hold values from 0.25 to 1.75
- shift_one: float32 [768], replicated, may hold values from -1.25 to 1.25
- w_in: bfloat16 [768, 3072], replicated, may hold values from -0.21875 to 0.21875
- b_in: float32 [3072], replicated, may hold values from -3 to 3
- w_down: bfloat16 [3072, 768], replicated, may hold values from -0.109375 to 0.109375
- b_down: float32 [768], replicated, may hold values from -3 to 3
- gain_two: float32 [768], replicated, may hold values from 0.25 to 1.75
- shift_two: float32 [768], replicated, may hold values from -0.625 to 0.625
Outputs:
- output_rows: bfloat16 [2, 16384, 768], P('tower', 'dp')
- grad_tokens: float32 [2, 16384, 768], P('tower', 'dp')
- grad_w_qkv: float32 [768, 2304], replicated
- grad_b_query: float32 [768], replicated
- grad_b_value: float32 [768], replicated
- grad_w_out: float32 [768, 768], replicated
- grad_b_out: float32 [768], replicated
- grad_gain_one: float32 [768], replicated
- grad_shift_one: float32 [768], replicated
- grad_w_in: float32 [768, 3072], replicated
- grad_b_in: float32 [3072], replicated
- grad_w_down: float32 [3072, 768], replicated
- grad_b_down: float32 [768], replicated
- grad_gain_two: float32 [768], replicated
- grad_shift_two: float32 [768], replicated
Inputs may be any that keep to these rules, and one draw needn't show every extreme that they name: `segments`: within each packed row the numbers never fall along the row and run from 0 to 7, each one present. `pairs`: every B sentence is the partner of exactly one A sentence.
All inputs are finite; a program needn't handle non-finite values.
Results may differ from a plain program's by a relative error of at most 0.008.
Values may be sent and summed in bfloat16 or wider, within the bound.
No kernel may reach another device: no remote copies, remote signals or barrier semaphores. Data moves between devices by JAX's collectives and lax.ppermute only.
A program may use at most 256 MiB of HBM per device.

v0:
```python
import math

import jax
import jax.numpy as jnp
from jax import lax
from jax.sharding import PartitionSpec as P

HEADS = 12
SEG_ROW = 8


loss_scale = 65536.0


def gelu_exact(values_in):
    return jax.nn.gelu(values_in, approximate=False)


def layer_norm(values_in, gain_vec, shift_vec):
    row_mean = jnp.mean(values_in, -1, keepdims=True)
    centered = values_in - row_mean
    inv_std = lax.rsqrt(jnp.mean(centered * centered, -1, keepdims=True) + 1e-12)
    normed = centered * inv_std
    return (normed * gain_vec + shift_vec, normed, inv_std)


def norm_back(gradient, normed, inv_std, gain_vec):
    scaled = gradient * gain_vec
    inner = (
        scaled
        - jnp.mean(scaled, -1, keepdims=True)
        - normed * jnp.mean(scaled * normed, -1, keepdims=True)
    )
    return (inner * inv_std, jnp.sum(gradient * normed, 0), jnp.sum(gradient, 0))


def on_device(
    tokens,
    segments,
    pairs,
    scores,
    w_qkv,
    b_query,
    b_value,
    w_out,
    b_out,
    gain_one,
    shift_one,
    w_in,
    b_in,
    w_down,
    b_down,
    gain_two,
    shift_two,
):
    f32 = jnp.float32
    bf16 = jnp.bfloat16
    flat_rows = tokens[0]
    seg_rows = segments[0]
    row_count = seg_rows.shape[0]
    row_len = seg_rows.shape[1]
    model_width = flat_rows.shape[1]
    token_count = flat_rows.shape[0]
    head_dim = model_width // HEADS
    head_shape = (row_count, row_len, HEADS, head_dim)
    score_scale = 1.0 / math.sqrt(head_dim)
    joint_rows = jnp.dot(flat_rows, w_qkv, preferred_element_type=f32)
    query_rows = (joint_rows[:, :model_width] + b_query).astype(bf16).reshape(head_shape)
    key_rows = joint_rows[:, model_width : 2 * model_width].astype(bf16).reshape(head_shape)
    value_rows = (joint_rows[:, 2 * model_width :] + b_value).astype(bf16).reshape(head_shape)
    same_segment = (seg_rows[:, :, None] == seg_rows[:, None, :])[:, None]

    def score_of():
        raw = (
            jnp.einsum("rqhd,rkhd->rhqk", query_rows, key_rows, preferred_element_type=f32)
            * score_scale
        )
        return jnp.where(same_segment, raw, -1e30)

    scores_now = score_of()
    row_max = jnp.max(scores_now, -1, keepdims=True)
    expo = jnp.exp(scores_now - row_max)
    denom = jnp.sum(expo, -1, keepdims=True)
    log_total = row_max + jnp.log(denom)
    attn_low = (expo / denom).astype(bf16)
    context = jnp.einsum("rhqk,rkhd->rqhd", attn_low, value_rows, preferred_element_type=f32)
    context = context.astype(bf16).reshape(token_count, model_width)
    attended = jnp.dot(context, w_out, preferred_element_type=f32) + b_out
    hidden, normed_one, inv_std_one = layer_norm(
        flat_rows.astype(f32) + attended, gain_one, shift_one
    )
    hidden_low = hidden.astype(bf16)
    up_rows = jnp.dot(hidden_low, w_in, preferred_element_type=f32) + b_in
    gelu_value, gelu_back = jax.vjp(gelu_exact, up_rows)
    activated = gelu_value.astype(bf16)
    down_rows = jnp.dot(activated, w_down, preferred_element_type=f32) + b_down
    output_rows, normed_two, inv_std_two = layer_norm(hidden + down_rows, gain_two, shift_two)
    onehot = (seg_rows[:, :, None] == jnp.arange(SEG_ROW, dtype=jnp.int32)[None, None, :]).astype(
        f32
    )
    counts = jnp.sum(onehot, 1)
    seg_sums = jnp.einsum(
        "rts,rtd->rsd",
        onehot,
        output_rows.reshape(row_count, row_len, model_width),
        precision=lax.Precision.HIGHEST,
    )
    seg_count = row_count * SEG_ROW
    pooled_low = (seg_sums / counts[:, :, None]).reshape(seg_count, model_width).astype(bf16)
    tower_index = lax.axis_index("tower")
    row_block = lax.axis_index("dp")
    pair_count = pairs.shape[0]
    everyone = lax.all_gather(pooled_low, ("tower", "dp"), axis=0, tiled=True)
    other_side = lax.dynamic_slice_in_dim(everyone, (1 - tower_index) * pair_count, pair_count, 0)
    own_index = row_block * seg_count + jnp.arange(seg_count, dtype=jnp.int32)
    inverse = (
        jnp.zeros((pair_count,), jnp.int32).at[pairs].set(jnp.arange(pair_count, dtype=jnp.int32))
    )
    back_pick = inverse[own_index]
    partner_index = jnp.where(tower_index == 0, pairs[own_index], back_pick)
    target_index = jnp.where(tower_index == 0, own_index, back_pick)
    partner = other_side[partner_index].astype(f32)
    target = scores[target_index]
    mine = pooled_low.astype(f32)
    inv_mine = lax.rsqrt(jnp.sum(mine * mine, -1) + 1e-06)
    inv_partner = lax.rsqrt(jnp.sum(partner * partner, -1) + 1e-06)
    cosine = jnp.sum(mine * partner, -1) * inv_mine * inv_partner
    coeff = loss_scale * 2.0 * (cosine - target) / pair_count
    d_pooled = coeff[:, None] * (
        partner * (inv_mine * inv_partner)[:, None] - (cosine * inv_mine * inv_mine)[:, None] * mine
    )
    per_token = d_pooled.reshape(row_count, SEG_ROW, model_width) / counts[:, :, None]
    d_output = jnp.einsum(
        "rts,rsd->rtd", onehot, per_token, precision=lax.Precision.HIGHEST
    ).reshape(token_count, model_width)
    d_mid, grad_gain_two, grad_shift_two = norm_back(d_output, normed_two, inv_std_two, gain_two)
    grad_b_down = jnp.sum(d_mid, 0)
    d_mid_low = d_mid.astype(bf16)
    grad_w_down = jnp.einsum("nf,nd->fd", activated, d_mid_low, preferred_element_type=f32)
    d_act = jnp.einsum("nd,fd->nf", d_mid_low, w_down, preferred_element_type=f32)
    d_up = gelu_back(d_act)[0]
    grad_b_in = jnp.sum(d_up, 0)
    d_up_low = d_up.astype(bf16)
    grad_w_in = jnp.einsum("nd,nf->df", hidden_low, d_up_low, preferred_element_type=f32)
    d_hidden = d_mid + jnp.einsum("nf,df->nd", d_up_low, w_in, preferred_element_type=f32)
    d_first, grad_gain_one, grad_shift_one = norm_back(d_hidden, normed_one, inv_std_one, gain_one)
    grad_b_out = jnp.sum(d_first, 0)
    d_first_low = d_first.astype(bf16)
    grad_w_out = jnp.einsum("nc,nd->cd", context, d_first_low, preferred_element_type=f32)
    d_context = jnp.einsum("nd,cd->nc", d_first_low, w_out, preferred_element_type=f32)
    d_context = d_context.astype(bf16).reshape(head_shape)
    attn_again = jnp.exp(score_of() - log_total)
    attn_again_low = attn_again.astype(bf16)
    d_values = jnp.einsum("rhqk,rqhd->rkhd", attn_again_low, d_context, preferred_element_type=f32)
    d_attn = jnp.einsum("rqhd,rkhd->rhqk", d_context, value_rows, preferred_element_type=f32)
    d_scores = attn_again * (d_attn - jnp.sum(attn_again * d_attn, -1, keepdims=True))
    d_scores_low = d_scores.astype(bf16)
    d_query = (
        jnp.einsum("rhqk,rkhd->rqhd", d_scores_low, key_rows, preferred_element_type=f32)
        * score_scale
    )
    d_keys = (
        jnp.einsum("rhqk,rqhd->rkhd", d_scores_low, query_rows, preferred_element_type=f32)
        * score_scale
    )
    d_query = d_query.reshape(token_count, model_width)
    d_keys = d_keys.reshape(token_count, model_width)
    d_values = d_values.reshape(token_count, model_width)
    grad_b_query = jnp.sum(d_query, 0)
    grad_b_value = jnp.sum(d_values, 0)
    d_joint = jnp.concatenate([d_query, d_keys, d_values], -1).astype(bf16)
    grad_w_qkv = jnp.einsum("nd,ne->de", flat_rows, d_joint, preferred_element_type=f32)
    grad_tokens = d_first + jnp.einsum("ne,de->nd", d_joint, w_qkv, preferred_element_type=f32)
    (
        grad_w_qkv,
        grad_b_query,
        grad_b_value,
        grad_w_out,
        grad_b_out,
        grad_gain_one,
        grad_shift_one,
        grad_w_in,
        grad_b_in,
        grad_w_down,
        grad_b_down,
        grad_gain_two,
        grad_shift_two,
    ) = lax.psum(
        (
            grad_w_qkv,
            grad_b_query,
            grad_b_value,
            grad_w_out,
            grad_b_out,
            grad_gain_one,
            grad_shift_one,
            grad_w_in,
            grad_b_in,
            grad_w_down,
            grad_b_down,
            grad_gain_two,
            grad_shift_two,
        ),
        ("tower", "dp"),
    )
    return (
        output_rows.astype(bf16)[None],
        grad_tokens[None],
        grad_w_qkv,
        grad_b_query,
        grad_b_value,
        grad_w_out,
        grad_b_out,
        grad_gain_one,
        grad_shift_one,
        grad_w_in,
        grad_b_in,
        grad_w_down,
        grad_b_down,
        grad_gain_two,
        grad_shift_two,
    )


def solution(mesh):
    return jax.shard_map(
        on_device,
        mesh=mesh,
        in_specs=(
            P("tower", "dp", None),
            P("tower", "dp", None),
            P(),
            P(),
            P(),
            P(),
            P(),
            P(),
            P(),
            P(),
            P(),
            P(),
            P(),
            P(),
            P(),
            P(),
            P(),
        ),
        out_specs=(
            P("tower", "dp", None),
            P("tower", "dp", None),
            P(),
            P(),
            P(),
            P(),
            P(),
            P(),
            P(),
            P(),
            P(),
            P(),
            P(),
            P(),
            P(),
        ),
        check_vma=False,
    )
```

profile of v0, /device:TPU:0, one launch (start us, length us, event | category | flops | bytes accessed | tf_op | source)
XLA Modules:
  0.0 731.7 jit_solution(16902538640138594596)
XLA Ops:
  10.4 5.2 fusion.28
  19.2 2.8 copy.45
  22.1 3.1 copy.70
  25.1 2.6 copy.47
  27.7 3.0 copy.72
  30.7 2.6 copy.46
  47.0 35.3 %multiply_convert_fusion = (bf16[1024,3072]{1,0:T(8,128)(2,1)S(1)}, f32[1024,3072]{1,0:T(8,128)}, f32[1024,3072]{1,0:T(8,128)}) fusion(f32[3072]{0:T(1024)S(1)} %copy-done.46, bf16[768,3072]{1,0:T(8,128)(2,1)S(1)} %bitcast.168, f32[1024,768]{1,0:T(8,128)S(1)} %get-tuple-element.86, f32[768]{0:T(1024)S(1)} %copy-done.34, f32[768]{0:T(1024)S(1)} %copy-done.28, ...), kind=kOutput, calls=%fused_computation.8 | convolution fusion | flops 5043388416 | bytes 39348224 | tf_op jit(solution)/shard_map/dot_general | solution.py:93
  82.3 5.4 fusion.80
  95.4 4.6 scatter_custom_fusion
  108.7 45.4 %all-gather.2.cloned.1.call-done = bf16[2048,768]{1,0:T(8,128)(2,1)} async-done(((bf16[64,768]{1,0:T(8,128)(2,1)}), bf16[2048,768]{1,0:T(8,128)(2,1)}) %all-gather.2.cloned.1.call-update) | async-done | bytes 3145744 | tf_op jit(solution)/shard_map/all_gather | solution.py:113
  154.1 2.7 constant_dynamic-slice_fusion
  156.7 3.1 gather_fusion.2
  165.3 3.4 fusion.74
  172.2 7.7 %fusion.47 = f32[3072,768]{1,0:T(8,128)} fusion(bf16[1024,3072]{1,0:T(8,128)(2,1)S(1)} %bitcast.170, f32[1024,768]{1,0:T(8,128)S(1)} %get-tuple-element.69), kind=kOutput, calls=%fused_computation.99 | convolution fusion | flops 4832624640 | bytes 18874368 | tf_op jit(solution)/shard_map/nf,nd->fd/dot_general | solution.py:139
  180.0 19.2 %fusion.81 = (f32[3072]{0:T(1024)}, bf16[1024,3072]{1,0:T(8,128)(2,1)}) fusion(f32[1024,3072]{1,0:T(8,128)} %get-tuple-element.75, bf16[3072,768]{1,0:T(8,128)(2,1)} %param.30, f32[1024,768]{1,0:T(8,128)} %copy-done.16, f32[1024,3072]{1,0:T(8,128)} %get-tuple-element.87, f32[3072]{0:T(1024)S(1)} %copy-done.47), kind=kOutput, calls=%fused_computation.162 | convolution fusion | flops 4882953216 | bytes 39346176 | tf_op jit(solution)/shard_map/nd,fd->nf/dot_general | solution.py:140
  199.2 11.6 %multiply_reduce_fusion.1 = (f32[768]{0:T(1024)}, f32[1024]{0:T(1024)S(1)}, f32[1024]{0:T(1024)S(1)}, f32[768]{0:T(1024)}, f32[1024,768]{1,0:T(8,128)S(1)}) fusion(f32[1024,768]{1,0:T(8,128)} %copy-done.6, f32[1024]{0:T(1024)S(1)} %add_rsqrt_fusion.2, f32[1024]{0:T(1024)S(1)} %broadcast_multiply_fusion.4, f32[768]{0:T(1024)S(1)} %copy-done.29, ...), kind=kOutput, calls=%fused_computation.44 | convolution fusion | flops 4839698432 | bytes 20472832 | tf_op jit(solution)/shard_map/nf,df->nd/dot_general | solution.py:145
  210.8 8.9 %fusion.14 = f32[768,3072]{1,0:T(8,128)} fusion(bf16[1024,3072]{1,0:T(8,128)(2,1)S(1)} %copy-done.8, f32[1024,768]{1,0:T(8,128)S(1)} %copy-done.7, f32[768]{0:T(1024)S(1)} %copy-done.35, f32[768]{0:T(1024)S(1)} %copy-done.29, f32[1024]{0:T(1024)S(1)} %add_rsqrt_fusion.2, f32[1024]{0:T(1024)S(1)} %broadcast_multiply_fusion.4), kind=kOutput, calls=%fused_computation.50 | convolution fusion | flops 4835770368 | bytes 18888704 | tf_op jit(solution)/shard_map/nd,nf->df/dot_general | solution.py:144
  221.5 2.8 fusion.24
  224.3 2.6 convolution_convert_fusion
  226.9 2.6 copy.53
  231.4 6.8 bitcast_convert_fusion
  238.2 7.3 %multiply_reduce_fusion = (f32[8,12,128]{2,1,0:T(8,128)S(1)}, f32[8,12,128,128]{2,3,1,0:T(8,128)}) fusion(f32[8,12,128,128]{2,3,1,0:T(8,128)} %copy-done.1, f32[8,12,128]{2,1,0:T(8,128)S(1)} %copy-done.19, bf16[8,128,12,64]{1,0,3,2:T(8,128)(2,1)S(1)} %bitcast.157, bf16[8,128,12,64]{1,0,3,2:T(8,128)(2,1)S(1)} %bitcast.141), kind=kOutput, calls=%fused_computation.23 | convolution fusion | flops 206032896 | bytes 15826944 | tf_op jit(solution)/shard_map/rqhd,rkhd->rhqk/dot_general | solution.py:155
  245.6 4.9 multiply_convert_fusion.1
  252.7 2.7 bitcast_convert_fusion.1
  262.7 5.8 convolution_bitcast_fusion
  274.5 41.7 %all-reduce = (f32[768]{0:T(1024)}, f32[768]{0:T(1024)}, f32[768]{0:T(1024)}, f32[768]{0:T(1024)}, f32[768]{0:T(1024)}, /*index=5*/f32[3072]{0:T(1024)}, f32[768]{0:T(1024)}, f32[768]{0:T(1024)}, f32[768]{0:T(1024)}) all-reduce(f32[768]{0:T(1024)} %reduce_sum.226, ...), channel_id=1, replica_groups=mesh['tower'=2,'dp'=16] {'tower','dp'}, use_global_device_ids=true, to_apply=%region_18.19 | all-reduce | flops 9216 | bytes 73728 | tf_op jit(solution)/shard_map/psum | solution.py:188
  316.2 8.5 %add_bitcast_fusion = f32[1,1024,768]{2,1,0:T(8,128)} fusion(f32[1024,768]{1,0:T(8,128)} %copy-done.15, bf16[1024,2304]{0,1:T(8,128)(2,1)} %copy-done.20, bf16[768,2304]{1,0:T(8,128)(2,1)S(1)} %copy-done), kind=kOutput, calls=%fused_computation.45 | convolution fusion | flops 3624665088 | bytes 14548992 | tf_op jit(solution)/shard_map/ne,de->nd/dot_general | solution.py:173
  324.7 376.1 %all-reduce.4.cloned.1.call-done = (f32[768,2304]{0,1:T(8,128)}, f32[768,768]{1,0:T(8,128)}, f32[768,3072]{1,0:T(8,128)}, f32[3072,768]{1,0:T(8,128)}) async-done(((f32[768,2304]{0,1:T(8,128)}, f32[768,768]{1,0:T(8,128)}, f32[768,3072]{1,0:T(8,128)}, f32[3072,768]{1,0:T(8,128)}), (f32[768,2304]{0,1:T(8,128)}, f32[768,768]{1,0:T(8,128)}, f32[768,3072]{1,0:T(8,128)}, ...) | async-done | bytes 28311568 | tf_op jit(solution)/shard_map/psum | solution.py:188
  700.8 8.0 %copy.65 = f32[768,2304]{1,0:T(8,128)} copy(f32[768,2304]{0,1:T(8,128)} %get-tuple-element.64) | data formatting | bytes 14155776
  708.8 3.4 copy.125
  712.1 8.8 %copy.126 = f32[768,3072]{1,0:T(8,128)} copy(f32[768,3072]{1,0:T(8,128)} %get-tuple-element.113) | data formatting | bytes 18874368
  720.9 3.7 copy.127
  (186 shorter events, 64.5 us)
Async XLA Ops:
  7.2 3.2 copy-start
  7.2 146.9 %all-gather.2.cloned.1.call-start = ((), (), s32[]{:S(2)}) async-start(), calls=%async_computation | async-start | bytes 3244032 | tf_op jit(solution)/shard_map/all_gather | solution.py:113
  42.1 2.9 slice-start.7
  42.6 39.7 %slice-start.5 = ((s8[4718592]{0:T(1024)(128)(4,1)}), s8[4194304]{0:T(1024)(128)(4,1)S(1)}, s32[]{:S(2)}) async-start(s8[4718592]{0:T(1024)(128)(4,1)} %bitcast.165), calls=%async_computation.7 | async-start | bytes 8388608
  44.3 38.0 %copy-start.6 = (f32[1024,768]{1,0:T(8,128)}, f32[1024,768]{1,0:T(8,128)S(1)}, u32[]{:S(2)}) copy-start(f32[1024,768]{1,0:T(8,128)S(1)} %get-tuple-element.86) | copy-start | bytes 9437188
  47.0 35.3 %slice-start.6 = ((s8[4718592]{0:T(1024)(128)(4,1)}), s8[524288]{0:T(1024)(128)(4,1)S(1)}, s32[]{:S(2)}) async-start(s8[4718592]{0:T(1024)(128)(4,1)} %bitcast.165), calls=%async_computation.8 | async-start | bytes 1048576
  47.0 35.3 %copy-start.49 = (f32[768]{0:T(1024)S(1)}, f32[768]{0:T(1024)}, u32[]{:S(2)}) copy-start(f32[768]{0:T(1024)} %param.31) | copy-start | bytes 9220
  82.3 5.5 copy-start.50
  90.3 12.9 %copy-start.3 = (f32[1024]{0:T(1024)S(1)}, f32[1024]{0:T(1024)}, u32[]{:S(2)}) copy-start(f32[1024]{0:T(1024)} %param.20) | copy-start | bytes 12292
  92.2 608.6 %all-reduce.4.cloned.1.call-start = ((), (), s32[]{:S(2)}) async-start(), calls=%async_computation.1 | async-start | bytes 56623104 | tf_op jit(solution)/shard_map/psum | solution.py:188
  101.4 63.9 %copy-start.25 = (s32[1,8,128]{2,1,0:T(8,128)S(1)}, s32[1,8,128]{2,1,0:T(8,128)}, u32[]{:S(2)}) copy-start(s32[1,8,128]{2,1,0:T(8,128)} %param.18) | copy-start | bytes 12292
  108.7 60.0 %copy-start.27 = (f32[1024]{0:T(1024)S(1)}, f32[1024]{0:T(1024)}, u32[]{:S(2)}) copy-start(f32[1024]{0:T(1024)} %copy-done.26) | copy-start | bytes 12292
  164.4 4.3 copy-start.5
  164.4 4.3 copy-start.31
  164.4 4.3 copy-start.33
  168.7 3.6 slice-start.9
  172.2 7.7 %copy-start.16 = (f32[1024,768]{1,0:T(8,128)}, f32[1024,768]{1,0:T(8,128)S(1)}, u32[]{:S(2)}) copy-start(f32[1024,768]{1,0:T(8,128)S(1)} %get-tuple-element.69) | copy-start | bytes 9437188
  172.2 7.7 %copy-start.47 = (f32[3072]{0:T(1024)S(1)}, f32[3072]{0:T(1024)}, u32[]{:S(2)}) copy-start(f32[3072]{0:T(1024)} %param.29) | copy-start | bytes 36868
  179.9 19.2 %copy-start.29 = (f32[768]{0:T(1024)S(1)}, f32[768]{0:T(1024)}, u32[]{:S(2)}) copy-start(f32[768]{0:T(1024)} %param.26) | copy-start | bytes 9220
  199.2 11.6 %copy-start.7 = (f32[1024,768]{1,0:T(8,128)S(1)}, f32[1024,768]{1,0:T(8,128)}, u32[]{:S(2)}) copy-start(f32[1024,768]{1,0:T(8,128)} %copy-done.6) | copy-start | bytes 9437188
  199.2 11.6 %copy-start.8 = (bf16[1024,3072]{1,0:T(8,128)(2,1)S(1)}, bf16[1024,3072]{1,0:T(8,128)(2,1)}, u32[]{:S(2)}) copy-start(bf16[1024,3072]{1,0:T(8,128)(2,1)} %get-tuple-element.99) | copy-start | bytes 18874372
  199.2 11.6 %copy-start.35 = (f32[768]{0:T(1024)S(1)}, f32[768]{0:T(1024)}, u32[]{:S(2)}) copy-start(f32[768]{0:T(1024)} %param.27) | copy-start | bytes 9220
  231.4 6.8 copy-start.14
  231.4 14.2 %slice-start = ((s8[6291456]{0:T(1024)(128)(4,1)}), s8[4194304]{0:T(1024)(128)(4,1)S(1)}, s32[]{:S(2)}) async-start(s8[6291456]{0:T(1024)(128)(4,1)} %bitcast.138), calls=%async_computation.2 | async-start | bytes 8388608
  238.2 7.4 %slice-start.1 = ((s8[6291456]{0:T(1024)(128)(4,1)}), s8[2097152]{0:T(1024)(128)(4,1)S(1)}, s32[]{:S(2)}) async-start(s8[6291456]{0:T(1024)(128)(4,1)} %bitcast.138), calls=%async_computation.3 | async-start | bytes 4194304
  245.6 4.9 copy-start.12
  259.7 3.0 copy-start.43
  268.6 5.9 copy-start.37
  268.6 5.9 copy-start.38
  708.8 12.1 %slice-start.2 = ((s8[9437184]{0:T(1024)(128)(4,1)}), s8[4194304]{0:T(1024)(128)(4,1)S(1)}, s32[]{:S(2)}) async-start(s8[9437184]{0:T(1024)(128)(4,1)} %bitcast.143), calls=%async_computation.4 | async-start | bytes 8388608
  712.1 8.8 %slice-start.3 = ((s8[9437184]{0:T(1024)(128)(4,1)}), s8[4194304]{0:T(1024)(128)(4,1)S(1)}, s32[]{:S(2)}) async-start(s8[9437184]{0:T(1024)(128)(4,1)} %bitcast.143), calls=%async_computation.5 | async-start | bytes 8388608
  712.1 8.8 %slice-start.4 = ((s8[9437184]{0:T(1024)(128)(4,1)}), s8[1048576]{0:T(1024)(128)(4,1)S(1)}, s32[]{:S(2)}) async-start(s8[9437184]{0:T(1024)(128)(4,1)} %bitcast.143), calls=%async_computation.6 | async-start | bytes 2097152
  (32 other events, 66.1 us)
Sparse Core Ops, SparseCore 0:
  92.3 61.7 all-gather.1
  268.7 432.0 all-reduce.3
where the time goes:
time: 736 us; the launch traced here: 732 us
  waiting for transfers between devices  422 us (57%)
  matrix products  142 us (19%)
  local copies, waits for them, and re-layouts  77.2 us (10%)
  blocking collectives  41.7 us (6%)
  other arithmetic  34.4 us (5%)
  between operations  14.9 us (2%)
    psum x1, waiting for transfers between devices, on_device(): lax.psum((grad_w_qkv, grad_b_query, grad_b_value, grad_w_out, grad_b_out,...  376 us
    all_gather x1, waiting for transfers between devices, on_device(): everyone = lax.all_gather(pooled_low, ('tower', 'dp'), axis=0, tiled=True)  45.4 us
    psum x1, blocking collectives, on_device(): lax.psum((grad_w_qkv, grad_b_query, grad_b_value, grad_w_out, grad_b_out,...  41.7 us
    unnamed x134, local copies, waits for them, and re-layouts  40.9 us
    dot_general x1, matrix products, on_device(): up_rows = jnp.dot(hidden_low, w_in, preferred_element_type=f32) + b_in  35.3 us
    dot_general x1, matrix products, on_device(): jnp.einsum('nd,fd->nf', d_mid_low, w_down, preferred_element_type=f32)  19.2 us
  transfers between devices with their start and end apart: 2, of which 2 were waited for; matrix products, arithmetic and copies ran while one was open for 4% of the time, Pallas kernels for 0%

commit v1 on v0

--- a/solution.py
+++ b/solution.py
@@ -1,15 +1,245 @@
 import math
+from functools import partial
 
 import jax
 import jax.numpy as jnp
 from jax import lax
+from jax.experimental import pallas as pl
+from jax.experimental.pallas import tpu as pltpu
 from jax.sharding import PartitionSpec as P
 
 HEADS = 12
 SEG_ROW = 8
-
+AXES = ("tower", "dp")
+HOPS = ((8, 2, 4, 1), (1, 8, 2, 4))
+POOL_HOPS = ((1, 4, 2), (4, 2, 1))
 
 loss_scale = 65536.0
+f32 = jnp.float32
+bf16 = jnp.bfloat16
+LIMIT = 56 << 20
+
+
+def call_params():
+    return pltpu.CompilerParams(vmem_limit_bytes=LIMIT)
+
+
+def hop_pairs(dp_size, flip):
+    result = []
+    for device in range(2 * dp_size):
+        tower, place = divmod(device, dp_size)
+        tower_bit, place_bits = flip(place & 1)
+        result.append((device, (tower ^ tower_bit) * dp_size + (place ^ place_bits)))
+    return result
+
+
+def swap_hop(value, dp_size, masks):
+    pairs = hop_pairs(dp_size, lambda core: (masks[core] >> 3, (masks[core] & 7) << 1))
+    return lax.ppermute(value, AXES, pairs)
+
+
+def swap_core(value, dp_size):
+    return lax.ppermute(value, AXES, hop_pairs(dp_size, lambda core: (0, 1)))
+
+
+def swap_place(value, dp_size, bits):
+    return lax.ppermute(value, AXES, hop_pairs(dp_size, lambda core: (0, bits)))
+
+
+def span(masks):
+    result = [0]
+    for mask in reversed(masks):
+        result = result + [mask ^ entry for entry in result]
+    return result
+
+
+def place_tables(dp_size):
+    tower = lax.axis_index("tower")
+    place = lax.axis_index("dp")
+    core = place & 1
+    unit = (tower << 3) | ((place >> 1) & 7)
+    lists = []
+    for hops in HOPS:
+        order = span(hops)
+        lists.append([order.index(mask) for mask in range(16)])
+    inverse = jnp.array(lists, jnp.int32)
+    rows = inverse[:, unit ^ jnp.arange(16, dtype=jnp.int32)]
+    return core, jnp.where(core == 0, rows, rows[::-1])
+
+
+def grad_half(terms, half, table, kind, small=None):
+    count = terms[0][0].shape[0]
+    rows = terms[0][0].shape[1]
+    block = rows // 16
+    tile = min(rows, 8 * block, 768)
+    per_tile = tile // block
+    widths = [rhs.shape[1] // 2 for _, rhs in terms]
+    total = sum(widths) + (128 if small is not None else 0)
+    meta = jnp.concatenate([half[None], table])
+
+    def body(meta_ref, *refs):
+        out_ref = refs[-1]
+        step = pl.program_id(0)
+        start = 0
+        for index, width in enumerate(widths):
+            part = lax.dot_general(
+                refs[2 * index][...],
+                refs[2 * index + 1][...],
+                (((0,), (0,)), ((), ())),
+                preferred_element_type=f32,
+            ).astype(kind)
+            for inner in range(per_tile):
+                spot = meta_ref[1 + step * per_tile + inner]
+                out_ref[spot, :, start : start + width] = part[inner * block : (inner + 1) * block]
+            start += width
+        if small is not None:
+            for inner in range(per_tile):
+                spot = meta_ref[1 + step * per_tile + inner]
+                extra = refs[2 * len(widths)][0, step * per_tile + inner]
+                out_ref[spot, :, start : start + 128] = jnp.concatenate(
+                    [extra, jnp.zeros((block - extra.shape[0], 128), f32)], 0
+                ).astype(kind)
+
+    in_specs = []
+    operands = []
+    for (lhs, rhs), width in zip(terms, widths):
+        in_specs.append(pl.BlockSpec((count, tile), lambda step, meta_ref: (0, step)))
+        in_specs.append(pl.BlockSpec((count, width), lambda step, meta_ref: (0, meta_ref[0])))
+        operands += [lhs, rhs]
+    if small is not None:
+        in_specs.append(
+            pl.BlockSpec((1,) + small.shape[1:], lambda step, meta_ref: (meta_ref[0], 0, 0, 0))
+        )
+        operands.append(small)
+    return pl.pallas_call(
+        body,
+        out_shape=jax.ShapeDtypeStruct((16, block, total), kind),
+        grid_spec=pltpu.PrefetchScalarGridSpec(
+            num_scalar_prefetch=1,
+            grid=(rows // tile,),
+            in_specs=in_specs,
+            out_specs=pl.BlockSpec((16, block, total), lambda step, meta_ref: (0, 0, 0)),
+        ),
+        compiler_params=call_params(),
+        cost_estimate=pl.CostEstimate(
+            flops=2 * count * rows * sum(widths),
+            bytes_accessed=2 * count * (len(widths) * rows + sum(widths)) + 3 * rows * total,
+            transcendentals=0,
+        ),
+    )(meta, *operands)
+
+
+def finish(mine, theirs, core, table, widths, small_rows=0):
+    block = mine.shape[1]
+    rows = 16 * block
+    tiles = 4
+    per_tile = 16 // tiles
+    meta = jnp.concatenate([core[None], table.reshape(32)])
+
+    def body(meta_ref, mine_ref, theirs_ref, *outs):
+        step = pl.program_id(0)
+
+        def fill(first_ref, first_at, second_ref, second_at):
+            for inner in range(per_tile):
+                number = step * per_tile + inner
+                first = meta_ref[first_at + number]
+                second = meta_ref[second_at + number]
+                start = 0
+                for out_ref, width in zip(outs, widths):
+                    lines = slice(inner * block, (inner + 1) * block)
+                    out_ref[lines, :width] = first_ref[first, :, start : start + width].astype(f32)
+                    out_ref[lines, width:] = second_ref[second, :, start : start + width].astype(
+                        f32
+                    )
+                    start += width
+                if small_rows:
+                    lines = slice(start, start + 128)
+                    outs[-1][0, number] = first_ref[first, :, lines].astype(f32)[:small_rows]
+                    outs[-1][1, number] = second_ref[second, :, lines].astype(f32)[:small_rows]
+
+        @pl.when(meta_ref[0] == 0)
+        def _():
+            fill(mine_ref, 1, theirs_ref, 17)
+
+        @pl.when(meta_ref[0] != 0)
+        def _():
+            fill(theirs_ref, 17, mine_ref, 1)
+
+    whole = pl.BlockSpec(mine.shape, lambda step, meta_ref: (0, 0, 0))
+    out_shape = [jax.ShapeDtypeStruct((rows, 2 * width), f32) for width in widths]
+    out_specs = [
+        pl.BlockSpec((rows // tiles, 2 * width), lambda step, meta_ref: (step, 0))
+        for width in widths
+    ]
+    if small_rows:
+        out_shape.append(jax.ShapeDtypeStruct((2, 16, small_rows, 128), f32))
+        out_specs.append(
+            pl.BlockSpec((2, 16, small_rows, 128), lambda step, meta_ref: (0, 0, 0, 0))
+        )
+    return pl.pallas_call(
+        body,
+        out_shape=out_shape,
+        grid_spec=pltpu.PrefetchScalarGridSpec(
+            num_scalar_prefetch=1, grid=(tiles,), in_specs=[whole, whole], out_specs=out_specs
+        ),
+        compiler_params=call_params(),
+        cost_estimate=pl.CostEstimate(
+            flops=0, bytes_accessed=6 * mine.size * 2, transcendentals=0
+        ),
+    )(meta, mine, theirs)
+
+
+def sum_over_all(sent, kept, dp_size):
+    terms = [kept, swap_core(sent, dp_size)]
+
+    def piece(start, stop):
+        return sum(term[start:stop].astype(f32) for term in terms)
+
+    size = 16
+    for hop in range(4):
+        size //= 2
+        part = piece(size, 2 * size).astype(bf16)
+        terms.append(swap_hop(part, dp_size, (HOPS[0][hop], HOPS[1][hop])))
+    own = piece(0, 1)
+    bits = 16
+    while bits < dp_size:
+        own = own + swap_place(own.astype(bf16), dp_size, bits).astype(f32)
+        bits *= 2
+    whole = own.astype(bf16)
+    for hop in (3, 2, 1, 0):
+        whole = jnp.concatenate(
+            [whole, swap_hop(whole, dp_size, (HOPS[0][hop], HOPS[1][hop]))], 0
+        )
+    return whole, swap_core(whole, dp_size)
+
+
+def gather_pooled(pooled_low, dp_size):
+    place = lax.axis_index("dp")
+    core = place & 1
+    rows = lax.ppermute(pooled_low, "tower", [(0, 1), (1, 0)])[None]
+    extra = []
+    bits = 8
+    while 2 * bits < dp_size:
+        extra.append(bits)
+        bits *= 2
+    orders = [list(hops) + extra for hops in POOL_HOPS]
+    spans = [[0], [0]]
+    for first, second in zip(*orders):
+        rows = jnp.concatenate(
+            [rows, swap_hop(rows, dp_size, (first, second))]
+            if max(first, second) < 8
+            else [rows, swap_place(rows, dp_size, 2 * first)],
+            0,
+        )
+        spans = [
+            entry + [mask ^ old for old in entry] for entry, mask in zip(spans, (first, second))
+        ]
+    other = swap_core(rows, dp_size)
+    spans = jnp.array(spans, jnp.int32) << 1
+    owner = jnp.stack([place ^ spans[0], place ^ 1 ^ spans[1]])
+    owner_other = jnp.stack([place ^ spans[1], place ^ 1 ^ spans[0]])
+    owner = jnp.where(core == 0, owner, owner_other).reshape(-1)
+    return jnp.concatenate([rows, other], 0), owner
 
 
 def gelu_exact(values_in):
@@ -53,8 +283,8 @@
     gain_two,
     shift_two,
 ):
-    f32 = jnp.float32
-    bf16 = jnp.bfloat16
+    dp_size = lax.axis_size("dp")
+    core, table = place_tables(dp_size)
     flat_rows = tokens[0]
     seg_rows = segments[0]
     row_count = seg_rows.shape[0]
@@ -110,17 +340,28 @@
     tower_index = lax.axis_index("tower")
     row_block = lax.axis_index("dp")
     pair_count = pairs.shape[0]
-    everyone = lax.all_gather(pooled_low, ("tower", "dp"), axis=0, tiled=True)
-    other_side = lax.dynamic_slice_in_dim(everyone, (1 - tower_index) * pair_count, pair_count, 0)
-    own_index = row_block * seg_count + jnp.arange(seg_count, dtype=jnp.int32)
-    inverse = (
-        jnp.zeros((pair_count,), jnp.int32).at[pairs].set(jnp.arange(pair_count, dtype=jnp.int32))
-    )
-    back_pick = inverse[own_index]
-    partner_index = jnp.where(tower_index == 0, pairs[own_index], back_pick)
-    target_index = jnp.where(tower_index == 0, own_index, back_pick)
-    partner = other_side[partner_index].astype(f32)
-    target = scores[target_index]
+    everyone, owner = gather_pooled(pooled_low, dp_size)
+    own_start = row_block * seg_count
+    own_index = own_start + jnp.arange(seg_count, dtype=jnp.int32)
+    slots = jnp.arange(seg_count, dtype=jnp.int32)
+    there = (owner[:, None] * seg_count + slots[None, :]).reshape(-1)
+    pairs_there = pairs.reshape(-1, seg_count)[owner].reshape(-1)
+    scores_there = scores.reshape(-1, seg_count)[owner].reshape(-1)
+    pairs_here = lax.dynamic_slice_in_dim(pairs, own_start, seg_count)
+    scores_here = lax.dynamic_slice_in_dim(scores, own_start, seg_count)
+    on_first = tower_index == 0
+    is_pair = (
+        jnp.where(on_first, pairs_here, own_index)[:, None]
+        == jnp.where(on_first, there, pairs_there)[None, :]
+    )
+    target = jnp.where(
+        on_first, scores_here, jnp.sum(jnp.where(is_pair, scores_there[None, :], 0.0), 1)
+    )
+    partner = jnp.dot(
+        is_pair.astype(bf16),
+        everyone.reshape(pair_count, model_width),
+        preferred_element_type=f32,
+    )
     mine = pooled_low.astype(f32)
     inv_mine = lax.rsqrt(jnp.sum(mine * mine, -1) + 1e-06)
     inv_partner = lax.rsqrt(jnp.sum(partner * partner, -1) + 1e-06)
@@ -136,17 +377,26 @@
     d_mid, grad_gain_two, grad_shift_two = norm_back(d_output, normed_two, inv_std_two, gain_two)
     grad_b_down = jnp.sum(d_mid, 0)
     d_mid_low = d_mid.astype(bf16)
-    grad_w_down = jnp.einsum("nf,nd->fd", activated, d_mid_low, preferred_element_type=f32)
+    down_terms = [(activated, d_mid_low)]
+    down_sum = sum_over_all(
+        grad_half(down_terms, 1 - core, table[1], bf16),
+        grad_half(down_terms, core, table[0], f32),
+        dp_size,
+    )
     d_act = jnp.einsum("nd,fd->nf", d_mid_low, w_down, preferred_element_type=f32)
     d_up = gelu_back(d_act)[0]
     grad_b_in = jnp.sum(d_up, 0)
     d_up_low = d_up.astype(bf16)
-    grad_w_in = jnp.einsum("nd,nf->df", hidden_low, d_up_low, preferred_element_type=f32)
     d_hidden = d_mid + jnp.einsum("nf,df->nd", d_up_low, w_in, preferred_element_type=f32)
     d_first, grad_gain_one, grad_shift_one = norm_back(d_hidden, normed_one, inv_std_one, gain_one)
     grad_b_out = jnp.sum(d_first, 0)
     d_first_low = d_first.astype(bf16)
-    grad_w_out = jnp.einsum("nc,nd->cd", context, d_first_low, preferred_element_type=f32)
+    in_terms = [(hidden_low, d_up_low), (context, d_first_low)]
+    in_sum = sum_over_all(
+        grad_half(in_terms, 1 - core, table[1], bf16),
+        grad_half(in_terms, core, table[0], f32),
+        dp_size,
+    )
     d_context = jnp.einsum("nd,cd->nc", d_first_low, w_out, preferred_element_type=f32)
     d_context = d_context.astype(bf16).reshape(head_shape)
     attn_again = jnp.exp(score_of() - log_total)
@@ -169,40 +419,51 @@
     grad_b_query = jnp.sum(d_query, 0)
     grad_b_value = jnp.sum(d_values, 0)
     d_joint = jnp.concatenate([d_query, d_keys, d_values], -1).astype(bf16)
-    grad_w_qkv = jnp.einsum("nd,ne->de", flat_rows, d_joint, preferred_element_type=f32)
+    small = jnp.concatenate(
+        [
+            grad_b_query,
+            grad_b_value,
+            grad_b_out,
+            grad_gain_one,
+            grad_shift_one,
+            grad_b_in,
+            grad_b_down,
+            grad_gain_two,
+            grad_shift_two,
+        ]
+    )
+    small_count = small.shape[0]
+    small_rows = -(-small_count // (32 * 128))
+    small = jnp.pad(small, (0, 32 * 128 * small_rows - small_count))
+    small = small.reshape(2, 16, small_rows, 128)
+    qkv_terms = [(flat_rows, d_joint)]
+    qkv_sum = sum_over_all(
+        grad_half(qkv_terms, 1 - core, table[1], bf16, small),
+        grad_half(qkv_terms, core, table[0], f32, small),
+        dp_size,
+    )
     grad_tokens = d_first + jnp.einsum("ne,de->nd", d_joint, w_qkv, preferred_element_type=f32)
+    ff_width = w_in.shape[1]
+    (grad_w_down,) = finish(*down_sum, core, table, [model_width // 2])
+    grad_w_in, grad_w_out = finish(*in_sum, core, table, [ff_width // 2, model_width // 2])
+    grad_w_qkv, small = finish(*qkv_sum, core, table, [3 * model_width // 2], small_rows)
+    small = small.reshape(-1)
+    pieces = []
+    start = 0
+    for length in [model_width] * 5 + [ff_width] + [model_width] * 3:
+        pieces.append(lax.slice_in_dim(small, start, start + length))
+        start += length
     (
-        grad_w_qkv,
         grad_b_query,
         grad_b_value,
-        grad_w_out,
         grad_b_out,
         grad_gain_one,
         grad_shift_one,
-        grad_w_in,
         grad_b_in,
-        grad_w_down,
         grad_b_down,
         grad_gain_two,
         grad_shift_two,
-    ) = lax.psum(
-        (
-            grad_w_qkv,
-            grad_b_query,
-            grad_b_value,
-            grad_w_out,
-            grad_b_out,
-            grad_gain_one,
-            grad_shift_one,
-            grad_w_in,
-            grad_b_in,
-            grad_w_down,
-            grad_b_down,
-            grad_gain_two,
-            grad_shift_two,
-        ),
-        ("tower", "dp"),
-    )
+    ) = pieces
     return (
         output_rows.astype(bf16)[None],
         grad_tokens[None],

time: 736 us -> 512 us (0.70)
  waiting for transfers between devices: 422 us -> 110 us
  Pallas kernels: 0 us -> 70.7 us
  blocking collectives: 41.7 us -> 0 us
  starting transfers between devices: 0.08 us -> 40.7 us
  other arithmetic: 34.4 us -> 72.9 us
  matrix products: 142 us -> 114 us
  local copies, waits for them, and re-layouts: 77.2 us -> 95.9 us
  between operations: 14.9 us -> 1.87 us
    psum x1 -> x0, waiting for transfers between devices: 376 us -> none  [on_device(): lax.psum((grad_w_qkv, grad_b_query, grad_b_value, grad_w_out, grad_b_out,...]
    ppermute x0 -> x35, waiting for transfers between devices: none -> 110 us  [the longest x27 110 us: swap_hop(): return lax.ppermute(value, AXES, pairs)]
    pallas_call x0 -> x9, Pallas kernels: none -> 70.7 us  [the longest x6 49.7 us: grad_half(): pl.pallas_call(body, out_shape=jax.ShapeDtypeStruct((16, block, total), k...]
    all_gather x1 -> x0, waiting for transfers between devices: 45.4 us -> none  [on_device(): everyone = lax.all_gather(pooled_low, ('tower', 'dp'), axis=0, tiled=True)]
    psum x1 -> x0, blocking collectives: 41.7 us -> none  [on_device(): lax.psum((grad_w_qkv, grad_b_query, grad_b_value, grad_w_out, grad_b_out,...]
    ppermute x0 -> x35, starting transfers between devices: none -> 40.7 us  [the longest x27 36.1 us: swap_hop(): return lax.ppermute(value, AXES, pairs)]
    dot_general x4 -> x1, matrix products: 25.2 us -> 1.58 us  [on_device(): jnp.dot(is_pair.astype(bf16), everyone.reshape(pair_count, model_width),...]
    convert_element_type x0 -> x15, other arithmetic: none -> 22.5 us  [the longest x12 20.4 us: sum_over_all(): part = piece(size, 2 * size).astype(bf16)]
  transfers between devices with their start and end apart: 2 -> 35, of which waited for: 2 -> 15; matrix products, arithmetic and copies ran while one was open for 4% -> 24% of each run, Pallas kernels for 0% -> 11%
where the time goes in v1:
time: 512 us; the launch traced here: 507 us
  matrix products  114 us (22%)
  waiting for transfers between devices  110 us (21%)
  local copies, waits for them, and re-layouts  95.9 us (19%)
  other arithmetic  72.9 us (14%)
  Pallas kernels  70.7 us (14%)
  starting transfers between devices  40.7 us (8%)
    ppermute x27, waiting for transfers between devices, swap_hop(): return lax.ppermute(value, AXES, pairs)  110 us
    pallas_call x6, Pallas kernels, grad_half(): pl.pallas_call(body, out_shape=jax.ShapeDtypeStruct((16, block, total), k...  49.7 us
    unnamed x167, local copies, waits for them, and re-layouts  44.9 us
    ppermute x27, starting transfers between devices, swap_hop(): return lax.ppermute(value, AXES, pairs)  36.1 us
    dot_general x1, matrix products, on_device(): up_rows = jnp.dot(hidden_low, w_in, preferred_element_type=f32) + b_in  33.1 us
    pallas_call x3, Pallas kernels, finish(): pl.pallas_call(body, out_shape=out_shape, grid_spec=pltpu.PrefetchScalarG...  21 us
    convert_element_type x12, other arithmetic, sum_over_all(): part = piece(size, 2 * size).astype(bf16)  20.4 us
    dot_general x1, matrix products, on_device(): jnp.einsum('nd,fd->nf', d_mid_low, w_down, preferred_element_type=f32)  18.8 us
  transfers between devices with their start and end apart: 35, of which 15 were waited for; matrix products, arithmetic and copies ran while one was open for 24% of the time, Pallas kernels for 11%

profile of v1, /device:TPU:0, one launch (start us, length us, event | category | flops | bytes accessed | tf_op | source)
XLA Modules:
  0.0 506.7 jit_solution(12334007789623328948)
XLA Ops:
  3.8 5.2 %fusion.100 = f32[1024,2304]{1,0:T(8,128)S(1)} fusion(bf16[768,2304]{1,0:T(8,128)(2,1)S(1)} %copy-done, bf16[1,1024,768]{2,1,0:T(8,128)(2,1)} %param.19), kind=kOutput, calls=%fused_computation.249 | convolution fusion | flops 3623878656 | bytes 14548992 | tf_op jit(solution)/shard_map/dot_general | solution.py:297
  39.8 33.1 %multiply_convert_fusion = (bf16[1024,3072]{1,0:T(8,128)(2,1)S(1)}, f32[1024,3072]{1,0:T(8,128)}, f32[1024,3072]{1,0:T(8,128)}) fusion(f32[3072]{0:T(1024)S(1)} %copy-done.57, bf16[1024,768]{1,0:T(8,128)(2,1)S(1)} %fusion.16.refs_0_, bf16[768,3072]{1,0:T(8,128)(2,1)S(1)} %bitcast.163), kind=kOutput, calls=%fused_computation.6 | convolution fusion | flops 5039456256 | bytes 37761024 | tf_op jit(solution)/shard_map/dot_general | solution.py:323
  72.9 5.5 %fusion.113 = (f32[1024]{0:T(1024)S(1)}, f32[1024,768]{1,0:T(8,128)S(1)}) fusion(f32[768]{0:T(1024)S(1)} %copy-done.60, bf16[1024,3072]{1,0:T(8,128)(2,1)S(1)} %get-tuple-element.49.refs_0_, bf16[3072,768]{1,0:T(8,128)(2,1)S(1)} %bitcast.161, f32[768]{0:T(1024)S(1)} %copy-done.49, f32[768]{0:T(1024)S(1)} %copy-done.41, f32[1024]{0:T(1024)S(1)} %add_rsqrt_fusion.2, ...), kind=kOutput, calls=%fused_computation.258 | convolution fusion | flops 4837342208 | bytes 17323008 | tf_op jit(solution)/shard_map/dot_general | solution.py:326
  103.9 3.9 collective-permute-done.2
  144.9 18.8 %fusion.109 = (f32[3072]{0:T(1024)}, bf16[1024,3072]{1,0:T(8,128)(2,1)}) fusion(f32[1024,3072]{1,0:T(8,128)} %get-tuple-element.50, bf16[1024,768]{1,0:T(8,128)(2,1)} %convert_element_type.260.refs_1_, bf16[3072,768]{1,0:T(8,128)(2,1)} %param.32, f32[1024,3072]{1,0:T(8,128)} %get-tuple-element.74, f32[3072]{0:T(1024)S(1)} %copy-done.58), kind=kOutput, calls=%fused_computation.254 | convolution fusion | flops 4882166784 | bytes 37773312 | tf_op jit(solution)/shard_map/nd,fd->nf/dot_general | solution.py:386
  163.7 10.7 %multiply_reduce_fusion.1 = (f32[768]{0:T(1024)}, f32[1024]{0:T(1024)S(1)}, f32[1024]{0:T(1024)S(1)}, f32[768]{0:T(1024)}, f32[1024,768]{1,0:T(8,128)S(1)}) fusion(f32[1024,768]{1,0:T(8,128)S(1)} %copy-done.5, f32[1024]{0:T(1024)S(1)} %copy-done.36, f32[1024]{0:T(1024)S(1)} %copy-done.30, f32[768]{0:T(1024)S(1)} %copy-done.42, f32[1024,768]{1,0:T(8,128)} %copy-done.11, ...), kind=kOutput, calls=%fused_computation.42 | convolution fusion | flops 4839698432 | bytes 20472832 | tf_op jit(solution)/shard_map/nf,df->nd/dot_general | solution.py:390
  186.4 6.8 %bitcast_convert_fusion = (bf16[8,128,12,64]{1,3,2,0:T(8,128)(2,1)S(1)}, f32[8,12,64,128]{3,2,1,0:T(8,128)}) fusion(f32[8,12,128,128]{2,3,1,0:T(8,128)} %copy-done.1, f32[8,12,128]{2,1,0:T(8,128)S(1)} %copy-done.21, bf16[8,128,12,64]{1,0,3,2:T(8,128)(2,1)S(1)} %bitcast.130), kind=kOutput, calls=%fused_computation.36 | convolution fusion | flops 205258752 | bytes 12632064 | tf_op jit(solution)/shard_map/rhqk,rqhd->rkhd/dot_general | solution.py:404
  193.3 4.6 multiply_reduce_fusion
  197.9 4.9 multiply_convert_fusion.1
  209.3 8.8 %shard_map.302 = bf16[16,48,1920]{2,1,0:T(8,128)(2,1)} custom-call(s32[17]{0:T(128)} %pad_add_fusion.2.meta_ref, bf16[1024,768]{1,0:T(8,128)(2,1)} %copy-done.8, bf16[1024,3072]{1,0:T(8,128)(2,1)} %get-tuple-element.52.refs_1_, bf16[1024,768]{1,0:T(8,128)(2,1)} %copy.101.refs_2_, bf16[1024,768]{1,0:T(8,128)(2,1)} %copy-done.9), custom_call_target="tpu_custom_call" | custom-call | flops 3019898880 | bytes 11501568 | tf_op jit(solution)/shard_map/pallas_call | solution.py:114
  252.5 4.0 pad_maximum_fusion.refs_1_
  258.6 6.4 %shard_map.299 = bf16[16,48,1280]{2,1,0:T(8,128)(2,1)} custom-call(s32[17]{0:T(128)} %pad_add_fusion.2.meta_ref, bf16[1024,768]{1,0:T(8,128)(2,1)} %bitcast.133, bf16[1024,2304]{1,0:T(8,128)(2,1)} %pad_maximum_fusion.refs_1_, f32[2,16,3,128]{3,2,1,0:T(4,128)} %reshape.293.refs_2_), custom_call_target="tpu_custom_call" | custom-call | flops 1811939328 | bytes 6881280 | tf_op jit(solution)/shard_map/pallas_call | solution.py:114
  265.0 8.2 %shard_map.305 = bf16[16,192,384]{2,1,0:T(8,128)(2,1)} custom-call(s32[17]{0:T(128)} %pad_add_fusion.2.meta_ref, bf16[1024,3072]{1,0:T(8,128)(2,1)} %copy-done.6, bf16[1024,768]{1,0:T(8,128)(2,1)} %convert_element_type.260.refs_1_), custom_call_target="tpu_custom_call" | custom-call | flops 2415919104 | bytes 10616832 | tf_op jit(solution)/shard_map/pallas_call | solution.py:114
  274.3 7.0 %shard_map.298 = f32[16,48,1280]{2,1,0:T(8,128)} custom-call(s32[17]{0:T(128)} %pad_add_fusion.1.meta_ref, bf16[1024,768]{1,0:T(8,128)(2,1)} %bitcast.134, bf16[1024,2304]{1,0:T(8,128)(2,1)} %pad_maximum_fusion.refs_1_, f32[2,16,3,128]{3,2,1,0:T(4,128)} %reshape.293.refs_2_), custom_call_target="tpu_custom_call" | custom-call | flops 1811939328 | bytes 6881280 | tf_op jit(solution)/shard_map/pallas_call | solution.py:114
  281.4 10.0 %shard_map.301 = f32[16,48,1920]{2,1,0:T(8,128)} custom-call(s32[17]{0:T(128)} %pad_add_fusion.1.meta_ref, bf16[1024,768]{1,0:T(8,128)(2,1)} %copy-done.8, bf16[1024,3072]{1,0:T(8,128)(2,1)} %get-tuple-element.52.refs_1_, bf16[1024,768]{1,0:T(8,128)(2,1)} %copy.101.refs_2_, bf16[1024,768]{1,0:T(8,128)(2,1)} %copy-done.9), custom_call_target="tpu_custom_call" | custom-call | flops 3019898880 | bytes 11501568 | tf_op jit(solution)/shard_map/pallas_call | solution.py:114
  294.3 3.7 fusion.15
  299.5 9.3 %shard_map.304 = f32[16,192,384]{2,1,0:T(8,128)} custom-call(s32[17]{0:T(128)} %pad_add_fusion.1.meta_ref, bf16[1024,3072]{1,0:T(8,128)(2,1)} %copy-done.6, bf16[1024,768]{1,0:T(8,128)(2,1)} %convert_element_type.260.refs_1_), custom_call_target="tpu_custom_call" | custom-call | flops 2415919104 | bytes 10616832 | tf_op jit(solution)/shard_map/pallas_call | solution.py:114
  313.4 17.1 %collective-permute-done.16 = bf16[8,48,1920]{2,1,0:T(8,128)(2,1)} collective-permute-done((bf16[8,48,1920]{2,1,0:T(8,128)(2,1)}, bf16[8,48,1920]{2,1,0:T(8,128)(2,1)}, u32[]{:S(2)}, u32[]{:S(2)}) %collective-permute-start.16) | collective-permute-done | bytes 1474592 | tf_op jit(solution)/shard_map/ppermute | solution.py:38
  336.5 19.2 %collective-permute-done.26 = bf16[8,192,384]{2,1,0:T(8,128)(2,1)S(1)} collective-permute-done((bf16[8,192,384]{2,1,0:T(8,128)(2,1)S(1)}, bf16[8,192,384]{2,1,0:T(8,128)(2,1)S(1)}, u32[]{:S(2)}, u32[]{:S(2)}) %collective-permute-start.26) | collective-permute-done | bytes 1179680 | tf_op jit(solution)/shard_map/ppermute | solution.py:38
  363.9 9.6 %collective-permute-done.18 = bf16[2,48,1920]{2,1,0:T(8,128)(2,1)S(1)} collective-permute-done((bf16[2,48,1920]{2,1,0:T(8,128)(2,1)S(1)}, bf16[2,48,1920]{2,1,0:T(8,128)(2,1)S(1)}, u32[]{:S(2)}, u32[]{:S(2)}) %collective-permute-start.18) | collective-permute-done | bytes 368672 | tf_op jit(solution)/shard_map/ppermute | solution.py:38
  377.6 3.4 collective-permute-start.28
  383.9 10.1 %collective-permute-done.28 = bf16[2,192,384]{2,1,0:T(8,128)(2,1)S(1)} collective-permute-done((bf16[2,192,384]{2,1,0:T(8,128)(2,1)S(1)}, bf16[2,192,384]{2,1,0:T(8,128)(2,1)S(1)}, u32[]{:S(2)}, u32[]{:S(2)}) %collective-permute-start.28) | collective-permute-done | bytes 294944 | tf_op jit(solution)/shard_map/ppermute | solution.py:38
  403.4 5.1 %collective-permute-done.21 = bf16[2,48,1920]{2,1,0:T(8,128)(2,1)S(1)} collective-permute-done((bf16[2,48,1920]{2,1,0:T(8,128)(2,1)S(1)}, bf16[2,48,1920]{2,1,0:T(8,128)(2,1)S(1)}, u32[]{:S(2)}, u32[]{:S(2)}) %collective-permute-start.21) | collective-permute-done | bytes 368672 | tf_op jit(solution)/shard_map/ppermute | solution.py:38
  412.5 7.8 %collective-permute-done.11 = bf16[2,48,1280]{2,1,0:T(8,128)(2,1)S(1)} collective-permute-done((bf16[2,48,1280]{2,1,0:T(8,128)(2,1)S(1)}, bf16[2,48,1280]{2,1,0:T(8,128)(2,1)S(1)}, u32[]{:S(2)}, u32[]{:S(2)}) %collective-permute-start.11) | collective-permute-done | bytes 245792 | tf_op jit(solution)/shard_map/ppermute | solution.py:38
  427.6 3.7 collective-permute-done.12
  432.7 4.8 collective-permute-done.32
  440.8 4.9 collective-permute-done.23
  449.2 19.7 %collective-permute-done.33 = bf16[8,192,384]{2,1,0:T(8,128)(2,1)S(1)} collective-permute-done((bf16[8,192,384]{2,1,0:T(8,128)(2,1)S(1)}, bf16[8,192,384]{2,1,0:T(8,128)(2,1)S(1)}, u32[]{:S(2)}, u32[]{:S(2)}) %collective-permute-start.33) | collective-permute-done | bytes 1179680 | tf_op jit(solution)/shard_map/ppermute | solution.py:38
  472.3 8.8 %add_bitcast_fusion = f32[1,1024,768]{2,1,0:T(8,128)} fusion(f32[1024,768]{1,0:T(8,128)} %copy-done.10, bf16[768,2304]{1,0:T(8,128)(2,1)S(1)} %copy-done, bf16[1024,768]{1,0:T(8,128)(2,1)} %copy.99, bf16[1024,768]{1,0:T(8,128)(2,1)} %copy.98, bf16[1024,768]{1,0:T(8,128)(2,1)} %copy.97), kind=kOutput, calls=%fused_computation.43 | convolution fusion | flops 3638820864 | bytes 14548992 | tf_op jit(solution)/shard_map/ne,de->nd/dot_general | solution.py:445
  481.2 6.1 %shard_map.300 = (f32[768,2304]{1,0:T(8,128)}, f32[2,16,3,128]{3,2,1,0:T(4,128)}) custom-call(s32[33]{0:T(128)} %pad_add_fusion.meta_ref, bf16[16,48,1280]{2,1,0:T(8,128)(2,1)} %constant_dynamic-update-slice_fusion.6.mine_ref, bf16[16,48,1280]{2,1,0:T(8,128)(2,1)} %collective-permute-done.14.theirs_ref), custom_call_target="tpu_custom_call" | custom-call | bytes 11796480 | tf_op jit(solution)/shard_map/pallas_call | solution.py:179
  491.5 7.0 %shard_map.306 = f32[3072,768]{1,0:T(8,128)} custom-call(s32[33]{0:T(128)} %pad_add_fusion.meta_ref, bf16[16,192,384]{2,1,0:T(8,128)(2,1)} %constant_dynamic-update-slice_fusion.16.mine_ref, bf16[16,192,384]{2,1,0:T(8,128)(2,1)} %collective-permute-done.34.theirs_ref), custom_call_target="tpu_custom_call" | custom-call | bytes 14155776 | tf_op jit(solution)/shard_map/pallas_call | solution.py:179
  498.4 7.9 %shard_map.303 = (f32[768,3072]{1,0:T(8,128)}, f32[768,768]{1,0:T(8,128)}) custom-call(s32[33]{0:T(128)} %pad_add_fusion.meta_ref, bf16[16,48,1920]{2,1,0:T(8,128)(2,1)} %constant_dynamic-update-slice_fusion.11.mine_ref, bf16[16,48,1920]{2,1,0:T(8,128)(2,1)} %collective-permute-done.24.theirs_ref), custom_call_target="tpu_custom_call" | custom-call | bytes 17694720 | tf_op jit(solution)/shard_map/pallas_call | solution.py:179
  (343 shorter events, 218.9 us)
Async XLA Ops:
  83.4 10.6 %collective-permute-start = (bf16[64,768]{1,0:T(8,128)(2,1)}, bf16[64,768]{1,0:T(8,128)(2,1)}, u32[]{:S(2)}, u32[]{:S(2)}) collective-permute-start(bf16[64,768]{1,0:T(8,128)(2,1)} %bitcast.5), channel_id=1, source_target_pairs={{0,16},{16,0},{1,17},{17,1},{2,18},{18,2},{3,19},{19,3},{4,20},{20... | collective-permute-start | bytes 294920 | tf_op jit(solution)/shard_map/ppermute | solution.py:219
  99.9 7.8 %collective-permute-start.2 = (bf16[2,64,768]{2,1,0:T(8,128)(2,1)S(1)}, bf16[2,64,768]{2,1,0:T(8,128)(2,1)S(1)}, u32[]{:S(2)}, u32[]{:S(2)}) collective-permute-start(bf16[2,64,768]{2,1,0:T(8,128)(2,1)S(1)} %pad_maximum_fusion.12), channel_id=1, source_target_pairs={{0,8},{1,5},{2,10},{3,7},{4,12},{5,1},{6,14},{7,3},{8,0},{9,13},{1... | collective-permute-start | bytes 589832 | tf_op jit(solution)/shard_map/ppermute | solution.py:38
  110.1 16.8 %collective-permute-start.3 = (bf16[4,64,768]{2,1,0:T(8,128)(2,1)}, bf16[4,64,768]{2,1,0:T(8,128)(2,1)}, u32[]{:S(2)}, u32[]{:S(2)}) collective-permute-start(bf16[4,64,768]{2,1,0:T(8,128)(2,1)} %pad_maximum_fusion.8), channel_id=1, source_target_pairs={{0,4},{1,3},{2,6},{3,1},{4,0},{5,7},{6,2},{7,5},{8,12},{9,11},{10,... | collective-permute-start | bytes 1179656 | tf_op jit(solution)/shard_map/ppermute | solution.py:38
  218.1 76.2 %collective-permute-start.15 = (bf16[16,48,1920]{2,1,0:T(8,128)(2,1)}, bf16[16,48,1920]{2,1,0:T(8,128)(2,1)}, u32[]{:S(2)}, u32[]{:S(2)}) collective-permute-start(bf16[16,48,1920]{2,1,0:T(8,128)(2,1)} %shard_map.302), channel_id=1, source_target_pairs={{0,1},{1,0},{2,3},{3,2},{4,5},{5,4},{6,7},{7,6},{8,9},{9,8},{10,11... | collective-permute-start | bytes 8847368 | tf_op jit(solution)/shard_map/ppermute | solution.py:42
  265.0 26.4 %collective-permute-start.5 = (bf16[16,48,1280]{2,1,0:T(8,128)(2,1)}, bf16[16,48,1280]{2,1,0:T(8,128)(2,1)}, u32[]{:S(2)}, u32[]{:S(2)}) collective-permute-start(bf16[16,48,1280]{2,1,0:T(8,128)(2,1)} %shard_map.299), channel_id=1, source_target_pairs={{0,1},{1,0},{2,3},{3,2},{4,5},{5,4},{6,7},{7,6},{8,9},{9,8},{10,11... | collective-permute-start | bytes 5898248 | tf_op jit(solution)/shard_map/ppermute | solution.py:42
  273.2 35.5 %collective-permute-start.25 = (bf16[16,192,384]{2,1,0:T(8,128)(2,1)}, bf16[16,192,384]{2,1,0:T(8,128)(2,1)}, u32[]{:S(2)}, u32[]{:S(2)}) collective-permute-start(bf16[16,192,384]{2,1,0:T(8,128)(2,1)} %shard_map.305), channel_id=1, source_target_pairs={{0,1},{1,0},{2,3},{3,2},{4,5},{5,4},{6,7},{7,6},{8,9},{9,8},{10,11... | collective-permute-start | bytes 7077896 | tf_op jit(solution)/shard_map/ppermute | solution.py:42
  293.8 17.9 %collective-permute-start.6 = (bf16[8,48,1280]{2,1,0:T(8,128)(2,1)}, bf16[8,48,1280]{2,1,0:T(8,128)(2,1)}, u32[]{:S(2)}, u32[]{:S(2)}) collective-permute-start(bf16[8,48,1280]{2,1,0:T(8,128)(2,1)} %fusion.18), channel_id=1, source_target_pairs={{0,16},{1,3},{2,18},{3,1},{4,20},{5,7},{6,22},{7,5},{8,24},{9,11},... | collective-permute-start | bytes 2949128 | tf_op jit(solution)/shard_map/ppermute | solution.py:38
  298.0 32.5 %collective-permute-start.16 = (bf16[8,48,1920]{2,1,0:T(8,128)(2,1)}, bf16[8,48,1920]{2,1,0:T(8,128)(2,1)}, u32[]{:S(2)}, u32[]{:S(2)}) collective-permute-start(bf16[8,48,1920]{2,1,0:T(8,128)(2,1)} %fusion.15), channel_id=1, source_target_pairs={{0,16},{1,3},{2,18},{3,1},{4,20},{5,7},{6,22},{7,5},{8,24},{9,11},... | collective-permute-start | bytes 4423688 | tf_op jit(solution)/shard_map/ppermute | solution.py:38
  311.1 44.6 %collective-permute-start.26 = (bf16[8,192,384]{2,1,0:T(8,128)(2,1)S(1)}, bf16[8,192,384]{2,1,0:T(8,128)(2,1)S(1)}, u32[]{:S(2)}, u32[]{:S(2)}) collective-permute-start(bf16[8,192,384]{2,1,0:T(8,128)(2,1)S(1)} %fusion.17), channel_id=1, source_target_pairs={{0,16},{1,3},{2,18},{3,1},{4,20},{5,7},{6,22},{7,5},{8,24},{9,11},... | collective-permute-start | bytes 3538952 | tf_op jit(solution)/shard_map/ppermute | solution.py:38
  313.3 19.3 %collective-permute-start.7 = (bf16[4,48,1280]{2,1,0:T(8,128)(2,1)S(1)}, bf16[4,48,1280]{2,1,0:T(8,128)(2,1)S(1)}, u32[]{:S(2)}, u32[]{:S(2)}) collective-permute-start(bf16[4,48,1280]{2,1,0:T(8,128)(2,1)S(1)} %fusion.38), channel_id=1, source_target_pairs={{0,4},{1,17},{2,6},{3,19},{4,0},{5,21},{6,2},{7,23},{8,12},{9,25},... | collective-permute-start | bytes 1474568 | tf_op jit(solution)/shard_map/ppermute | solution.py:38
  332.5 24.6 %collective-permute-start.17 = (bf16[4,48,1920]{2,1,0:T(8,128)(2,1)S(1)}, bf16[4,48,1920]{2,1,0:T(8,128)(2,1)S(1)}, u32[]{:S(2)}, u32[]{:S(2)}) collective-permute-start(bf16[4,48,1920]{2,1,0:T(8,128)(2,1)S(1)} %fusion.23), channel_id=1, source_target_pairs={{0,4},{1,17},{2,6},{3,19},{4,0},{5,21},{6,2},{7,23},{8,12},{9,25},... | collective-permute-start | bytes 2211848 | tf_op jit(solution)/shard_map/ppermute | solution.py:38
  333.8 27.5 %collective-permute-start.8 = (bf16[2,48,1280]{2,1,0:T(8,128)(2,1)S(1)}, bf16[2,48,1280]{2,1,0:T(8,128)(2,1)S(1)}, u32[]{:S(2)}, u32[]{:S(2)}) collective-permute-start(bf16[2,48,1280]{2,1,0:T(8,128)(2,1)S(1)} %fusion.47), channel_id=1, source_target_pairs={{0,8},{1,5},{2,10},{3,7},{4,12},{5,1},{6,14},{7,3},{8,0},{9,13},{1... | collective-permute-start | bytes 737288 | tf_op jit(solution)/shard_map/ppermute | solution.py:38
  357.0 19.5 %collective-permute-start.27 = (bf16[4,192,384]{2,1,0:T(8,128)(2,1)S(1)}, bf16[4,192,384]{2,1,0:T(8,128)(2,1)S(1)}, u32[]{:S(2)}, u32[]{:S(2)}) collective-permute-start(bf16[4,192,384]{2,1,0:T(8,128)(2,1)S(1)} %fusion.35), channel_id=1, source_target_pairs={{0,4},{1,17},{2,6},{3,19},{4,0},{5,21},{6,2},{7,23},{8,12},{9,25},... | collective-permute-start | bytes 1769480 | tf_op jit(solution)/shard_map/ppermute | solution.py:38
  358.6 15.0 %collective-permute-start.18 = (bf16[2,48,1920]{2,1,0:T(8,128)(2,1)S(1)}, bf16[2,48,1920]{2,1,0:T(8,128)(2,1)S(1)}, u32[]{:S(2)}, u32[]{:S(2)}) collective-permute-start(bf16[2,48,1920]{2,1,0:T(8,128)(2,1)S(1)} %fusion.41), channel_id=1, source_target_pairs={{0,8},{1,5},{2,10},{3,7},{4,12},{5,1},{6,14},{7,3},{8,0},{9,13},{1... | collective-permute-start | bytes 1105928 | tf_op jit(solution)/shard_map/ppermute | solution.py:38
  362.4 34.4 %collective-permute-start.9 = (bf16[1,48,1280]{2,1,0:T(8,128)(2,1)S(1)}, bf16[1,48,1280]{2,1,0:T(8,128)(2,1)S(1)}, u32[]{:S(2)}, u32[]{:S(2)}) collective-permute-start(bf16[1,48,1280]{2,1,0:T(8,128)(2,1)S(1)} %fusion.72), channel_id=1, source_target_pairs={{0,2},{1,9},{2,0},{3,11},{4,6},{5,13},{6,4},{7,15},{8,10},{9,1},{1... | collective-permute-start | bytes 368648 | tf_op jit(solution)/shard_map/ppermute | solution.py:38
  374.8 6.2 %collective-permute-start.19 = (bf16[1,48,1920]{2,1,0:T(8,128)(2,1)S(1)}, bf16[1,48,1920]{2,1,0:T(8,128)(2,1)S(1)}, u32[]{:S(2)}, u32[]{:S(2)}) collective-permute-start(bf16[1,48,1920]{2,1,0:T(8,128)(2,1)S(1)} %fusion.51), channel_id=1, source_target_pairs={{0,2},{1,9},{2,0},{3,11},{4,6},{5,13},{6,4},{7,15},{8,10},{9,1},{1... | collective-permute-start | bytes 552968 | tf_op jit(solution)/shard_map/ppermute | solution.py:38
  377.6 16.4 %collective-permute-start.28 = (bf16[2,192,384]{2,1,0:T(8,128)(2,1)S(1)}, bf16[2,192,384]{2,1,0:T(8,128)(2,1)S(1)}, u32[]{:S(2)}, u32[]{:S(2)}) collective-permute-start(bf16[2,192,384]{2,1,0:T(8,128)(2,1)S(1)} %fusion.44), channel_id=1, source_target_pairs={{0,8},{1,5},{2,10},{3,7},{4,12},{5,1},{6,14},{7,3},{8,0},{9,13},{1... | collective-permute-start | bytes 884744 | tf_op jit(solution)/shard_map/ppermute | solution.py:38
  383.0 13.6 %collective-permute-start.20 = (bf16[1,48,1920]{2,1,0:T(8,128)(2,1)S(1)}, bf16[1,48,1920]{2,1,0:T(8,128)(2,1)S(1)}, u32[]{:S(2)}, u32[]{:S(2)}) collective-permute-start(bf16[1,48,1920]{2,1,0:T(8,128)(2,1)S(1)} %get-tuple-element.38), channel_id=1, source_target_pairs={{0,2},{1,9},{2,0},{3,11},{4,6},{5,13},{6,4},{7,15},{8,10},{9,1},{1... | collective-permute-start | bytes 552968 | tf_op jit(solution)/shard_map/ppermute | solution.py:38
  396.6 11.9 %collective-permute-start.21 = (bf16[2,48,1920]{2,1,0:T(8,128)(2,1)S(1)}, bf16[2,48,1920]{2,1,0:T(8,128)(2,1)S(1)}, u32[]{:S(2)}, u32[]{:S(2)}) collective-permute-start(bf16[2,48,1920]{2,1,0:T(8,128)(2,1)S(1)} %pad_maximum_fusion.9), channel_id=1, source_target_pairs={{0,8},{1,5},{2,10},{3,7},{4,12},{5,1},{6,14},{7,3},{8,0},{9,13},{1... | collective-permute-start | bytes 1105928 | tf_op jit(solution)/shard_map/ppermute | solution.py:38
  398.4 10.3 %collective-permute-start.10 = (bf16[1,48,1280]{2,1,0:T(8,128)(2,1)S(1)}, bf16[1,48,1280]{2,1,0:T(8,128)(2,1)S(1)}, u32[]{:S(2)}, u32[]{:S(2)}) collective-permute-start(bf16[1,48,1280]{2,1,0:T(8,128)(2,1)S(1)} %get-tuple-element.40), channel_id=1, source_target_pairs={{0,2},{1,9},{2,0},{3,11},{4,6},{5,13},{6,4},{7,15},{8,10},{9,1},{1... | collective-permute-start | bytes 368648 | tf_op jit(solution)/shard_map/ppermute | solution.py:38
  401.9 8.9 %collective-permute-start.30 = (bf16[1,192,384]{2,1,0:T(8,128)(2,1)S(1)}, bf16[1,192,384]{2,1,0:T(8,128)(2,1)S(1)}, u32[]{:S(2)}, u32[]{:S(2)}) collective-permute-start(bf16[1,192,384]{2,1,0:T(8,128)(2,1)S(1)} %get-tuple-element.36), channel_id=1, source_target_pairs={{0,2},{1,9},{2,0},{3,11},{4,6},{5,13},{6,4},{7,15},{8,10},{9,1},{1... | collective-permute-start | bytes 442376 | tf_op jit(solution)/shard_map/ppermute | solution.py:38
  408.6 17.5 %collective-permute-start.22 = (bf16[4,48,1920]{2,1,0:T(8,128)(2,1)S(1)}, bf16[4,48,1920]{2,1,0:T(8,128)(2,1)S(1)}, u32[]{:S(2)}, u32[]{:S(2)}) collective-permute-start(bf16[4,48,1920]{2,1,0:T(8,128)(2,1)S(1)} %pad_maximum_fusion.5), channel_id=1, source_target_pairs={{0,4},{1,17},{2,6},{3,19},{4,0},{5,21},{6,2},{7,23},{8,12},{9,25},... | collective-permute-start | bytes 2211848 | tf_op jit(solution)/shard_map/ppermute | solution.py:38
  408.7 11.6 %collective-permute-start.11 = (bf16[2,48,1280]{2,1,0:T(8,128)(2,1)S(1)}, bf16[2,48,1280]{2,1,0:T(8,128)(2,1)S(1)}, u32[]{:S(2)}, u32[]{:S(2)}) collective-permute-start(bf16[2,48,1280]{2,1,0:T(8,128)(2,1)S(1)} %pad_maximum_fusion.11), channel_id=1, source_target_pairs={{0,8},{1,5},{2,10},{3,7},{4,12},{5,1},{6,14},{7,3},{8,0},{9,13},{1... | collective-permute-start | bytes 737288 | tf_op jit(solution)/shard_map/ppermute | solution.py:38
  410.8 12.6 %collective-permute-start.31 = (bf16[2,192,384]{2,1,0:T(8,128)(2,1)S(1)}, bf16[2,192,384]{2,1,0:T(8,128)(2,1)S(1)}, u32[]{:S(2)}, u32[]{:S(2)}) collective-permute-start(bf16[2,192,384]{2,1,0:T(8,128)(2,1)S(1)} %pad_maximum_fusion.10), channel_id=1, source_target_pairs={{0,8},{1,5},{2,10},{3,7},{4,12},{5,1},{6,14},{7,3},{8,0},{9,13},{1... | collective-permute-start | bytes 884744 | tf_op jit(solution)/shard_map/ppermute | solution.py:38
  420.4 10.8 %collective-permute-start.12 = (bf16[4,48,1280]{2,1,0:T(8,128)(2,1)S(1)}, bf16[4,48,1280]{2,1,0:T(8,128)(2,1)S(1)}, u32[]{:S(2)}, u32[]{:S(2)}) collective-permute-start(bf16[4,48,1280]{2,1,0:T(8,128)(2,1)S(1)} %pad_maximum_fusion.7), channel_id=1, source_target_pairs={{0,4},{1,17},{2,6},{3,19},{4,0},{5,21},{6,2},{7,23},{8,12},{9,25},... | collective-permute-start | bytes 1474568 | tf_op jit(solution)/shard_map/ppermute | solution.py:38
  423.5 14.0 %collective-permute-start.32 = (bf16[4,192,384]{2,1,0:T(8,128)(2,1)S(1)}, bf16[4,192,384]{2,1,0:T(8,128)(2,1)S(1)}, u32[]{:S(2)}, u32[]{:S(2)}) collective-permute-start(bf16[4,192,384]{2,1,0:T(8,128)(2,1)S(1)} %pad_maximum_fusion.6), channel_id=1, source_target_pairs={{0,4},{1,17},{2,6},{3,19},{4,0},{5,21},{6,2},{7,23},{8,12},{9,25},... | collective-permute-start | bytes 1769480 | tf_op jit(solution)/shard_map/ppermute | solution.py:38
  426.3 19.4 %collective-permute-start.23 = (bf16[8,48,1920]{2,1,0:T(8,128)(2,1)S(1)}, bf16[8,48,1920]{2,1,0:T(8,128)(2,1)S(1)}, u32[]{:S(2)}, u32[]{:S(2)}) collective-permute-start(bf16[8,48,1920]{2,1,0:T(8,128)(2,1)S(1)} %pad_maximum_fusion.1), channel_id=1, source_target_pairs={{0,16},{1,3},{2,18},{3,1},{4,20},{5,7},{6,22},{7,5},{8,24},{9,11},... | collective-permute-start | bytes 4423688 | tf_op jit(solution)/shard_map/ppermute | solution.py:38
  431.3 38.7 %collective-permute-start.13 = (bf16[8,48,1280]{2,1,0:T(8,128)(2,1)S(1)}, bf16[8,48,1280]{2,1,0:T(8,128)(2,1)S(1)}, u32[]{:S(2)}, u32[]{:S(2)}) collective-permute-start(bf16[8,48,1280]{2,1,0:T(8,128)(2,1)S(1)} %pad_maximum_fusion.3), channel_id=1, source_target_pairs={{0,16},{1,3},{2,18},{3,1},{4,20},{5,7},{6,22},{7,5},{8,24},{9,11},... | collective-permute-start | bytes 2949128 | tf_op jit(solution)/shard_map/ppermute | solution.py:38
  437.7 31.2 %collective-permute-start.33 = (bf16[8,192,384]{2,1,0:T(8,128)(2,1)S(1)}, bf16[8,192,384]{2,1,0:T(8,128)(2,1)S(1)}, u32[]{:S(2)}, u32[]{:S(2)}) collective-permute-start(bf16[8,192,384]{2,1,0:T(8,128)(2,1)S(1)} %pad_maximum_fusion.2), channel_id=1, source_target_pairs={{0,16},{1,3},{2,18},{3,1},{4,20},{5,7},{6,22},{7,5},{8,24},{9,11},... | collective-permute-start | bytes 3538952 | tf_op jit(solution)/shard_map/ppermute | solution.py:38
  446.9 51.5 %collective-permute-start.24 = (bf16[16,48,1920]{2,1,0:T(8,128)(2,1)}, bf16[16,48,1920]{2,1,0:T(8,128)(2,1)}, u32[]{:S(2)}, u32[]{:S(2)}) collective-permute-start(bf16[16,48,1920]{2,1,0:T(8,128)(2,1)} %constant_dynamic-update-slice_fusion.11.mine_ref), channel_id=1, source_target_pairs={{0,1},{1,0},{2,3},{3,2},{4,5},{5,4},{6,7},{7,6},{8,9},{9,8},{10,11... | collective-permute-start | bytes 8847368 | tf_op jit(solution)/shard_map/ppermute | solution.py:42
  470.0 21.5 %collective-permute-start.34 = (bf16[16,192,384]{2,1,0:T(8,128)(2,1)}, bf16[16,192,384]{2,1,0:T(8,128)(2,1)}, u32[]{:S(2)}, u32[]{:S(2)}) collective-permute-start(bf16[16,192,384]{2,1,0:T(8,128)(2,1)} %constant_dynamic-update-slice_fusion.16.mine_ref), channel_id=1, source_target_pairs={{0,1},{1,0},{2,3},{3,2},{4,5},{5,4},{6,7},{7,6},{8,9},{9,8},{10,11... | collective-permute-start | bytes 7077896 | tf_op jit(solution)/shard_map/ppermute | solution.py:42
  471.0 10.2 %collective-permute-start.14 = (bf16[16,48,1280]{2,1,0:T(8,128)(2,1)}, bf16[16,48,1280]{2,1,0:T(8,128)(2,1)}, u32[]{:S(2)}, u32[]{:S(2)}) collective-permute-start(bf16[16,48,1280]{2,1,0:T(8,128)(2,1)} %constant_dynamic-update-slice_fusion.6.mine_ref), channel_id=1, source_target_pairs={{0,1},{1,0},{2,3},{3,2},{4,5},{5,4},{6,7},{7,6},{8,9},{9,8},{10,11... | collective-permute-start | bytes 5898248 | tf_op jit(solution)/shard_map/ppermute | solution.py:42
  (72 other events, 644.6 us)

commit v2 on v1

v2 whole, which is shorter than its diff:
```python
import math
from functools import partial

import jax
import jax.numpy as jnp
from jax import lax
from jax.experimental import pallas as pl
from jax.experimental.pallas import tpu as pltpu
from jax.sharding import PartitionSpec as P

HEADS = 12
SEG_ROW = 8
AXES = ("tower", "dp")
HOPS = ((8, 2, 4, 1), (1, 8, 2, 4))
POOL_HOPS = ((1, 4, 2), (4, 2, 1))

loss_scale = 65536.0
f32 = jnp.float32
bf16 = jnp.bfloat16
LIMIT = 56 << 20


def call_params():
    return pltpu.CompilerParams(vmem_limit_bytes=LIMIT)


def hop_pairs(dp_size, flip):
    result = []
    for device in range(2 * dp_size):
        tower, place = divmod(device, dp_size)
        tower_bit, place_bits = flip(place & 1)
        result.append((device, (tower ^ tower_bit) * dp_size + (place ^ place_bits)))
    return result


def swap_hop(value, dp_size, masks):
    pairs = hop_pairs(dp_size, lambda core: (masks[core] >> 3, (masks[core] & 7) << 1))
    return lax.ppermute(value, AXES, pairs)


def swap_core(value, dp_size):
    return lax.ppermute(value, AXES, hop_pairs(dp_size, lambda core: (0, 1)))


def swap_place(value, dp_size, bits):
    return lax.ppermute(value, AXES, hop_pairs(dp_size, lambda core: (0, bits)))


def span(masks):
    result = [0]
    for mask in reversed(masks):
        result = result + [mask ^ entry for entry in result]
    return result


def place_tables(dp_size):
    tower = lax.axis_index("tower")
    place = lax.axis_index("dp")
    core = place & 1
    unit = (tower << 3) | ((place >> 1) & 7)
    lists = []
    for hops in HOPS:
        order = span(hops)
        lists.append([order.index(mask) for mask in range(16)])
    inverse = jnp.array(lists, jnp.int32)
    rows = inverse[:, unit ^ jnp.arange(16, dtype=jnp.int32)]
    return core, jnp.where(core == 0, rows, rows[::-1])


def grad_blocks(lhs, rhs, core, table, extra=None, smalls=()):
    count, rows = lhs.shape
    half = rhs.shape[1] // 2
    half_extra = extra[1].shape[1] // 2 if extra else 0
    tile = half // 3
    block = rows // 16
    total = half + half_extra + (128 if smalls else 0)
    per_block = -(-sum(entry.shape[1] for entry, _ in smalls) // (32 * 128))
    meta = jnp.concatenate([core[None], table.reshape(32)])

    def body(meta_ref, lhs_ref, rhs_ref, *refs):
        refs = list(refs)
        turned_ref = refs.pop()
        kept_ref = refs.pop()
        sent_ref = refs.pop()
        step = pl.program_id(0)
        on_zero = meta_ref[0] == 0

        @pl.when(step == 0)
        def _():
            turned_ref[...] = lhs_ref[...].T

        part = dot(turned_ref[...], rhs_ref[...])

        @pl.when(step < 3)
        def _():
            at = pl.multiple_of(step * tile, 128)
            for number in range(16):
                sent_ref[meta_ref[17 + number], :, pl.ds(at, tile)] = part[
                    number * block : (number + 1) * block
                ].astype(bf16)

        @pl.when(step >= 3)
        def _():
            at = pl.multiple_of((step - 3) * tile, 128)
            for number in range(16):
                kept_ref[meta_ref[1 + number], :, pl.ds(at, tile)] = part[
                    number * block : (number + 1) * block
                ]

        @pl.when(step == 5)
        def _():
            at = half
            if extra:
                more = dot(refs[0][...], refs[1][...], 0, 0)
                left, right = more[:, :half_extra], more[:, half_extra:]
                kept = jnp.where(on_zero, left, right)
                sent = jnp.where(on_zero, right, left).astype(bf16)
                for number in range(16):
                    lines = slice(number * block, (number + 1) * block)
                    sent_ref[meta_ref[17 + number], :, at : at + half_extra] = sent[lines]
                    kept_ref[meta_ref[1 + number], :, at : at + half_extra] = kept[lines]
                at += half_extra
            if smalls:
                lines = []
                for (entry, row), ref in zip(smalls, refs[2 if extra else 0 :]):
                    for start in range(0, entry.shape[1], 128):
                        lines.append(ref[row : row + 1, start : start + 128])
                lines += [jnp.zeros((1, 128), f32)] * (32 * per_block - len(lines))
                fill = jnp.zeros((block - per_block, 128), f32)
                for number in range(16):
                    first = number * per_block
                    second = (16 + number) * per_block
                    left = jnp.concatenate(lines[first : first + per_block] + [fill], 0)
                    right = jnp.concatenate(lines[second : second + per_block] + [fill], 0)
                    sent_ref[meta_ref[17 + number], :, at:] = jnp.where(
                        on_zero, right, left
                    ).astype(bf16)
                    kept_ref[meta_ref[1 + number], :, at:] = jnp.where(on_zero, left, right)

    def column(step, meta_ref):
        side = jnp.where(step < 3, 1 - meta_ref[0], meta_ref[0])
        return (0, side * 3 + lax.rem(step, 3))

    operands = [lhs, rhs] + list(extra or ()) + [entry for entry, _ in smalls]
    in_specs = [
        pl.BlockSpec(lhs.shape, lambda step, meta_ref: (0, 0), pipeline_mode=pl.Buffered(1)),
        pl.BlockSpec((count, tile), column),
    ] + [
        pl.BlockSpec(entry.shape, lambda step, meta_ref: (0, 0), pipeline_mode=pl.Buffered(1))
        for entry in operands[2:]
    ]
    return pl.pallas_call(
        body,
        out_shape=[
            jax.ShapeDtypeStruct((16, block, total), bf16),
            jax.ShapeDtypeStruct((16, block, total), f32),
        ],
        grid_spec=pltpu.PrefetchScalarGridSpec(
            num_scalar_prefetch=1,
            grid=(6,),
            in_specs=in_specs,
            out_specs=[
                pl.BlockSpec((16, block, total), lambda step, meta_ref: (0, 0, 0))
                for _ in range(2)
            ],
            scratch_shapes=[pltpu.VMEM((rows, count), bf16)],
        ),
        compiler_params=call_params(),
        cost_estimate=pl.CostEstimate(
            flops=4 * count * rows * (half + half_extra),
            bytes_accessed=2 * count * (rows + 2 * half) + 6 * rows * total,
            transcendentals=0,
        ),
    )(meta, *operands)


def finish(mine, theirs, core, table, widths, small_widths=()):
    block = mine.shape[1]
    rows = 16 * block
    tiles = 4
    per_tile = 16 // tiles
    meta = jnp.concatenate([core[None], table.reshape(32)])
    per_block = -(-sum(small_widths) // (32 * 128))

    def body(meta_ref, mine_ref, theirs_ref, *outs):
        step = pl.program_id(0)

        def fill(first_ref, first_at, second_ref, second_at):
            for inner in range(per_tile):
                number = step * per_tile + inner
                first = meta_ref[first_at + number]
                second = meta_ref[second_at + number]
                start = 0
                for out_ref, width in zip(outs, widths):
                    lines = slice(inner * block, (inner + 1) * block)
                    out_ref[lines, :width] = first_ref[first, :, start : start + width].astype(f32)
                    out_ref[lines, width:] = second_ref[second, :, start : start + width].astype(
                        f32
                    )
                    start += width

            @pl.when(step == tiles - 1)
            def _():
                index = 0
                for out_ref, width in zip(outs[len(widths) :], small_widths):
                    for start_at in range(0, width, 128):
                        group, line = divmod(index, per_block)
                        ref, at = (first_ref, first_at) if group < 16 else (second_ref, second_at)
                        spot = meta_ref[at + group % 16]
                        out_ref[:, start_at : start_at + 128] = ref[
                            spot, line : line + 1, sum(widths) :
                        ].astype(f32)
                        index += 1

        @pl.when(meta_ref[0] == 0)
        def _():
            fill(mine_ref, 1, theirs_ref, 17)

        @pl.when(meta_ref[0] != 0)
        def _():
            fill(theirs_ref, 17, mine_ref, 1)

    whole = pl.BlockSpec(mine.shape, lambda step, meta_ref: (0, 0, 0))
    out_shape = [jax.ShapeDtypeStruct((rows, 2 * width), f32) for width in widths]
    out_specs = [
        pl.BlockSpec((rows // tiles, 2 * width), lambda step, meta_ref: (step, 0))
        for width in widths
    ]
    for width in small_widths:
        out_shape.append(jax.ShapeDtypeStruct((1, width), f32))
        out_specs.append(pl.BlockSpec((1, width), lambda step, meta_ref: (0, 0)))
    return pl.pallas_call(
        body,
        out_shape=out_shape,
        grid_spec=pltpu.PrefetchScalarGridSpec(
            num_scalar_prefetch=1, grid=(tiles,), in_specs=[whole, whole], out_specs=out_specs
        ),
        compiler_params=call_params(),
        cost_estimate=pl.CostEstimate(
            flops=0, bytes_accessed=6 * mine.size * 2, transcendentals=0
        ),
    )(meta, mine, theirs)


def sum_over_all(sent, kept, dp_size):
    terms = [kept, swap_core(sent, dp_size)]

    def piece(start, stop):
        return sum(term[start:stop].astype(f32) for term in terms)

    size = 16
    for hop in range(4):
        size //= 2
        part = piece(size, 2 * size).astype(bf16)
        terms.append(swap_hop(part, dp_size, (HOPS[0][hop], HOPS[1][hop])))
    own = piece(0, 1)
    bits = 16
    while bits < dp_size:
        own = own + swap_place(own.astype(bf16), dp_size, bits).astype(f32)
        bits *= 2
    whole = own.astype(bf16)
    for hop in (3, 2, 1, 0):
        whole = jnp.concatenate(
            [whole, swap_hop(whole, dp_size, (HOPS[0][hop], HOPS[1][hop]))], 0
        )
    return whole, swap_core(whole, dp_size)


def gather_pooled(pooled_low, dp_size):
    rows = lax.ppermute(pooled_low, "tower", [(0, 1), (1, 0)])[None]
    extra = []
    bits = 8
    while 2 * bits < dp_size:
        extra.append(bits)
        bits *= 2
    orders = [list(hops) + extra for hops in POOL_HOPS]
    spans = [[0], [0]]
    for first, second in zip(*orders):
        rows = jnp.concatenate(
            [rows, swap_hop(rows, dp_size, (first, second))]
            if max(first, second) < 8
            else [rows, swap_place(rows, dp_size, 2 * first)],
            0,
        )
        spans = [
            entry + [mask ^ old for old in entry] for entry, mask in zip(spans, (first, second))
        ]
    return rows, swap_core(rows, dp_size), spans


def dot(left, right, left_dim=1, right_dim=0, **kwargs):
    return lax.dot_general(
        left,
        right,
        (((left_dim,), (right_dim,)), ((), ())),
        preferred_element_type=f32,
        **kwargs,
    )


def exact_dot(left, right, left_dim=1, right_dim=0):
    return dot(left, right, left_dim, right_dim, precision=lax.Precision.HIGHEST)


def norm_parts(values_in):
    centered = values_in - jnp.mean(values_in, -1, keepdims=True)
    inv_std = lax.rsqrt(jnp.mean(centered * centered, -1, keepdims=True) + 1e-12)
    return centered * inv_std, inv_std


def norm_back(gradient, normed, inv_std, gain_vec):
    scaled = gradient * gain_vec
    inner = (
        scaled
        - jnp.mean(scaled, -1, keepdims=True)
        - normed * jnp.mean(scaled * normed, -1, keepdims=True)
    )
    return inner * inv_std


ERFC = (
    0.22567586600780487,
    0.22566956281661987,
    0.20784325897693634,
    0.16853809356689453,
    0.14144566655158997,
    -0.0056367916986346245,
    0.16911932826042175,
    -0.1829221397638321,
    0.05026727914810181,
)


def gelu_pair(up):
    bell = jnp.exp2((-0.5 / math.log(2.0)) * (up * up))
    inner = 1.0 / (1.0 + (0.4 / math.sqrt(2.0)) * jnp.abs(up))
    series = jnp.full_like(up, 0.5 * ERFC[-1])
    for factor in ERFC[-2::-1]:
        series = series * inner + 0.5 * factor
    tail = series * inner * bell
    below = jnp.where(up < 0.0, tail, 1.0 - tail)
    return up * below, below + (up * bell) * (1.0 / math.sqrt(2.0 * math.pi))


def row_spec(shape):
    return pl.BlockSpec(shape, lambda step: (step,) + (0,) * (len(shape) - 1))


def full_spec(array):
    rank = len(array.shape)
    return pl.BlockSpec(array.shape, lambda step: (0,) * rank, pipeline_mode=pl.Buffered(1))


def same_sentence(seg_row):
    length = seg_row.shape[1]
    across = jnp.broadcast_to(seg_row.astype(f32), (length, length))
    return across == across.T


def sentence_onehot(seg_refs, rows):
    length = seg_refs[0].shape[1]
    parts = []
    for row in range(rows):
        numbers = lax.broadcasted_iota(jnp.int32, (SEG_ROW, length), 0)
        hit = (numbers == seg_refs[row]).astype(f32)
        empty = jnp.zeros((SEG_ROW, length), f32)
        parts.append(jnp.concatenate([empty] * row + [hit] + [empty] * (rows - 1 - row), 1))
    return jnp.concatenate(parts, 0)


def attention_kernel(tokens, seg_rows, w_qkv, b_query, b_value, w_out, b_out):
    count, width = tokens.shape
    rows_all, length = seg_rows.shape[0], seg_rows.shape[2]
    rows = math.gcd(2, rows_all)
    tile = rows * length
    head_dim = width // HEADS
    scale = 1.0 / math.sqrt(head_dim)

    def body(tok_ref, seg_ref, wqkv_ref, bq_ref, bv_ref, wout_ref, bout_ref, *outs):
        qkv_ref, ctx_ref, sum_ref = outs
        tok = tok_ref[...]
        qkv_ref[:, :width] = (dot(tok, wqkv_ref[:, :width]) + bq_ref[...]).astype(bf16)
        qkv_ref[:, width : 2 * width] = dot(tok, wqkv_ref[:, width : 2 * width]).astype(bf16)
        qkv_ref[:, 2 * width :] = (dot(tok, wqkv_ref[:, 2 * width :]) + bv_ref[...]).astype(bf16)
        first = lax.broadcasted_iota(jnp.int32, (length, 2 * head_dim), 1) < head_dim
        zero = jnp.zeros((length, 2 * head_dim), bf16)
        for row in range(rows):
            lines = slice(row * length, (row + 1) * length)
            mask = same_sentence(seg_ref[row])
            mask = jnp.concatenate([mask, mask], 0)
            for pair in range(HEADS // 2):
                at = pair * 2 * head_dim
                query = qkv_ref[lines, at : at + 2 * head_dim]
                key = qkv_ref[lines, width + at : width + at + 2 * head_dim]
                value = qkv_ref[lines, 2 * width + at : 2 * width + at + 2 * head_dim]
                both = jnp.concatenate(
                    [jnp.where(first, query, zero), jnp.where(first, zero, query)], 0
                )
                score = jnp.where(mask, dot(both, key, 1, 1) * scale, -1e30)
                expo = jnp.exp(score - jnp.max(score, -1, keepdims=True))
                attn = (expo * (1.0 / jnp.sum(expo, -1, keepdims=True))).astype(bf16)
                attn = jnp.concatenate([attn[:length], attn[length:]], 1)
                values = jnp.concatenate(
                    [jnp.where(first, value, zero), jnp.where(first, zero, value)], 0
                )
                ctx_ref[lines, at : at + 2 * head_dim] = dot(attn, values).astype(bf16)
        sum_ref[...] = tok.astype(f32) + (dot(ctx_ref[...], wout_ref[...]) + bout_ref[...])

    operands = [w_qkv, b_query[None], b_value[None], w_out, b_out[None]]
    return pl.pallas_call(
        body,
        out_shape=[
            jax.ShapeDtypeStruct((count, 3 * width), bf16),
            jax.ShapeDtypeStruct((count, width), bf16),
            jax.ShapeDtypeStruct((count, width), f32),
        ],
        grid=(rows_all // rows,),
        in_specs=[row_spec((tile, width)), row_spec((rows, 1, length))]
        + [full_spec(entry) for entry in operands],
        out_specs=[
            row_spec((tile, 3 * width)),
            row_spec((tile, width)),
            row_spec((tile, width)),
        ],
        compiler_params=call_params(),
        cost_estimate=pl.CostEstimate(
            flops=2 * count * width * (4 * width + 2 * length),
            bytes_accessed=16 * count * width,
            transcendentals=count * HEADS * length,
        ),
    )(tokens, seg_rows, *operands)


def forward_kernel(first_sum, seg_rows, gain_one, shift_one, w_in, b_in, w_down, b_down, gain_two, shift_two):
    count, width = first_sum.shape
    rows_all, length = seg_rows.shape[0], seg_rows.shape[2]
    rows = math.gcd(2, rows_all)
    tile = rows * length
    ff_width = w_in.shape[1]
    chunk = 256

    def body(x_ref, seg_ref, g1_ref, s1_ref, win_ref, bin_ref, wdown_ref, bdown_ref, g2_ref, s2_ref, *outs):
        low_ref, act_ref, slope_ref, sum_ref, out_ref, pool_ref = outs
        normed, _ = norm_parts(x_ref[...])
        hidden = normed * g1_ref[...] + s1_ref[...]
        low = hidden.astype(bf16)
        low_ref[...] = low
        total = hidden + bdown_ref[...]
        for start in range(0, ff_width, chunk):
            part = slice(start, start + chunk)
            value, slope = gelu_pair(dot(low, win_ref[:, part]) + bin_ref[:, part])
            act = value.astype(bf16)
            act_ref[:, part] = act
            slope_ref[:, part] = slope.astype(bf16)
            total = total + dot(act, wdown_ref[part, :])
        sum_ref[...] = total
        normed, _ = norm_parts(total)
        result = normed * g2_ref[...] + s2_ref[...]
        out_ref[...] = result.astype(bf16)
        onehot = sentence_onehot([seg_ref[row] for row in range(rows)], rows)
        pool_ref[...] = (
            exact_dot(onehot, result) / jnp.sum(onehot, -1, keepdims=True)
        ).astype(bf16)

    operands = [
        gain_one[None],
        shift_one[None],
        w_in,
        b_in[None],
        w_down,
        b_down[None],
        gain_two[None],
        shift_two[None],
    ]
    return pl.pallas_call(
        body,
        out_shape=[
            jax.ShapeDtypeStruct((count, width), bf16),
            jax.ShapeDtypeStruct((count, ff_width), bf16),
            jax.ShapeDtypeStruct((count, ff_width), bf16),
            jax.ShapeDtypeStruct((count, width), f32),
            jax.ShapeDtypeStruct((count, width), bf16),
            jax.ShapeDtypeStruct((rows_all * SEG_ROW, width), bf16),
        ],
        grid=(rows_all // rows,),
        in_specs=[row_spec((tile, width)), row_spec((rows, 1, length))]
        + [full_spec(entry) for entry in operands],
        out_specs=[
            row_spec((tile, width)),
            row_spec((tile, ff_width)),
            row_spec((tile, ff_width)),
            row_spec((tile, width)),
            row_spec((tile, width)),
            row_spec((rows * SEG_ROW, width)),
        ],
        compiler_params=call_params(),
        cost_estimate=pl.CostEstimate(
            flops=4 * count * width * ff_width + 40 * count * ff_width,
            bytes_accessed=4 * count * ff_width + 12 * count * width + 4 * width * ff_width,
            transcendentals=2 * count * ff_width,
        ),
    )(first_sum, seg_rows, *operands)


def loss_kernel(meta, pairs, scores, mine, theirs, pooled_low, seg_rows, second_sum, gain_two, spans):
    count, width = second_sum.shape
    rows_all, length = seg_rows.shape[0], seg_rows.shape[2]
    rows = math.gcd(2, rows_all)
    tile = rows * length
    sentences = rows * SEG_ROW
    slots = pooled_low.shape[0]
    pair_count = pairs.shape[0] * 128
    per_row = 128 // slots
    groups = rows_all // rows

    def body(
        meta_ref, pairs_ref, scores_ref, mine_ref, theirs_ref, pool_ref, seg_ref, x_ref, g2_ref, *rest
    ):
        mid_ref, low_ref, grads_ref, other_ref, target_ref = rest
        step = pl.program_id(0)

        @pl.when(step == 0)
        def _():
            grads_ref[...] = jnp.zeros_like(grads_ref)
            place = meta_ref[1]
            on_first = meta_ref[0] == 0
            core = place & 1
            lane = lax.broadcasted_iota(jnp.int32, (1, 128), 1)

            def own_column(ref):
                line = ref[pl.ds(place // per_row, 1), :].astype(f32)
                column = jnp.broadcast_to(line, (128, 128)).T
                result = column[:slots]
                for part in range(1, per_row):
                    result = jnp.where(
                        place % per_row == part, column[part * slots : (part + 1) * slots], result
                    )
                return result

            ids = (lax.broadcasted_iota(jnp.int32, (slots, 128), 0) + place * slots).astype(f32)
            wanted = jnp.where(on_first, own_column(pairs_ref), ids)
            target = jnp.where(on_first, own_column(scores_ref), jnp.zeros((slots, 128), f32))
            other = jnp.zeros((slots, width), f32)
            gathered = jnp.zeros((slots, 128), f32)
            for side, ref in enumerate((mine_ref, theirs_ref)):
                for spot in range(len(spans[0])):
                    here = place ^ side ^ (jnp.where(core == side, spans[0][spot], spans[1][spot]) << 1)
                    line = here // per_row
                    offered = jnp.where(
                        on_first,
                        (line * 128 + lane).astype(f32),
                        pairs_ref[pl.ds(line, 1), :].astype(f32),
                    )
                    inside = (lane // slots) == here % per_row
                    hit = jnp.logical_and(wanted == offered, inside)
                    block = ref[spot]
                    other = other + dot(
                        hit.astype(f32).astype(bf16), jnp.concatenate([block] * per_row, 0)
                    )
                    gathered = gathered + jnp.where(hit, scores_ref[pl.ds(line, 1), :], 0.0)
            gathered = jnp.broadcast_to(jnp.sum(gathered, -1, keepdims=True), (slots, 128))
            target = jnp.where(on_first, target, gathered)
            for group in range(groups):
                part = slice(group * sentences, (group + 1) * sentences)
                other_ref[group] = other[part]
                target_ref[group] = target[part]

        mine = pool_ref[...].astype(f32)
        other = other_ref[step]
        inv_mine = lax.rsqrt(jnp.sum(mine * mine, -1, keepdims=True) + 1e-06)
        inv_other = lax.rsqrt(jnp.sum(other * other, -1, keepdims=True) + 1e-06)
        cosine = jnp.sum(mine * other, -1, keepdims=True) * inv_mine * inv_other
        coeff = loss_scale * 2.0 * (cosine - target_ref[step][:, :1]) / pair_count
        d_pooled = coeff * (
            other * (inv_mine * inv_other) - (cosine * inv_mine * inv_mine) * mine
        )
        onehot = sentence_onehot([seg_ref[row] for row in range(rows)], rows)
        per_token = d_pooled / jnp.sum(onehot, -1, keepdims=True)
        d_output = exact_dot(onehot, per_token, 0, 0)
        normed, inv_std = norm_parts(x_ref[...])
        d_mid = norm_back(d_output, normed, inv_std, g2_ref[...])
        mid_ref[...] = d_mid
        low_ref[...] = d_mid.astype(bf16)
        grads_ref[0:1] += jnp.sum(d_output * normed, 0, keepdims=True)
        grads_ref[1:2] += jnp.sum(d_output, 0, keepdims=True)
        grads_ref[2:3] += jnp.sum(d_mid, 0, keepdims=True)

    return pl.pallas_call(
        body,
        out_shape=[
            jax.ShapeDtypeStruct((count, width), f32),
            jax.ShapeDtypeStruct((count, width), bf16),
            jax.ShapeDtypeStruct((8, width), f32),
        ],
        grid=(groups,),
        in_specs=[
            pl.BlockSpec(memory_space=pltpu.SMEM),
            full_spec(pairs),
            full_spec(scores),
            full_spec(mine),
            full_spec(theirs),
            row_spec((sentences, width)),
            row_spec((rows, 1, length)),
            row_spec((tile, width)),
            full_spec(gain_two[None]),
        ],
        out_specs=[
            row_spec((tile, width)),
            row_spec((tile, width)),
            pl.BlockSpec((8, width), lambda step: (0, 0)),
        ],
        scratch_shapes=[
            pltpu.VMEM((groups, sentences, width), f32),
            pltpu.VMEM((groups, sentences, 128), f32),
        ],
        compiler_params=call_params(),
        cost_estimate=pl.CostEstimate(
            flops=100 * count * width, bytes_accessed=10 * count * width, transcendentals=count
        ),
    )(meta, pairs, scores, mine, theirs, pooled_low, seg_rows, second_sum, gain_two[None])


def backward_kernel(d_mid, slope, first_sum, gain_one, w_in, w_down, w_out):
    count, width = first_sum.shape
    ff_width = w_in.shape[1]
    tile = math.gcd(count, 256)
    chunk = 512

    def body(mid_ref, slope_ref, x_ref, g1_ref, win_ref, wdown_ref, wout_ref, *outs):
        up_ref, first_ref, low_ref, ctx_ref, wide_ref, grads_ref = outs

        @pl.when(pl.program_id(0) == 0)
        def _():
            grads_ref[...] = jnp.zeros_like(grads_ref)
            wide_ref[...] = jnp.zeros_like(wide_ref)

        d_hidden = mid_ref[...]
        mid_low = d_hidden.astype(bf16)
        for start in range(0, ff_width, chunk):
            part = slice(start, start + chunk)
            d_up = dot(mid_low, wdown_ref[part, :], 1, 1) * slope_ref[:, part].astype(f32)
            wide_ref[0:1, part] += jnp.sum(d_up, 0, keepdims=True)
            up_low = d_up.astype(bf16)
            up_ref[:, part] = up_low
            d_hidden = d_hidden + dot(up_low, win_ref[:, part], 1, 1)
        normed, inv_std = norm_parts(x_ref[...])
        d_first = norm_back(d_hidden, normed, inv_std, g1_ref[...])
        first_ref[...] = d_first
        first_low = d_first.astype(bf16)
        low_ref[...] = first_low
        ctx_ref[...] = dot(first_low, wout_ref[...], 1, 1).astype(bf16)
        grads_ref[0:1] += jnp.sum(d_first, 0, keepdims=True)
        grads_ref[1:2] += jnp.sum(d_hidden * normed, 0, keepdims=True)
        grads_ref[2:3] += jnp.sum(d_hidden, 0, keepdims=True)

    operands = [gain_one[None], w_in, w_down, w_out]
    return pl.pallas_call(
        body,
        out_shape=[
            jax.ShapeDtypeStruct((count, ff_width), bf16),
            jax.ShapeDtypeStruct((count, width), f32),
            jax.ShapeDtypeStruct((count, width), bf16),
            jax.ShapeDtypeStruct((count, width), bf16),
            jax.ShapeDtypeStruct((8, ff_width), f32),
            jax.ShapeDtypeStruct((8, width), f32),
        ],
        grid=(count // tile,),
        in_specs=[row_spec((tile, width)), row_spec((tile, ff_width)), row_spec((tile, width))]
        + [full_spec(entry) for entry in operands],
        out_specs=[
            row_spec((tile, ff_width)),
            row_spec((tile, width)),
            row_spec((tile, width)),
            row_spec((tile, width)),
            pl.BlockSpec((8, ff_width), lambda step: (0, 0)),
            pl.BlockSpec((8, width), lambda step: (0, 0)),
        ],
        compiler_params=call_params(),
        cost_estimate=pl.CostEstimate(
            flops=4 * count * width * ff_width + 2 * count * width * width,
            bytes_accessed=4 * count * ff_width + 16 * count * width + 4 * width * ff_width,
            transcendentals=0,
        ),
    )(d_mid, slope, first_sum, *operands)


def attention_back_kernel(qkv, d_context, seg_rows):
    count, width = d_context.shape
    rows_all, length = seg_rows.shape[0], seg_rows.shape[2]
    rows = math.gcd(2, rows_all)
    tile = rows * length
    head_dim = width // HEADS
    scale = 1.0 / math.sqrt(head_dim)

    def body(qkv_ref, dctx_ref, seg_ref, joint_ref, grads_ref):
        @pl.when(pl.program_id(0) == 0)
        def _():
            grads_ref[...] = jnp.zeros_like(grads_ref)

        first = lax.broadcasted_iota(jnp.int32, (length, 2 * head_dim), 1) < head_dim
        zero = jnp.zeros((length, 2 * head_dim), bf16)

        def split(part):
            return jnp.concatenate([jnp.where(first, part, zero), jnp.where(first, zero, part)], 0)

        def beside(part):
            return jnp.concatenate([part[:length], part[length:]], 1)

        for row in range(rows):
            lines = slice(row * length, (row + 1) * length)
            mask = same_sentence(seg_ref[row])
            mask = jnp.concatenate([mask, mask], 0)
            for pair in range(HEADS // 2):
                at = pair * 2 * head_dim
                here = slice(at, at + 2 * head_dim)
                key_here = slice(width + at, width + at + 2 * head_dim)
                value_here = slice(2 * width + at, 2 * width + at + 2 * head_dim)
                query = split(qkv_ref[lines, here])
                key = qkv_ref[lines, key_here]
                grad = split(dctx_ref[lines, here])
                score = jnp.where(mask, dot(query, key, 1, 1) * scale, -1e30)
                expo = jnp.exp(score - jnp.max(score, -1, keepdims=True))
                attn = expo * (1.0 / jnp.sum(expo, -1, keepdims=True))
                d_attn = dot(grad, qkv_ref[lines, value_here], 1, 1)
                weighted = attn * d_attn
                d_score = weighted - attn * jnp.sum(weighted, -1, keepdims=True)
                d_score = d_score.astype(bf16)
                d_value = dot(attn.astype(bf16), grad, 0, 0)
                d_key = dot(d_score, query, 0, 0) * scale
                d_query = dot(beside(d_score), split(key)) * scale
                joint_ref[lines, here] = d_query.astype(bf16)
                joint_ref[lines, key_here] = d_key.astype(bf16)
                joint_ref[lines, value_here] = d_value.astype(bf16)
                grads_ref[0:1, here] += jnp.sum(d_query, 0, keepdims=True)
                grads_ref[1:2, here] += jnp.sum(d_value, 0, keepdims=True)

    return pl.pallas_call(
        body,
        out_shape=[
            jax.ShapeDtypeStruct((count, 3 * width), bf16),
            jax.ShapeDtypeStruct((8, width), f32),
        ],
        grid=(rows_all // rows,),
        in_specs=[
            row_spec((tile, 3 * width)),
            row_spec((tile, width)),
            row_spec((rows, 1, length)),
        ],
        out_specs=[row_spec((tile, 3 * width)), pl.BlockSpec((8, width), lambda step: (0, 0))],
        compiler_params=call_params(),
        cost_estimate=pl.CostEstimate(
            flops=14 * count * width * length,
            bytes_accessed=14 * count * width,
            transcendentals=count * HEADS * length,
        ),
    )(qkv, d_context, seg_rows)


def on_device(
    tokens,
    segments,
    pairs,
    scores,
    w_qkv,
    b_query,
    b_value,
    w_out,
    b_out,
    gain_one,
    shift_one,
    w_in,
    b_in,
    w_down,
    b_down,
    gain_two,
    shift_two,
):
    dp_size = lax.axis_size("dp")
    core, table = place_tables(dp_size)
    place = jnp.stack([lax.axis_index("tower"), lax.axis_index("dp")]).astype(jnp.int32)
    flat_rows = tokens[0]
    seg_rows = segments[0][:, None, :]
    width = flat_rows.shape[1]
    ff_width = w_in.shape[1]
    qkv, context, first_sum = attention_kernel(
        flat_rows, seg_rows, w_qkv, b_query, b_value, w_out, b_out
    )
    hidden_low, act, slope, second_sum, output_rows, pooled_low = forward_kernel(
        first_sum, seg_rows, gain_one, shift_one, w_in, b_in, w_down, b_down, gain_two, shift_two
    )
    mine, theirs, spans = gather_pooled(pooled_low, dp_size)
    d_mid, d_mid_low, grads_two = loss_kernel(
        place,
        pairs.reshape(-1, 128),
        scores.reshape(-1, 128),
        mine,
        theirs,
        pooled_low,
        seg_rows,
        second_sum,
        gain_two,
        spans,
    )
    grad_w_down = jnp.einsum("nf,nd->fd", act, d_mid_low, preferred_element_type=f32)
    grad_w_down = lax.psum(grad_w_down.astype(bf16), AXES)
    d_up_low, d_first, d_first_low, d_context, grads_wide, grads_one = backward_kernel(
        d_mid, slope, first_sum, gain_one, w_in, w_down, w_out
    )
    in_sum = sum_over_all(
        *grad_blocks(hidden_low, d_up_low, core, table, (context, d_first_low)), dp_size
    )
    d_joint, grads_attn = attention_back_kernel(qkv, d_context, seg_rows)
    qkv_sum = sum_over_all(
        *grad_blocks(
            flat_rows,
            d_joint,
            core,
            table,
            None,
            [
                (grads_attn, 0),
                (grads_attn, 1),
                (grads_one, 0),
                (grads_one, 1),
                (grads_one, 2),
                (grads_wide, 0),
                (grads_two, 2),
                (grads_two, 0),
                (grads_two, 1),
            ],
        ),
        dp_size,
    )
    grad_tokens = d_first + jnp.einsum("ne,de->nd", d_joint, w_qkv, preferred_element_type=f32)
    grad_w_in, grad_w_out = finish(*in_sum, core, table, [ff_width // 2, width // 2])
    small_widths = [width] * 5 + [ff_width] + [width] * 3
    grad_w_qkv, *smalls = finish(*qkv_sum, core, table, [3 * width // 2], small_widths)
    smalls = [entry.reshape(-1) for entry in smalls]
    return (
        output_rows[None],
        grad_tokens[None],
        grad_w_qkv,
        smalls[0],
        smalls[1],
        grad_w_out,
        smalls[2],
        smalls[3],
        smalls[4],
        grad_w_in,
        smalls[5],
        grad_w_down.astype(f32),
        smalls[6],
        smalls[7],
        smalls[8],
    )


def solution(mesh):
    return jax.shard_map(
        on_device,
        mesh=mesh,
        in_specs=(
            P("tower", "dp", None),
            P("tower", "dp", None),
            P(),
            P(),
            P(),
            P(),
            P(),
            P(),
            P(),
            P(),
            P(),
            P(),
            P(),
            P(),
            P(),
            P(),
            P(),
        ),
        out_specs=(
            P("tower", "dp", None),
            P("tower", "dp", None),
            P(),
            P(),
            P(),
            P(),
            P(),
            P(),
            P(),
            P(),
            P(),
            P(),
            P(),
            P(),
            P(),
        ),
        check_vma=False,
    )
```

time: 512 us -> 479 us (0.936)
  matrix products: 114 us -> 13.5 us
  waiting for transfers between devices: 110 us -> 210 us
  local copies, waits for them, and re-layouts: 95.9 us -> 22.5 us
  Pallas kernels: 70.7 us -> 143 us
  other arithmetic: 72.9 us -> 33.1 us
  between operations: 1.87 us -> 14.3 us
    psum x0 -> x1, waiting for transfers between devices: none -> 131 us  [on_device(): grad_w_down = lax.psum(grad_w_down.astype(bf16), AXES)]
    dot_general x16 -> x1, matrix products: 105 us -> 6.91 us  [on_device(): jnp.einsum('nf,nd->fd', act, d_mid_low, preferred_element_type=f32)]
    pallas_call x6 -> x7, Pallas kernels: 49.7 us -> 129 us  [the longest x2 28 us: grad_blocks(): pl.pallas_call(body, out_shape=[jax.ShapeDtypeStruct((16, block, total),...]
    unnamed x167 -> x30, local copies, waits for them, and re-layouts: 44.9 us -> 8.13 us
    ppermute x27 -> x19, waiting for transfers between devices: 110 us -> 76.2 us  [swap_hop(): return lax.ppermute(value, AXES, pairs)]
    reshape x8 -> x0, local copies, waits for them, and re-layouts: 15.2 us -> none  [the longest x1 2.96 us: on_device(): context = context.astype(bf16).reshape(token_count, model_width)]
    reduce_sum x10 -> x0, other arithmetic: 14.7 us -> none  [the longest x1 2.19 us: on_device(): grad_b_query = jnp.sum(d_query, 0)]
    convert_element_type x12 -> x8, other arithmetic: 20.4 us -> 8.63 us  [sum_over_all(): part = piece(size, 2 * size).astype(bf16)]
  transfers between devices with their start and end apart: 35 -> 26, of which waited for: 15 -> 17; matrix products, arithmetic and copies ran while one was open for 24% -> 11% of each run, Pallas kernels for 11% -> 9%
where the time goes in v2:
time: 479 us; the launch traced here: 478 us
  waiting for transfers between devices  210 us (44%)
  Pallas kernels  143 us (30%)
  starting transfers between devices  41.4 us (9%)
  other arithmetic  33.1 us (7%)
  local copies, waits for them, and re-layouts  22.5 us (5%)
  between operations  14.3 us (3%)
  matrix products  13.5 us (3%)
    psum x1, waiting for transfers between devices, on_device(): grad_w_down = lax.psum(grad_w_down.astype(bf16), AXES)  131 us
    ppermute x19, waiting for transfers between devices, swap_hop(): return lax.ppermute(value, AXES, pairs)  76.2 us
    ppermute x19, starting transfers between devices, swap_hop(): return lax.ppermute(value, AXES, pairs)  37.5 us
    pallas_call x2, Pallas kernels, grad_blocks(): pl.pallas_call(body, out_shape=[jax.ShapeDtypeStruct((16, block, total),...  28 us
    pallas_call x1, Pallas kernels, forward_kernel(): pl.pallas_call(body, out_shape=[jax.ShapeDtypeStruct((count, width), bf16...  27.7 us
    pallas_call x1, Pallas kernels, attention_back_kernel(): pl.pallas_call(body, out_shape=[jax.ShapeDtypeStruct((count, 3 * width),...  26.3 us
    pallas_call x1, Pallas kernels, backward_kernel(): pl.pallas_call(body, out_shape=[jax.ShapeDtypeStruct((count, ff_width), b...  22.7 us
    pallas_call x1, Pallas kernels, attention_kernel(): pl.pallas_call(body, out_shape=[jax.ShapeDtypeStruct((count, 3 * width),...  15.6 us
  transfers between devices with their start and end apart: 26, of which 17 were waited for; matrix products, arithmetic and copies ran while one was open for 11% of the time, Pallas kernels for 9%

profile of v2, /device:TPU:0, one launch (start us, length us, event | category | flops | bytes accessed | tf_op | source)
XLA Modules:
  0.0 478.3 jit_solution(11609537522582921949)
XLA Ops:
  17.4 15.6 %shard_map.289 = (bf16[1024,2304]{1,0:T(8,128)(2,1)}, bf16[1024,768]{1,0:T(8,128)(2,1)}, f32[1024,768]{1,0:T(8,128)}) custom-call(bf16[1024,768]{1,0:T(8,128)(2,1)} %bitcast.32, s32[8,1,128]{2,1,0:T(1,128)} %bitcast.26, bf16[768,2304]{1,0:T(8,128)(2,1)} %wqkv_ref.1, f32[1,768]{1,0:T(1,128)} %broadcast_in_dim.45.bq_ref, f32[1,768]{1,0:T(1,128)} %broadcast_in_dim.46.bv_ref, ...), custom_call_target="tpu_custom_call" | custom-call | flops 5234491392 | bytes 12582912 | tf_op jit(solution)/shard_map/pallas_call | solution.py:410
  32.9 27.7 %shard_map.290 = (bf16[1024,768]{1,0:T(8,128)(2,1)}, bf16[1024,3072]{1,0:T(8,128)(2,1)}, bf16[1024,3072]{1,0:T(8,128)(2,1)}, f32[1024,768]{1,0:T(8,128)}, bf16[1...) custom-call(f32[1024,768]{1,0:T(8,128)} %get-tuple-element.51.x_ref, s32[8,1,128]{2,1,0:T(1,128)} %bitcast.27, ...), custom_call_target="tpu_custom_call" | custom-call | flops 9789505536 | bytes 31457280 | tf_op jit(solution)/shard_map/pallas_call | solution.py:475
  60.7 3.0 collective-permute-start
  63.7 3.0 collective-permute-done
  71.3 3.0 collective-permute-start.2
  74.3 5.8 %collective-permute-done.2 = bf16[2,64,768]{2,1,0:T(8,128)(2,1)S(1)} collective-permute-done((bf16[2,64,768]{2,1,0:T(8,128)(2,1)S(1)}, bf16[2,64,768]{2,1,0:T(8,128)(2,1)S(1)}, u32[]{:S(2)}, u32[]{:S(2)}) %collective-permute-start.2) | collective-permute-done | bytes 196640 | tf_op jit(solution)/shard_map/ppermute | solution.py:38
  81.2 6.8 %collective-permute-done.3 = bf16[4,64,768]{2,1,0:T(8,128)(2,1)S(1)} collective-permute-done((bf16[4,64,768]{2,1,0:T(8,128)(2,1)S(1)}, bf16[4,64,768]{2,1,0:T(8,128)(2,1)S(1)}, u32[]{:S(2)}, u32[]{:S(2)}) %collective-permute-start.3) | collective-permute-done | bytes 393248 | tf_op jit(solution)/shard_map/ppermute | solution.py:38
  91.3 8.9 %shard_map.291 = (f32[1024,768]{1,0:T(8,128)}, bf16[1024,768]{1,0:T(8,128)(2,1)}, f32[8,768]{1,0:T(8,128)}) custom-call(s32[2]{0:T(128)} %pad_add_fusion.meta_ref, s32[8,128]{1,0:T(8,128)} %bitcast.30, f32[8,128]{1,0:T(8,128)} %bitcast.31, bf16[8,64,768]{2,1,0:T(8,128)(2,1)} %copy-done.3, bf16[8,64,768]{2,1,0:T(8,128)(2,1)} %copy-done.6, ...), custom_call_target="tpu_custom_call" | custom-call | flops 78643200 | bytes 7864320 | tf_op jit(solution)/shard_map/pallas_call | solution.py:588
  100.3 22.7 %shard_map.292 = (bf16[1024,3072]{1,0:T(8,128)(2,1)}, f32[1024,768]{1,0:T(8,128)}, bf16[1024,768]{1,0:T(8,128)(2,1)}, bf16[1024,768]{1,0:T(8,128)(2,1)}, f32[8,3072]{1,0:T(8,128)}, /*index=5*/f32[8,768]{1,0:T(8,128)}) custom-call(f32[1024,768]{1,0:T(8,128)} %get-tuple-element.55.mid_ref, bf16[1024,3072]{1,0:T(8,128)(2,1)} %get-tuple-element.56.slope_ref, ...), custom_call_target="tpu_custom_call" | custom-call | flops 10871635968 | bytes 34603008 | tf_op jit(solution)/shard_map/pallas_call | solution.py:657
  122.9 15.7 %shard_map.296 = (bf16[16,48,1920]{2,1,0:T(8,128)(2,1)}, f32[16,48,1920]{2,1,0:T(8,128)}) custom-call(s32[33]{0:T(128)} %pad_add_fusion.1.meta_ref, bf16[1024,768]{1,0:T(8,128)(2,1)} %get-tuple-element.70.lhs_ref, bf16[1024,3072]{1,0:T(8,128)(2,1)} %get-tuple-element.71.rhs_ref, bf16[1024,768]{1,0:T(8,128)(2,1)} %get-tuple-element.72.refs_0_, ...), custom_call_target="tpu_custom_call" | custom-call | flops 6039797760 | bytes 16711680 | tf_op jit(solution)/shard_map/pallas_call | solution.py:152
  138.9 26.3 %shard_map.293 = (bf16[1024,2304]{1,0:T(8,128)(2,1)}, f32[8,768]{1,0:T(8,128)}) custom-call(bf16[1024,2304]{1,0:T(8,128)(2,1)} %get-tuple-element.58.qkv_ref, bf16[1024,768]{1,0:T(8,128)(2,1)} %get-tuple-element.59.dctx_ref, s32[8,1,128]{2,1,0:T(1,128)} %bitcast.29), custom_call_target="tpu_custom_call" | custom-call | flops 1409286144 | bytes 11010048 | tf_op jit(solution)/shard_map/pallas_call | solution.py:737
  169.8 12.3 %shard_map.294 = (bf16[16,48,1280]{2,1,0:T(8,128)(2,1)}, f32[16,48,1280]{2,1,0:T(8,128)}) custom-call(s32[33]{0:T(128)} %pad_add_fusion.1.meta_ref, bf16[1024,768]{1,0:T(8,128)(2,1)} %bitcast.33, bf16[1024,2304]{1,0:T(8,128)(2,1)} %get-tuple-element.60.rhs_ref, f32[8,768]{1,0:T(8,128)} %get-tuple-element.61.refs_0_.refs_1_, ...), custom_call_target="tpu_custom_call" | custom-call | flops 3623878656 | bytes 12189696 | tf_op jit(solution)/shard_map/pallas_call | solution.py:152
  182.1 5.5 %collective-permute-done.16 = bf16[8,48,1920]{2,1,0:T(8,128)(2,1)S(1)} collective-permute-done((bf16[8,48,1920]{2,1,0:T(8,128)(2,1)}, bf16[8,48,1920]{2,1,0:T(8,128)(2,1)S(1)}, u32[]{:S(2)}, u32[]{:S(2)}) %collective-permute-start.16) | collective-permute-done | bytes 1474592 | tf_op jit(solution)/shard_map/ppermute | solution.py:38
  193.4 7.0 %collective-permute-done.17 = bf16[4,48,1920]{2,1,0:T(8,128)(2,1)S(1)} collective-permute-done((bf16[4,48,1920]{2,1,0:T(8,128)(2,1)S(1)}, bf16[4,48,1920]{2,1,0:T(8,128)(2,1)S(1)}, u32[]{:S(2)}, u32[]{:S(2)}) %collective-permute-start.17) | collective-permute-done | bytes 737312 | tf_op jit(solution)/shard_map/ppermute | solution.py:38
  204.0 10.0 %collective-permute-done.18 = bf16[2,48,1920]{2,1,0:T(8,128)(2,1)S(1)} collective-permute-done((bf16[2,48,1920]{2,1,0:T(8,128)(2,1)S(1)}, bf16[2,48,1920]{2,1,0:T(8,128)(2,1)S(1)}, u32[]{:S(2)}, u32[]{:S(2)}) %collective-permute-start.18) | collective-permute-done | bytes 368672 | tf_op jit(solution)/shard_map/ppermute | solution.py:38
  217.6 3.1 collective-permute-done.19
  226.4 2.8 collective-permute-start.8
  229.9 7.1 %collective-permute-done.8 = bf16[2,48,1280]{2,1,0:T(8,128)(2,1)S(1)} collective-permute-done((bf16[2,48,1280]{2,1,0:T(8,128)(2,1)S(1)}, bf16[2,48,1280]{2,1,0:T(8,128)(2,1)S(1)}, u32[]{:S(2)}, u32[]{:S(2)}) %collective-permute-start.8) | collective-permute-done | bytes 245792 | tf_op jit(solution)/shard_map/ppermute | solution.py:38
  237.1 4.7 collective-permute-start.9
  241.8 5.6 %collective-permute-done.21 = bf16[2,48,1920]{2,1,0:T(8,128)(2,1)S(1)} collective-permute-done((bf16[2,48,1920]{2,1,0:T(8,128)(2,1)S(1)}, bf16[2,48,1920]{2,1,0:T(8,128)(2,1)S(1)}, u32[]{:S(2)}, u32[]{:S(2)}) %collective-permute-start.21) | collective-permute-done | bytes 368672 | tf_op jit(solution)/shard_map/ppermute | solution.py:38
  247.4 3.3 collective-permute-start.22
  251.5 5.0 %collective-permute-done.10 = bf16[1,48,1280]{2,1,0:T(8,128)(2,1)S(1)} collective-permute-done((bf16[1,48,1280]{2,1,0:T(8,128)(2,1)S(1)}, bf16[1,48,1280]{2,1,0:T(8,128)(2,1)S(1)}, u32[]{:S(2)}, u32[]{:S(2)}) %collective-permute-start.10) | collective-permute-done | bytes 122912 | tf_op jit(solution)/shard_map/ppermute | solution.py:38
  256.5 4.3 collective-permute-start.11
  260.9 4.6 collective-permute-done.22
  268.4 7.6 %collective-permute-done.12 = bf16[4,48,1280]{2,1,0:T(8,128)(2,1)S(1)} collective-permute-done((bf16[4,48,1280]{2,1,0:T(8,128)(2,1)S(1)}, bf16[4,48,1280]{2,1,0:T(8,128)(2,1)S(1)}, u32[]{:S(2)}, u32[]{:S(2)}) %collective-permute-start.12) | collective-permute-done | bytes 491552 | tf_op jit(solution)/shard_map/ppermute | solution.py:38
  281.9 3.2 collective-permute-done.23
  286.3 6.9 %convolution_convert_fusion = bf16[3072,768]{1,0:T(8,128)(2,1)} fusion(bf16[1024,3072]{1,0:T(8,128)(2,1)S(1)} %bitcast.38, bf16[1024,768]{1,0:T(8,128)(2,1)S(1)} %copy-done.9), kind=kOutput, calls=%fused_computation.1 | convolution fusion | flops 4834197504 | bytes 12582912 | tf_op jit(solution)/shard_map/nf,nd->fd/dot_general | solution.py:804
  299.2 6.6 %fusion.1 = f32[1024,768]{1,0:T(8,128)S(1)} fusion(bf16[1024,2304]{1,0:T(8,128)(2,1)} %get-tuple-element.60.rhs_ref, bf16[768,2304]{1,0:T(8,128)(2,1)S(1)} %copy-done.8), kind=kOutput, calls=%fused_computation.38 | convolution fusion | flops 3623878656 | bytes 11403264 | tf_op jit(solution)/shard_map/ne,de->nd/dot_general | solution.py:834
  307.9 130.8 %all-reduce.2.cloned.1.call-done = bf16[3072,768]{1,0:T(8,128)(2,1)} async-done(((bf16[3072,768]{1,0:T(8,128)(2,1)}), bf16[3072,768]{1,0:T(8,128)(2,1)}) %all-reduce.2.cloned.1.call-update) | async-done | bytes 4718608 | tf_op jit(solution)/shard_map/psum | solution.py:805
  438.7 6.8 %convert_element_type.167 = f32[3072,768]{1,0:T(8,128)} convert(bf16[3072,768]{1,0:T(8,128)(2,1)} %all-reduce.2.cloned.1.call-done) | non-fusion elementwise | flops 2359296 | bytes 14155776 | tf_op jit(solution)/shard_map/convert_element_type | solution.py:851
  445.5 6.1 %shard_map.295 = (f32[768,2304]{1,0:T(8,128)}, f32[1,768]{1,0:T(1,128)}, f32[1,768]{1,0:T(1,128)}, f32[1,768]{1,0:T(1,128)}, f32[1,768]{1,0:T(1,128)}, /*index=5...) custom-call(s32[33]{0:T(128)} %pad_add_fusion.1.meta_ref, ...), custom_call_target="tpu_custom_call" | custom-call | bytes 11796480 | tf_op jit(solution)/shard_map/pallas_call | solution.py:232
  463.5 7.9 %shard_map.297 = (f32[768,3072]{1,0:T(8,128)}, f32[768,768]{1,0:T(8,128)}) custom-call(s32[33]{0:T(128)} %pad_add_fusion.1.meta_ref, bf16[16,48,1920]{2,1,0:T(8,128)(2,1)} %constant_dynamic-update-slice_fusion.5.mine_ref, bf16[16,48,1920]{2,1,0:T(8,128)(2,1)} %copy-done.4), custom_call_target="tpu_custom_call" | custom-call | bytes 17694720 | tf_op jit(solution)/shard_map/pallas_call | solution.py:232
  (111 shorter events, 74.1 us)
Async XLA Ops:
  7.2 431.5 %all-reduce.2.cloned.1.call-start = ((), (), s32[]{:S(2)}) async-start(), calls=%async_computation | async-start | bytes 9437184 | tf_op jit(solution)/shard_map/psum | solution.py:805
  32.9 55.3 %copy-start.7 = (s32[2,16]{0,1:T(8,128)S(1)}, s32[2,16]{0,1:T(8,128)}, u32[]{:S(2)}) copy-start(s32[2,16]{0,1:T(8,128)} %constant.22.clone) | copy-start | bytes 388
  60.7 6.0 %collective-permute-start = (bf16[64,768]{1,0:T(8,128)(2,1)}, bf16[64,768]{1,0:T(8,128)(2,1)S(1)}, u32[]{:S(2)}, u32[]{:S(2)}) collective-permute-start(bf16[64,768]{1,0:T(8,128)(2,1)} %get-tuple-element.53.pool_ref), channel_id=1, source_target_pairs={{0,16},{16,0},{1,17},{17,1},{2,18},{18,2},{3,19},{19,3},{4,20},{20... | collective-permute-start | bytes 294920 | tf_op jit(solution)/shard_map/ppermute | solution.py:270
  66.7 4.6 collective-permute-start.1
  71.3 8.8 %collective-permute-start.2 = (bf16[2,64,768]{2,1,0:T(8,128)(2,1)S(1)}, bf16[2,64,768]{2,1,0:T(8,128)(2,1)S(1)}, u32[]{:S(2)}, u32[]{:S(2)}) collective-permute-start(bf16[2,64,768]{2,1,0:T(8,128)(2,1)S(1)} %pad_maximum_fusion.8), channel_id=1, source_target_pairs={{0,8},{1,5},{2,10},{3,7},{4,12},{5,1},{6,14},{7,3},{8,0},{9,13},{1... | collective-permute-start | bytes 589832 | tf_op jit(solution)/shard_map/ppermute | solution.py:38
  80.2 7.8 %collective-permute-start.3 = (bf16[4,64,768]{2,1,0:T(8,128)(2,1)S(1)}, bf16[4,64,768]{2,1,0:T(8,128)(2,1)S(1)}, u32[]{:S(2)}, u32[]{:S(2)}) collective-permute-start(bf16[4,64,768]{2,1,0:T(8,128)(2,1)S(1)} %pad_maximum_fusion.5), channel_id=1, source_target_pairs={{0,4},{1,3},{2,6},{3,1},{4,0},{5,7},{6,2},{7,5},{8,12},{9,11},{10,... | collective-permute-start | bytes 1179656 | tf_op jit(solution)/shard_map/ppermute | solution.py:38
  88.1 2.4 collective-permute-start.4
  138.7 26.6 %collective-permute-start.15 = (bf16[16,48,1920]{2,1,0:T(8,128)(2,1)}, bf16[16,48,1920]{2,1,0:T(8,128)(2,1)}, u32[]{:S(2)}, u32[]{:S(2)}) collective-permute-start(bf16[16,48,1920]{2,1,0:T(8,128)(2,1)} %get-tuple-element.75), channel_id=1, source_target_pairs={{0,1},{1,0},{2,3},{3,2},{4,5},{5,4},{6,7},{7,6},{8,9},{9,8},{10,11... | collective-permute-start | bytes 8847368 | tf_op jit(solution)/shard_map/ppermute | solution.py:42
  138.9 26.3 %copy-start = (f32[16,48,1920]{2,1,0:T(8,128)S(1)}, f32[16,48,1920]{2,1,0:T(8,128)}, u32[]{:S(2)}) copy-start(f32[16,48,1920]{2,1,0:T(8,128)} %get-tuple-element.74) | copy-start | bytes 17694724
  168.0 19.6 %collective-permute-start.16 = (bf16[8,48,1920]{2,1,0:T(8,128)(2,1)}, bf16[8,48,1920]{2,1,0:T(8,128)(2,1)S(1)}, u32[]{:S(2)}, u32[]{:S(2)}) collective-permute-start(bf16[8,48,1920]{2,1,0:T(8,128)(2,1)} %add_convert_fusion), channel_id=1, source_target_pairs={{0,16},{1,3},{2,18},{3,1},{4,20},{5,7},{6,22},{7,5},{8,24},{9,11},... | collective-permute-start | bytes 4423688 | tf_op jit(solution)/shard_map/ppermute | solution.py:38
  182.1 7.9 %collective-permute-start.5 = (bf16[16,48,1280]{2,1,0:T(8,128)(2,1)}, bf16[16,48,1280]{2,1,0:T(8,128)(2,1)S(1)}, u32[]{:S(2)}, u32[]{:S(2)}) collective-permute-start(bf16[16,48,1280]{2,1,0:T(8,128)(2,1)} %get-tuple-element.66), channel_id=1, source_target_pairs={{0,1},{1,0},{2,3},{3,2},{4,5},{5,4},{6,7},{7,6},{8,9},{9,8},{10,11... | collective-permute-start | bytes 5898248 | tf_op jit(solution)/shard_map/ppermute | solution.py:42
  188.9 11.5 %collective-permute-start.17 = (bf16[4,48,1920]{2,1,0:T(8,128)(2,1)S(1)}, bf16[4,48,1920]{2,1,0:T(8,128)(2,1)S(1)}, u32[]{:S(2)}, u32[]{:S(2)}) collective-permute-start(bf16[4,48,1920]{2,1,0:T(8,128)(2,1)S(1)} %add_convert_fusion.2), channel_id=1, source_target_pairs={{0,4},{1,17},{2,6},{3,19},{4,0},{5,21},{6,2},{7,23},{8,12},{9,25},... | collective-permute-start | bytes 2211848 | tf_op jit(solution)/shard_map/ppermute | solution.py:38
  189.9 27.0 %copy-start.1 = (f32[16,48,1280]{2,1,0:T(8,128)S(1)}, f32[16,48,1280]{2,1,0:T(8,128)}, u32[]{:S(2)}) copy-start(f32[16,48,1280]{2,1,0:T(8,128)} %get-tuple-element.65) | copy-start | bytes 11796484
  191.9 25.1 %collective-permute-start.6 = (bf16[8,48,1280]{2,1,0:T(8,128)(2,1)S(1)}, bf16[8,48,1280]{2,1,0:T(8,128)(2,1)S(1)}, u32[]{:S(2)}, u32[]{:S(2)}) collective-permute-start(bf16[8,48,1280]{2,1,0:T(8,128)(2,1)S(1)} %add_convert_fusion.1), channel_id=1, source_target_pairs={{0,16},{1,3},{2,18},{3,1},{4,20},{5,7},{6,22},{7,5},{8,24},{9,11},... | collective-permute-start | bytes 2949128 | tf_op jit(solution)/shard_map/ppermute | solution.py:38
  201.6 12.4 %collective-permute-start.18 = (bf16[2,48,1920]{2,1,0:T(8,128)(2,1)S(1)}, bf16[2,48,1920]{2,1,0:T(8,128)(2,1)S(1)}, u32[]{:S(2)}, u32[]{:S(2)}) collective-permute-start(bf16[2,48,1920]{2,1,0:T(8,128)(2,1)S(1)} %add_convert_fusion.4), channel_id=1, source_target_pairs={{0,8},{1,5},{2,10},{3,7},{4,12},{5,1},{6,14},{7,3},{8,0},{9,13},{1... | collective-permute-start | bytes 1105928 | tf_op jit(solution)/shard_map/ppermute | solution.py:38
  215.1 5.6 %collective-permute-start.19 = (bf16[1,48,1920]{2,1,0:T(8,128)(2,1)S(1)}, bf16[1,48,1920]{2,1,0:T(8,128)(2,1)S(1)}, u32[]{:S(2)}, u32[]{:S(2)}) collective-permute-start(bf16[1,48,1920]{2,1,0:T(8,128)(2,1)S(1)} %add_convert_fusion.7), channel_id=1, source_target_pairs={{0,2},{1,9},{2,0},{3,11},{4,6},{5,13},{6,4},{7,15},{8,10},{9,1},{1... | collective-permute-start | bytes 552968 | tf_op jit(solution)/shard_map/ppermute | solution.py:38
  217.2 9.1 %collective-permute-start.7 = (bf16[4,48,1280]{2,1,0:T(8,128)(2,1)S(1)}, bf16[4,48,1280]{2,1,0:T(8,128)(2,1)S(1)}, u32[]{:S(2)}, u32[]{:S(2)}) collective-permute-start(bf16[4,48,1280]{2,1,0:T(8,128)(2,1)S(1)} %add_convert_fusion.3), channel_id=1, source_target_pairs={{0,4},{1,17},{2,6},{3,19},{4,0},{5,21},{6,2},{7,23},{8,12},{9,25},... | collective-permute-start | bytes 1474568 | tf_op jit(solution)/shard_map/ppermute | solution.py:38
  222.4 6.8 %collective-permute-start.20 = (bf16[1,48,1920]{2,1,0:T(8,128)(2,1)S(1)}, bf16[1,48,1920]{2,1,0:T(8,128)(2,1)S(1)}, u32[]{:S(2)}, u32[]{:S(2)}) collective-permute-start(bf16[1,48,1920]{2,1,0:T(8,128)(2,1)S(1)} %get-tuple-element.88), channel_id=1, source_target_pairs={{0,2},{1,9},{2,0},{3,11},{4,6},{5,13},{6,4},{7,15},{8,10},{9,1},{1... | collective-permute-start | bytes 552968 | tf_op jit(solution)/shard_map/ppermute | solution.py:38
  226.3 60.0 %slice-start = ((s8[6291456]{0:T(1024)(128)(4,1)}), s8[4194304]{0:T(1024)(128)(4,1)S(1)}, s32[]{:S(2)}) async-start(s8[6291456]{0:T(1024)(128)(4,1)} %bitcast.37), calls=%async_computation.1 | async-start | bytes 8388608
  226.4 10.6 %collective-permute-start.8 = (bf16[2,48,1280]{2,1,0:T(8,128)(2,1)S(1)}, bf16[2,48,1280]{2,1,0:T(8,128)(2,1)S(1)}, u32[]{:S(2)}, u32[]{:S(2)}) collective-permute-start(bf16[2,48,1280]{2,1,0:T(8,128)(2,1)S(1)} %add_convert_fusion.5), channel_id=1, source_target_pairs={{0,8},{1,5},{2,10},{3,7},{4,12},{5,1},{6,14},{7,3},{8,0},{9,13},{1... | collective-permute-start | bytes 737288 | tf_op jit(solution)/shard_map/ppermute | solution.py:38
  229.3 18.0 %collective-permute-start.21 = (bf16[2,48,1920]{2,1,0:T(8,128)(2,1)S(1)}, bf16[2,48,1920]{2,1,0:T(8,128)(2,1)S(1)}, u32[]{:S(2)}, u32[]{:S(2)}) collective-permute-start(bf16[2,48,1920]{2,1,0:T(8,128)(2,1)S(1)} %pad_maximum_fusion.6), channel_id=1, source_target_pairs={{0,8},{1,5},{2,10},{3,7},{4,12},{5,1},{6,14},{7,3},{8,0},{9,13},{1... | collective-permute-start | bytes 1105928 | tf_op jit(solution)/shard_map/ppermute | solution.py:38
  237.1 13.7 %collective-permute-start.9 = (bf16[1,48,1280]{2,1,0:T(8,128)(2,1)S(1)}, bf16[1,48,1280]{2,1,0:T(8,128)(2,1)S(1)}, u32[]{:S(2)}, u32[]{:S(2)}) collective-permute-start(bf16[1,48,1280]{2,1,0:T(8,128)(2,1)S(1)} %add_convert_fusion.9), channel_id=1, source_target_pairs={{0,2},{1,9},{2,0},{3,11},{4,6},{5,13},{6,4},{7,15},{8,10},{9,1},{1... | collective-permute-start | bytes 368648 | tf_op jit(solution)/shard_map/ppermute | solution.py:38
  247.4 18.0 %collective-permute-start.22 = (bf16[4,48,1920]{2,1,0:T(8,128)(2,1)S(1)}, bf16[4,48,1920]{2,1,0:T(8,128)(2,1)S(1)}, u32[]{:S(2)}, u32[]{:S(2)}) collective-permute-start(bf16[4,48,1920]{2,1,0:T(8,128)(2,1)S(1)} %pad_maximum_fusion.3), channel_id=1, source_target_pairs={{0,4},{1,17},{2,6},{3,19},{4,0},{5,21},{6,2},{7,23},{8,12},{9,25},... | collective-permute-start | bytes 2211848 | tf_op jit(solution)/shard_map/ppermute | solution.py:38
  251.5 5.0 %collective-permute-start.10 = (bf16[1,48,1280]{2,1,0:T(8,128)(2,1)S(1)}, bf16[1,48,1280]{2,1,0:T(8,128)(2,1)S(1)}, u32[]{:S(2)}, u32[]{:S(2)}) collective-permute-start(bf16[1,48,1280]{2,1,0:T(8,128)(2,1)S(1)} %get-tuple-element.90), channel_id=1, source_target_pairs={{0,2},{1,9},{2,0},{3,11},{4,6},{5,13},{6,4},{7,15},{8,10},{9,1},{1... | collective-permute-start | bytes 368648 | tf_op jit(solution)/shard_map/ppermute | solution.py:38
  256.5 29.8 %slice-start.1 = ((s8[6291456]{0:T(1024)(128)(4,1)}), s8[2097152]{0:T(1024)(128)(4,1)S(1)}, s32[]{:S(2)}) async-start(s8[6291456]{0:T(1024)(128)(4,1)} %bitcast.37), calls=%async_computation.2 | async-start | bytes 4194304
  256.5 10.5 %collective-permute-start.11 = (bf16[2,48,1280]{2,1,0:T(8,128)(2,1)S(1)}, bf16[2,48,1280]{2,1,0:T(8,128)(2,1)S(1)}, u32[]{:S(2)}, u32[]{:S(2)}) collective-permute-start(bf16[2,48,1280]{2,1,0:T(8,128)(2,1)S(1)} %pad_maximum_fusion.7), channel_id=1, source_target_pairs={{0,8},{1,5},{2,10},{3,7},{4,12},{5,1},{6,14},{7,3},{8,0},{9,13},{1... | collective-permute-start | bytes 737288 | tf_op jit(solution)/shard_map/ppermute | solution.py:38
  265.7 19.4 %collective-permute-start.23 = (bf16[8,48,1920]{2,1,0:T(8,128)(2,1)S(1)}, bf16[8,48,1920]{2,1,0:T(8,128)(2,1)S(1)}, u32[]{:S(2)}, u32[]{:S(2)}) collective-permute-start(bf16[8,48,1920]{2,1,0:T(8,128)(2,1)S(1)} %pad_maximum_fusion), channel_id=1, source_target_pairs={{0,16},{1,3},{2,18},{3,1},{4,20},{5,7},{6,22},{7,5},{8,24},{9,11},... | collective-permute-start | bytes 4423688 | tf_op jit(solution)/shard_map/ppermute | solution.py:38
  267.1 8.9 %collective-permute-start.12 = (bf16[4,48,1280]{2,1,0:T(8,128)(2,1)S(1)}, bf16[4,48,1280]{2,1,0:T(8,128)(2,1)S(1)}, u32[]{:S(2)}, u32[]{:S(2)}) collective-permute-start(bf16[4,48,1280]{2,1,0:T(8,128)(2,1)S(1)} %pad_maximum_fusion.4), channel_id=1, source_target_pairs={{0,4},{1,17},{2,6},{3,19},{4,0},{5,21},{6,2},{7,23},{8,12},{9,25},... | collective-permute-start | bytes 1474568 | tf_op jit(solution)/shard_map/ppermute | solution.py:38
  277.1 9.2 %copy-start.9 = (bf16[1024,768]{1,0:T(8,128)(2,1)S(1)}, bf16[1024,768]{1,0:T(8,128)(2,1)}, u32[]{:S(2)}) copy-start(bf16[1024,768]{1,0:T(8,128)(2,1)} %get-tuple-element.83) | copy-start | bytes 4718596
  277.1 19.4 %collective-permute-start.13 = (bf16[8,48,1280]{2,1,0:T(8,128)(2,1)}, bf16[8,48,1280]{2,1,0:T(8,128)(2,1)}, u32[]{:S(2)}, u32[]{:S(2)}) collective-permute-start(bf16[8,48,1280]{2,1,0:T(8,128)(2,1)} %pad_maximum_fusion.1), channel_id=1, source_target_pairs={{0,16},{1,3},{2,18},{3,1},{4,20},{5,7},{6,22},{7,5},{8,24},{9,11},... | collective-permute-start | bytes 2949128 | tf_op jit(solution)/shard_map/ppermute | solution.py:38
  286.3 175.6 %collective-permute-start.24 = (bf16[16,48,1920]{2,1,0:T(8,128)(2,1)}, bf16[16,48,1920]{2,1,0:T(8,128)(2,1)S(1)}, u32[]{:S(2)}, u32[]{:S(2)}) collective-permute-start(bf16[16,48,1920]{2,1,0:T(8,128)(2,1)} %constant_dynamic-update-slice_fusion.5.mine_ref), channel_id=1, source_target_pairs={{0,1},{1,0},{2,3},{3,2},{4,5},{5,4},{6,7},{7,6},{8,9},{9,8},{10,11... | collective-permute-start | bytes 8847368 | tf_op jit(solution)/shard_map/ppermute | solution.py:42
  298.7 146.8 %collective-permute-start.14 = (bf16[16,48,1280]{2,1,0:T(8,128)(2,1)}, bf16[16,48,1280]{2,1,0:T(8,128)(2,1)}, u32[]{:S(2)}, u32[]{:S(2)}) collective-permute-start(bf16[16,48,1280]{2,1,0:T(8,128)(2,1)} %constant_dynamic-update-slice_fusion.mine_ref), channel_id=1, source_target_pairs={{0,1},{1,0},{2,3},{3,2},{4,5},{5,4},{6,7},{7,6},{8,9},{9,8},{10,11... | collective-permute-start | bytes 5898248 | tf_op jit(solution)/shard_map/ppermute | solution.py:42
  (6 other events, 26.9 us)
Sparse Core Ops, SparseCore 0:
  293.4 145.2 all-reduce.1

commit v3 on v2

--- a/solution.py
+++ b/solution.py
@@ -67,62 +67,45 @@
     return core, jnp.where(core == 0, rows, rows[::-1])
 
 
-def grad_blocks(lhs, rhs, core, table, extra=None, smalls=()):
-    count, rows = lhs.shape
-    half = rhs.shape[1] // 2
-    half_extra = extra[1].shape[1] // 2 if extra else 0
-    tile = half // 3
+def grad_half(turned, rhs, half, table, kind, extra=None, smalls=()):
+    rows, count = turned.shape
+    width = rhs.shape[1] // 2
+    tile = 384
+    steps = width // tile
+    more = extra[1].shape[1] // (2 * tile) if extra else 0
     block = rows // 16
-    total = half + half_extra + (128 if smalls else 0)
+    total = (steps + more) * tile + (128 if smalls else 0)
     per_block = -(-sum(entry.shape[1] for entry, _ in smalls) // (32 * 128))
-    meta = jnp.concatenate([core[None], table.reshape(32)])
-
-    def body(meta_ref, lhs_ref, rhs_ref, *refs):
-        refs = list(refs)
-        turned_ref = refs.pop()
-        kept_ref = refs.pop()
-        sent_ref = refs.pop()
+    meta = jnp.concatenate([half[None], table])
+
+    def body(meta_ref, turned_ref, rhs_ref, *refs):
+        out_ref = refs[-1]
         step = pl.program_id(0)
-        on_zero = meta_ref[0] == 0
-
-        @pl.when(step == 0)
-        def _():
-            turned_ref[...] = lhs_ref[...].T
-
-        part = dot(turned_ref[...], rhs_ref[...])
-
-        @pl.when(step < 3)
-        def _():
-            at = pl.multiple_of(step * tile, 128)
+
+        def store(part, at):
             for number in range(16):
-                sent_ref[meta_ref[17 + number], :, pl.ds(at, tile)] = part[
-                    number * block : (number + 1) * block
-                ].astype(bf16)
-
-        @pl.when(step >= 3)
-        def _():
-            at = pl.multiple_of((step - 3) * tile, 128)
-            for number in range(16):
-                kept_ref[meta_ref[1 + number], :, pl.ds(at, tile)] = part[
-                    number * block : (number + 1) * block
-                ]
-
-        @pl.when(step == 5)
-        def _():
-            at = half
-            if extra:
-                more = dot(refs[0][...], refs[1][...], 0, 0)
-                left, right = more[:, :half_extra], more[:, half_extra:]
-                kept = jnp.where(on_zero, left, right)
-                sent = jnp.where(on_zero, right, left).astype(bf16)
-                for number in range(16):
-                    lines = slice(number * block, (number + 1) * block)
-                    sent_ref[meta_ref[17 + number], :, at : at + half_extra] = sent[lines]
-                    kept_ref[meta_ref[1 + number], :, at : at + half_extra] = kept[lines]
-                at += half_extra
-            if smalls:
+                lines = slice(number * block, (number + 1) * block)
+                out_ref[meta_ref[1 + number], :, at] = part[lines].astype(kind)
+
+        def main():
+            at = pl.ds(pl.multiple_of(step * tile, 128), tile) if smalls else slice(None)
+            store(dot(turned_ref[...], rhs_ref[...]), at)
+
+        if more:
+            pl.when(step < steps)(main)
+
+            @pl.when(step >= steps)
+            def _():
+                store(dot(refs[0][...], refs[1][...]), slice(None))
+
+        else:
+            main()
+        if smalls:
+
+            @pl.when(step == steps - 1)
+            def _():
                 lines = []
-                for (entry, row), ref in zip(smalls, refs[2 if extra else 0 :]):
+                for (entry, row), ref in zip(smalls, refs):
                     for start in range(0, entry.shape[1], 128):
                         lines.append(ref[row : row + 1, start : start + 128])
                 lines += [jnp.zeros((1, 128), f32)] * (32 * per_block - len(lines))
@@ -130,45 +113,52 @@
                 for number in range(16):
                     first = number * per_block
                     second = (16 + number) * per_block
-                    left = jnp.concatenate(lines[first : first + per_block] + [fill], 0)
-                    right = jnp.concatenate(lines[second : second + per_block] + [fill], 0)
-                    sent_ref[meta_ref[17 + number], :, at:] = jnp.where(
-                        on_zero, right, left
-                    ).astype(bf16)
-                    kept_ref[meta_ref[1 + number], :, at:] = jnp.where(on_zero, left, right)
-
-    def column(step, meta_ref):
-        side = jnp.where(step < 3, 1 - meta_ref[0], meta_ref[0])
-        return (0, side * 3 + lax.rem(step, 3))
-
-    operands = [lhs, rhs] + list(extra or ()) + [entry for entry, _ in smalls]
+                    left = jnp.concatenate(lines[first : first + per_block], 0)
+                    right = jnp.concatenate(lines[second : second + per_block], 0)
+                    own = jnp.where(meta_ref[0] == 0, left, right)
+                    out_ref[meta_ref[1 + number], :, total - 128 :] = jnp.concatenate(
+                        [own, fill], 0
+                    ).astype(kind)
+
+    def whole(array):
+        return pl.BlockSpec(
+            array.shape, lambda step, meta_ref: (0, 0), pipeline_mode=pl.Buffered(1)
+        )
+
     in_specs = [
-        pl.BlockSpec(lhs.shape, lambda step, meta_ref: (0, 0), pipeline_mode=pl.Buffered(1)),
-        pl.BlockSpec((count, tile), column),
-    ] + [
-        pl.BlockSpec(entry.shape, lambda step, meta_ref: (0, 0), pipeline_mode=pl.Buffered(1))
-        for entry in operands[2:]
+        whole(turned),
+        pl.BlockSpec(
+            (count, tile),
+            lambda step, meta_ref: (0, meta_ref[0] * steps + jnp.minimum(step, steps - 1)),
+        ),
     ]
+    operands = [turned, rhs]
+    if extra:
+        in_specs += [
+            whole(extra[0]),
+            pl.BlockSpec(
+                (count, tile),
+                lambda step, meta_ref: (0, meta_ref[0] * more + jnp.maximum(step - steps, 0)),
+            ),
+        ]
+        operands += list(extra)
+    in_specs += [whole(entry) for entry, _ in smalls]
+    operands += [entry for entry, _ in smalls]
     return pl.pallas_call(
         body,
-        out_shape=[
-            jax.ShapeDtypeStruct((16, block, total), bf16),
-            jax.ShapeDtypeStruct((16, block, total), f32),
-        ],
+        out_shape=jax.ShapeDtypeStruct((16, block, total), kind),
         grid_spec=pltpu.PrefetchScalarGridSpec(
             num_scalar_prefetch=1,
-            grid=(6,),
+            grid=(steps + more,),
             in_specs=in_specs,
-            out_specs=[
-                pl.BlockSpec((16, block, total), lambda step, meta_ref: (0, 0, 0))
-                for _ in range(2)
-            ],
-            scratch_shapes=[pltpu.VMEM((rows, count), bf16)],
+            out_specs=pl.BlockSpec((16, block, total), lambda step, meta_ref: (0, 0, 0))
+            if smalls
+            else pl.BlockSpec((16, block, tile), lambda step, meta_ref: (0, 0, step)),
         ),
         compiler_params=call_params(),
         cost_estimate=pl.CostEstimate(
-            flops=4 * count * rows * (half + half_extra),
-            bytes_accessed=2 * count * (rows + 2 * half) + 6 * rows * total,
+            flops=2 * count * rows * total,
+            bytes_accessed=2 * count * (rows + total) + 3 * rows * total,
             transcendentals=0,
         ),
     )(meta, *operands)
@@ -207,9 +197,8 @@
                         group, line = divmod(index, per_block)
                         ref, at = (first_ref, first_at) if group < 16 else (second_ref, second_at)
                         spot = meta_ref[at + group % 16]
-                        out_ref[:, start_at : start_at + 128] = ref[
-                            spot, line : line + 1, sum(widths) :
-                        ].astype(f32)
+                        values = ref[spot, line : line + 1, sum(widths) :].astype(f32)
+                        out_ref[start_at : start_at + 128] = values.reshape(128)
                         index += 1
 
         @pl.when(meta_ref[0] == 0)
@@ -227,8 +216,8 @@
         for width in widths
     ]
     for width in small_widths:
-        out_shape.append(jax.ShapeDtypeStruct((1, width), f32))
-        out_specs.append(pl.BlockSpec((1, width), lambda step, meta_ref: (0, 0)))
+        out_shape.append(jax.ShapeDtypeStruct((width,), f32))
+        out_specs.append(pl.BlockSpec((width,), lambda step, meta_ref: (0,)))
     return pl.pallas_call(
         body,
         out_shape=out_shape,
@@ -242,28 +231,98 @@
     )(meta, mine, theirs)
 
 
-def sum_over_all(sent, kept, dp_size):
-    terms = [kept, swap_core(sent, dp_size)]
-
-    def piece(start, stop):
-        return sum(term[start:stop].astype(f32) for term in terms)
-
-    size = 16
-    for hop in range(4):
-        size //= 2
-        part = piece(size, 2 * size).astype(bf16)
-        terms.append(swap_hop(part, dp_size, (HOPS[0][hop], HOPS[1][hop])))
-    own = piece(0, 1)
-    bits = 16
-    while bits < dp_size:
-        own = own + swap_place(own.astype(bf16), dp_size, bits).astype(f32)
-        bits *= 2
-    whole = own.astype(bf16)
-    for hop in (3, 2, 1, 0):
-        whole = jnp.concatenate(
-            [whole, swap_hop(whole, dp_size, (HOPS[0][hop], HOPS[1][hop]))], 0
-        )
-    return whole, swap_core(whole, dp_size)
+def finish_turned(mine, theirs, core, table):
+    block, half = mine.shape[1:]
+    tile = 384
+    steps = half // tile
+    meta = jnp.concatenate([core[None], table.reshape(32)])
+
+    def body(meta_ref, mine_ref, theirs_ref, out_ref):
+        own = (pl.program_id(0) // steps) == meta_ref[0]
+
+        def fill(ref, first):
+            parts = [ref[meta_ref[first + number]] for number in range(16)]
+            out_ref[...] = jnp.concatenate(parts, 0).T.astype(f32)
+
+        @pl.when(own)
+        def _():
+            fill(mine_ref, 1)
+
+        @pl.when(jnp.logical_not(own))
+        def _():
+            fill(theirs_ref, 17)
+
+    piece = pl.BlockSpec((16, block, tile), lambda step, meta_ref: (0, 0, lax.rem(step, steps)))
+    return pl.pallas_call(
+        body,
+        out_shape=jax.ShapeDtypeStruct((2 * half, 16 * block), f32),
+        grid_spec=pltpu.PrefetchScalarGridSpec(
+            num_scalar_prefetch=1,
+            grid=(2 * steps,),
+            in_specs=[piece, piece],
+            out_specs=pl.BlockSpec((tile, 16 * block), lambda step, meta_ref: (step, 0)),
+        ),
+        compiler_params=call_params(),
+        cost_estimate=pl.CostEstimate(
+            flops=0, bytes_accessed=12 * mine.size, transcendentals=0
+        ),
+    )(meta, mine, theirs)
+
+
+class Sum:
+    def __init__(self, sent, dp_size):
+        self.dp_size = dp_size
+        self.piece = sent
+        self.stage = 0
+        self.terms = []
+        self.whole = None
+        self.result = None
+
+    def send(self, piece):
+        if self.stage in (0, 9):
+            return swap_core(piece, self.dp_size)
+        hop = self.stage - 1 if self.stage < 5 else 8 - self.stage
+        return swap_hop(piece, self.dp_size, (HOPS[0][hop], HOPS[1][hop]))
+
+    def take(self, received):
+        def part(start, stop):
+            return sum(term[start:stop].astype(f32) for term in self.terms)
+
+        if self.stage < 5:
+            self.terms.append(received)
+        if self.stage < 4:
+            size = 8 >> self.stage
+            self.piece = part(size, 2 * size).astype(bf16)
+        elif self.stage == 4:
+            own = part(0, 1)
+            bits = 16
+            while bits < self.dp_size:
+                own = own + swap_place(own.astype(bf16), self.dp_size, bits).astype(f32)
+                bits *= 2
+            self.piece = own.astype(bf16)
+        elif self.stage < 9:
+            self.piece = jnp.concatenate([self.piece, received], 0)
+        else:
+            self.result = (self.piece, received)
+        self.stage += 1
+
+    def run(self):
+        while self.result is None:
+            self.take(self.send(self.piece))
+        return self.result
+
+
+def beside(work, entry, *sums, keeps=None):
+    entry, pieces = lax.optimization_barrier((entry, [each.piece for each in sums]))
+    for each, piece in zip(sums, pieces):
+        each.piece = piece
+    received = [each.send(each.piece) for each in sums]
+    result, received = lax.optimization_barrier((work(entry), received))
+    if keeps:
+        keeps.terms.append(result)
+    for each, value in zip(sums, received):
+        each.take(value)
+    return result
 
 
 def gather_pooled(pooled_low, dp_size):
@@ -342,8 +401,16 @@
     return up * below, below + (up * bell) * (1.0 / math.sqrt(2.0 * math.pi))
 
 
+def line(ref, part=slice(None)):
+    return ref[part].reshape(1, -1)
+
+
 def row_spec(shape):
     return pl.BlockSpec(shape, lambda step: (step,) + (0,) * (len(shape) - 1))
+
+
+def column_spec(shape):
+    return pl.BlockSpec(shape, lambda step: (0, step))
 
 
 def full_spec(array):
@@ -377,11 +444,12 @@
     scale = 1.0 / math.sqrt(head_dim)
 
     def body(tok_ref, seg_ref, wqkv_ref, bq_ref, bv_ref, wout_ref, bout_ref, *outs):
-        qkv_ref, ctx_ref, sum_ref = outs
+        qkv_ref, turned_ref, tok_turned_ref, sum_ref, ctx_ref = outs
         tok = tok_ref[...]
-        qkv_ref[:, :width] = (dot(tok, wqkv_ref[:, :width]) + bq_ref[...]).astype(bf16)
+        tok_turned_ref[...] = tok.T
+        qkv_ref[:, :width] = (dot(tok, wqkv_ref[:, :width]) + line(bq_ref)).astype(bf16)
         qkv_ref[:, width : 2 * width] = dot(tok, wqkv_ref[:, width : 2 * width]).astype(bf16)
-        qkv_ref[:, 2 * width :] = (dot(tok, wqkv_ref[:, 2 * width :]) + bv_ref[...]).astype(bf16)
+        qkv_ref[:, 2 * width :] = (dot(tok, wqkv_ref[:, 2 * width :]) + line(bv_ref)).astype(bf16)
         first = lax.broadcasted_iota(jnp.int32, (length, 2 * head_dim), 1) < head_dim
         zero = jnp.zeros((length, 2 * head_dim), bf16)
         for row in range(rows):
@@ -404,14 +472,17 @@
                     [jnp.where(first, value, zero), jnp.where(first, zero, value)], 0
                 )
                 ctx_ref[lines, at : at + 2 * head_dim] = dot(attn, values).astype(bf16)
-        sum_ref[...] = tok.astype(f32) + (dot(ctx_ref[...], wout_ref[...]) + bout_ref[...])
-
-    operands = [w_qkv, b_query[None], b_value[None], w_out, b_out[None]]
+        context = ctx_ref[...]
+        turned_ref[...] = context.T
+        sum_ref[...] = tok.astype(f32) + (dot(context, wout_ref[...]) + line(bout_ref))
+
+    operands = [w_qkv, b_query, b_value, w_out, b_out]
     return pl.pallas_call(
         body,
         out_shape=[
             jax.ShapeDtypeStruct((count, 3 * width), bf16),
-            jax.ShapeDtypeStruct((count, width), bf16),
+            jax.ShapeDtypeStruct((width, count), bf16),
+            jax.ShapeDtypeStruct((width, count), bf16),
             jax.ShapeDtypeStruct((count, width), f32),
         ],
         grid=(rows_all // rows,),
@@ -419,9 +490,11 @@
         + [full_spec(entry) for entry in operands],
         out_specs=[
             row_spec((tile, 3 * width)),
+            column_spec((width, tile)),
+            column_spec((width, tile)),
             row_spec((tile, width)),
-            row_spec((tile, width)),
-        ],
+        ],
+        scratch_shapes=[pltpu.VMEM((tile, width), bf16)],
         compiler_params=call_params(),
         cost_estimate=pl.CostEstimate(
             flops=2 * count * width * (4 * width + 2 * length),
@@ -442,20 +515,20 @@
     def body(x_ref, seg_ref, g1_ref, s1_ref, win_ref, bin_ref, wdown_ref, bdown_ref, g2_ref, s2_ref, *outs):
         low_ref, act_ref, slope_ref, sum_ref, out_ref, pool_ref = outs
         normed, _ = norm_parts(x_ref[...])
-        hidden = normed * g1_ref[...] + s1_ref[...]
+        hidden = normed * line(g1_ref) + line(s1_ref)
         low = hidden.astype(bf16)
-        low_ref[...] = low
-        total = hidden + bdown_ref[...]
+        low_ref[...] = low.T
+        total = hidden + line(bdown_ref)
         for start in range(0, ff_width, chunk):
             part = slice(start, start + chunk)
-            value, slope = gelu_pair(dot(low, win_ref[:, part]) + bin_ref[:, part])
+            value, slope = gelu_pair(dot(low, win_ref[:, part]) + line(bin_ref, part))
             act = value.astype(bf16)
             act_ref[:, part] = act
             slope_ref[:, part] = slope.astype(bf16)
             total = total + dot(act, wdown_ref[part, :])
         sum_ref[...] = total
         normed, _ = norm_parts(total)
-        result = normed * g2_ref[...] + s2_ref[...]
+        result = normed * line(g2_ref) + line(s2_ref)
         out_ref[...] = result.astype(bf16)
         onehot = sentence_onehot([seg_ref[row] for row in range(rows)], rows)
         pool_ref[...] = (
@@ -463,19 +536,19 @@
         ).astype(bf16)
 
     operands = [
-        gain_one[None],
-        shift_one[None],
+        gain_one,
+        shift_one,
         w_in,
-        b_in[None],
+        b_in,
         w_down,
-        b_down[None],
-        gain_two[None],
-        shift_two[None],
+        b_down,
+        gain_two,
+        shift_two,
     ]
     return pl.pallas_call(
         body,
         out_shape=[
-            jax.ShapeDtypeStruct((count, width), bf16),
+            jax.ShapeDtypeStruct((width, count), bf16),
             jax.ShapeDtypeStruct((count, ff_width), bf16),
             jax.ShapeDtypeStruct((count, ff_width), bf16),
             jax.ShapeDtypeStruct((count, width), f32),
@@ -486,7 +559,7 @@
         in_specs=[row_spec((tile, width)), row_spec((rows, 1, length))]
         + [full_spec(entry) for entry in operands],
         out_specs=[
-            row_spec((tile, width)),
+            column_spec((width, tile)),
             row_spec((tile, ff_width)),
             row_spec((tile, ff_width)),
             row_spec((tile, width)),
@@ -578,9 +651,9 @@
         per_token = d_pooled / jnp.sum(onehot, -1, keepdims=True)
         d_output = exact_dot(onehot, per_token, 0, 0)
         normed, inv_std = norm_parts(x_ref[...])
-        d_mid = norm_back(d_output, normed, inv_std, g2_ref[...])
+        d_mid = norm_back(d_output, normed, inv_std, line(g2_ref))
         mid_ref[...] = d_mid
-        low_ref[...] = d_mid.astype(bf16)
+        low_ref[...] = d_mid.astype(bf16).T
         grads_ref[0:1] += jnp.sum(d_output * normed, 0, keepdims=True)
         grads_ref[1:2] += jnp.sum(d_output, 0, keepdims=True)
         grads_ref[2:3] += jnp.sum(d_mid, 0, keepdims=True)
@@ -589,7 +662,7 @@
         body,
         out_shape=[
             jax.ShapeDtypeStruct((count, width), f32),
-            jax.ShapeDtypeStruct((count, width), bf16),
+            jax.ShapeDtypeStruct((width, count), bf16),
             jax.ShapeDtypeStruct((8, width), f32),
         ],
         grid=(groups,),
@@ -602,11 +675,11 @@
             row_spec((sentences, width)),
             row_spec((rows, 1, length)),
             row_spec((tile, width)),
-            full_spec(gain_two[None]),
+            full_spec(gain_two),
         ],
         out_specs=[
             row_spec((tile, width)),
-            row_spec((tile, width)),
+            column_spec((width, tile)),
             pl.BlockSpec((8, width), lambda step: (0, 0)),
         ],
         scratch_shapes=[
@@ -617,7 +690,7 @@
         cost_estimate=pl.CostEstimate(
             flops=100 * count * width, bytes_accessed=10 * count * width, transcendentals=count
         ),
-    )(meta, pairs, scores, mine, theirs, pooled_low, seg_rows, second_sum, gain_two[None])
+    )(meta, pairs, scores, mine, theirs, pooled_low, seg_rows, second_sum, gain_two)
 
 
 def backward_kernel(d_mid, slope, first_sum, gain_one, w_in, w_down, w_out):
@@ -644,7 +717,7 @@
             up_ref[:, part] = up_low
             d_hidden = d_hidden + dot(up_low, win_ref[:, part], 1, 1)
         normed, inv_std = norm_parts(x_ref[...])
-        d_first = norm_back(d_hidden, normed, inv_std, g1_ref[...])
+        d_first = norm_back(d_hidden, normed, inv_std, line(g1_ref))
         first_ref[...] = d_first
         first_low = d_first.astype(bf16)
         low_ref[...] = first_low
@@ -653,7 +726,7 @@
         grads_ref[1:2] += jnp.sum(d_hidden * normed, 0, keepdims=True)
         grads_ref[2:3] += jnp.sum(d_hidden, 0, keepdims=True)
 
-    operands = [gain_one[None], w_in, w_down, w_out]
+    operands = [gain_one, w_in, w_down, w_out]
     return pl.pallas_call(
         body,
         out_shape=[
@@ -684,7 +757,7 @@
     )(d_mid, slope, first_sum, *operands)
 
 
-def attention_back_kernel(qkv, d_context, seg_rows):
+def attention_back_kernel(qkv, d_context, seg_rows, part, parts, before=None):
     count, width = d_context.shape
     rows_all, length = seg_rows.shape[0], seg_rows.shape[2]
     rows = math.gcd(2, rows_all)
@@ -692,10 +765,15 @@
     head_dim = width // HEADS
     scale = 1.0 / math.sqrt(head_dim)
 
-    def body(qkv_ref, dctx_ref, seg_ref, joint_ref, grads_ref):
+    steps = rows_all // (rows * parts)
+    base = part * steps
+
+    def body(qkv_ref, dctx_ref, seg_ref, *rest):
+        joint_ref, grads_ref = rest[-2:]
+
         @pl.when(pl.program_id(0) == 0)
         def _():
-            grads_ref[...] = jnp.zeros_like(grads_ref)
+            grads_ref[...] = rest[1][...] if before else jnp.zeros_like(grads_ref)
 
         first = lax.broadcasted_iota(jnp.int32, (length, 2 * head_dim), 1) < head_dim
         zero = jnp.zeros((length, 2 * head_dim), bf16)
@@ -740,20 +818,25 @@
             jax.ShapeDtypeStruct((count, 3 * width), bf16),
             jax.ShapeDtypeStruct((8, width), f32),
         ],
-        grid=(rows_all // rows,),
+        grid=(steps,),
         in_specs=[
-            row_spec((tile, 3 * width)),
-            row_spec((tile, width)),
-            row_spec((rows, 1, length)),
-        ],
-        out_specs=[row_spec((tile, 3 * width)), pl.BlockSpec((8, width), lambda step: (0, 0))],
+            pl.BlockSpec((tile, 3 * width), lambda step: (base + step, 0)),
+            pl.BlockSpec((tile, width), lambda step: (base + step, 0)),
+            pl.BlockSpec((rows, 1, length), lambda step: (base + step, 0, 0)),
+        ]
+        + ([pl.BlockSpec(memory_space=pl.ANY), full_spec(before[1])] if before else []),
+        out_specs=[
+            pl.BlockSpec((tile, 3 * width), lambda step: (base + step, 0)),
+            pl.BlockSpec((8, width), lambda step: (0, 0)),
+        ],
+        input_output_aliases={3: 0} if before else {},
         compiler_params=call_params(),
         cost_estimate=pl.CostEstimate(
-            flops=14 * count * width * length,
-            bytes_accessed=14 * count * width,
-            transcendentals=count * HEADS * length,
-        ),
-    )(qkv, d_context, seg_rows)
+            flops=14 * count * width * length // parts,
+            bytes_accessed=14 * count * width // parts,
+            transcendentals=count * HEADS * length // parts,
+        ),
+    )(qkv, d_context, seg_rows, *(before or ()))
 
 
 def on_device(
@@ -782,14 +865,14 @@
     seg_rows = segments[0][:, None, :]
     width = flat_rows.shape[1]
     ff_width = w_in.shape[1]
-    qkv, context, first_sum = attention_kernel(
+    qkv, context_turned, tokens_turned, first_sum = attention_kernel(
         flat_rows, seg_rows, w_qkv, b_query, b_value, w_out, b_out
     )
-    hidden_low, act, slope, second_sum, output_rows, pooled_low = forward_kernel(
+    hidden_turned, act, slope, second_sum, output_rows, pooled_low = forward_kernel(
         first_sum, seg_rows, gain_one, shift_one, w_in, b_in, w_down, b_down, gain_two, shift_two
     )
     mine, theirs, spans = gather_pooled(pooled_low, dp_size)
-    d_mid, d_mid_low, grads_two = loss_kernel(
+    d_mid, d_mid_turned, grads_two = loss_kernel(
         place,
         pairs.reshape(-1, 128),
         scores.reshape(-1, 128),
@@ -801,41 +884,70 @@
         gain_two,
         spans,
     )
-    grad_w_down = jnp.einsum("nf,nd->fd", act, d_mid_low, preferred_element_type=f32)
-    grad_w_down = lax.psum(grad_w_down.astype(bf16), AXES)
-    d_up_low, d_first, d_first_low, d_context, grads_wide, grads_one = backward_kernel(
-        d_mid, slope, first_sum, gain_one, w_in, w_down, w_out
-    )
-    in_sum = sum_over_all(
-        *grad_blocks(hidden_low, d_up_low, core, table, (context, d_first_low)), dp_size
-    )
-    d_joint, grads_attn = attention_back_kernel(qkv, d_context, seg_rows)
-    qkv_sum = sum_over_all(
-        *grad_blocks(
-            flat_rows,
-            d_joint,
-            core,
-            table,
-            None,
-            [
-                (grads_attn, 0),
-                (grads_attn, 1),
-                (grads_one, 0),
-                (grads_one, 1),
-                (grads_one, 2),
-                (grads_wide, 0),
-                (grads_two, 2),
-                (grads_two, 0),
-                (grads_two, 1),
-            ],
-        ),
-        dp_size,
-    )
-    grad_tokens = d_first + jnp.einsum("ne,de->nd", d_joint, w_qkv, preferred_element_type=f32)
-    grad_w_in, grad_w_out = finish(*in_sum, core, table, [ff_width // 2, width // 2])
+
+    def own_half(rhs, turned, *more):
+        return grad_half(turned, rhs, core, table[0], f32, *more)
+
+    def other_half(rhs, turned, *more):
+        return grad_half(turned, rhs, 1 - core, table[1], bf16, *more)
+
+    down = Sum(other_half(act, d_mid_turned), dp_size)
+    beside(lambda entry: own_half(act, entry), d_mid_turned, down, keeps=down)
+    d_up_low, d_first, d_first_low, d_context, grads_wide, grads_one = beside(
+        lambda entry: backward_kernel(entry, slope, first_sum, gain_one, w_in, w_down, w_out),
+        d_mid,
+        down,
+    )
+    out_pair = (context_turned, d_first_low)
+    sent = beside(lambda entry: other_half(entry, hidden_turned, out_pair), d_up_low, down)
+    feed = Sum(sent, dp_size)
+    beside(
+        lambda entry: own_half(entry, hidden_turned, out_pair), d_up_low, down, feed, keeps=feed
+    )
+    half_joint = beside(
+        lambda entry: attention_back_kernel(qkv, entry, seg_rows, 0, 2), d_context, down, feed
+    )
+    d_joint, grads_attn = beside(
+        lambda entry: attention_back_kernel(qkv, d_context, seg_rows, 1, 2, entry),
+        half_joint,
+        down,
+        feed,
+    )
+    smalls = [
+        (grads_attn, 0),
+        (grads_attn, 1),
+        (grads_one, 0),
+        (grads_one, 1),
+        (grads_one, 2),
+        (grads_wide, 0),
+        (grads_two, 2),
+        (grads_two, 0),
+        (grads_two, 1),
+    ]
+    sent = beside(
+        lambda entry: other_half(entry, tokens_turned, None, smalls), d_joint, down, feed
+    )
+    joint = Sum(sent, dp_size)
+    beside(
+        lambda entry: own_half(entry, tokens_turned, None, smalls),
+        d_joint,
+        down,
+        feed,
+        joint,
+        keeps=joint,
+    )
+    grad_tokens = beside(
+        lambda entry: d_first
+        + jnp.einsum("ne,de->nd", entry, w_qkv, preferred_element_type=f32),
+        d_joint,
+        down,
+        feed,
+        joint,
+    )
+    grad_w_down = finish_turned(*down.run(), core, table)
+    grad_w_in, grad_w_out = finish(*feed.run(), core, table, [ff_width // 2, width // 2])
     small_widths = [width] * 5 + [ff_width] + [width] * 3
-    grad_w_qkv, *smalls = finish(*qkv_sum, core, table, [3 * width // 2], small_widths)
-    smalls = [entry.reshape(-1) for entry in smalls]
+    grad_w_qkv, *smalls = finish(*joint.run(), core, table, [3 * width // 2], small_widths)
     return (
         output_rows[None],
         grad_tokens[None],
@@ -848,7 +960,7 @@
         smalls[4],
         grad_w_in,
         smalls[5],
-        grad_w_down.astype(f32),
+        grad_w_down,
         smalls[6],
         smalls[7],
         smalls[8],

time: 479 us -> 372 us (0.78)
  waiting for transfers between devices: 210 us -> 108 us
  Pallas kernels: 143 us -> 178 us
  between operations: 14.3 us -> 1.01 us
  local copies, waits for them, and re-layouts: 22.5 us -> 10.5 us
  matrix products: 13.5 us -> 3.85 us
  starting transfers between devices: 41.4 us -> 34 us
    psum x1 -> x0, waiting for transfers between devices: 131 us -> none  [on_device(): grad_w_down = lax.psum(grad_w_down.astype(bf16), AXES)]
    pallas_call x3 -> x8, Pallas kernels: 55.8 us -> 87.6 us  [the longest x6 49.1 us: grad_half(): pl.pallas_call(body, out_shape=jax.ShapeDtypeStruct((16, block, total), k...]
    ppermute x19 -> x27, waiting for transfers between devices: 76.2 us -> 105 us  [swap_hop(): return lax.ppermute(value, AXES, pairs)]
    convert_element_type x9 -> x14, other arithmetic: 15.4 us -> 25.8 us  [the longest x12 22.6 us: take(): self.piece = part(size, 2 * size).astype(bf16)]
    pallas_call x8 -> x0, other arithmetic: 10.3 us -> none  [finish(): pl.pallas_call(body, out_shape=out_shape, grid_spec=pltpu.PrefetchScalarG...]
    broadcast_in_dim x8 -> x0, local copies, waits for them, and re-layouts: 10.1 us -> none  [the longest x3 3.8 us: attention_kernel(): operands = [w_qkv, b_query[None], b_value[None], w_out, b_out[None]]]
    dot_general x2 -> x1, matrix products: 13.5 us -> 3.85 us  [on_device(): jnp.einsum('ne,de->nd', entry, w_qkv, preferred_element_type=f32)]
    ppermute x19 -> x27, starting transfers between devices: 37.5 us -> 29.5 us  [swap_hop(): return lax.ppermute(value, AXES, pairs)]
  transfers between devices with their start and end apart: 26 -> 35, of which waited for: 17 -> 20; matrix products, arithmetic and copies ran while one was open for 11% -> 5% of each run, Pallas kernels for 9% -> 30%
where the time goes in v3:
time: 372 us; the launch traced here: 370 us
  Pallas kernels  178 us (48%)
  waiting for transfers between devices  108 us (29%)
  other arithmetic  34.9 us (9%)
  starting transfers between devices  34 us (9%)
  local copies, waits for them, and re-layouts  10.5 us (3%)
  matrix products  3.85 us (1%)
    ppermute x27, waiting for transfers between devices, swap_hop(): return lax.ppermute(value, AXES, pairs)  105 us
    pallas_call x6, Pallas kernels, grad_half(): pl.pallas_call(body, out_shape=jax.ShapeDtypeStruct((16, block, total), k...  49.1 us
    ppermute x27, starting transfers between devices, swap_hop(): return lax.ppermute(value, AXES, pairs)  29.5 us
    pallas_call x2, Pallas kernels, attention_back_kernel(): pl.pallas_call(body, out_shape=[jax.ShapeDtypeStruct((count, 3 * width),...  28.6 us
    pallas_call x1, Pallas kernels, forward_kernel(): pl.pallas_call(body, out_shape=[jax.ShapeDtypeStruct((width, count), bf16...  27.8 us
    convert_element_type x12, other arithmetic, take(): self.piece = part(size, 2 * size).astype(bf16)  22.6 us
    pallas_call x1, Pallas kernels, backward_kernel(): pl.pallas_call(body, out_shape=[jax.ShapeDtypeStruct((count, ff_width), b...  22.5 us
    pallas_call x1, Pallas kernels, attention_kernel(): pl.pallas_call(body, out_shape=[jax.ShapeDtypeStruct((count, 3 * width),...  15.7 us
  transfers between devices with their start and end apart: 35, of which 20 were waited for; matrix products, arithmetic and copies ran while one was open for 5% of the time, Pallas kernels for 30%

profile of v3, /device:TPU:0, one launch (start us, length us, event | category | flops | bytes accessed | tf_op | source)
XLA Modules:
  0.0 370.1 jit_solution(7198845584757965930)
XLA Ops:
  0.6 15.7 %shard_map.289 = (bf16[1024,2304]{1,0:T(8,128)(2,1)}, bf16[768,1024]{1,0:T(8,128)(2,1)}, bf16[768,1024]{1,0:T(8,128)(2,1)}, f32[1024,768]{1,0:T(8,128)}) custom-call(bf16[1024,768]{1,0:T(8,128)(2,1)} %bitcast.34, s32[8,1,128]{2,1,0:T(1,128)} %bitcast.27, bf16[768,2304]{1,0:T(8,128)(2,1)} %wqkv_ref.1, f32[768]{0:T(1024)} %bq_ref.1, f32[768]{0:T(1024)} %bv_ref.1, ...), custom_call_target="tpu_custom_call" | custom-call | flops 5234491392 | bytes 12582912 | tf_op jit(solution)/shard_map/pallas_call | solution.py:480
  16.4 27.8 %shard_map.290 = (bf16[768,1024]{1,0:T(8,128)(2,1)}, bf16[1024,3072]{1,0:T(8,128)(2,1)}, bf16[1024,3072]{1,0:T(8,128)(2,1)}, f32[1024,768]{1,0:T(8,128)}, bf16[1...) custom-call(f32[1024,768]{1,0:T(8,128)} %get-tuple-element.110.x_ref, s32[8,1,128]{2,1,0:T(1,128)} %bitcast.28, f32[768]{0:T(1024)} %g1_ref.3, ...), custom_call_target="tpu_custom_call" | custom-call | flops 9789505536 | bytes 31457280 | tf_op jit(solution)/shard_map/pallas_call | solution.py:548
  57.9 5.8 %collective-permute-done.2 = bf16[2,64,768]{2,1,0:T(8,128)(2,1)S(1)} collective-permute-done((bf16[2,64,768]{2,1,0:T(8,128)(2,1)S(1)}, bf16[2,64,768]{2,1,0:T(8,128)(2,1)S(1)}, u32[]{:S(2)}, u32[]{:S(2)}) %collective-permute-start.2) | collective-permute-done | bytes 196640 | tf_op jit(solution)/shard_map/ppermute | solution.py:38
  64.7 6.8 %collective-permute-done.3 = bf16[4,64,768]{2,1,0:T(8,128)(2,1)S(1)} collective-permute-done((bf16[4,64,768]{2,1,0:T(8,128)(2,1)S(1)}, bf16[4,64,768]{2,1,0:T(8,128)(2,1)S(1)}, u32[]{:S(2)}, u32[]{:S(2)}) %collective-permute-start.3) | collective-permute-done | bytes 393248 | tf_op jit(solution)/shard_map/ppermute | solution.py:38
  74.9 9.1 %shard_map.291 = (f32[1024,768]{1,0:T(8,128)}, bf16[768,1024]{1,0:T(8,128)(2,1)}, f32[8,768]{1,0:T(8,128)}) custom-call(s32[2]{0:T(128)} %pad_add_fusion.meta_ref, s32[8,128]{1,0:T(8,128)} %bitcast.32, f32[8,128]{1,0:T(8,128)} %bitcast.33, bf16[8,64,768]{2,1,0:T(8,128)(2,1)} %copy-done.2, bf16[8,64,768]{2,1,0:T(8,128)(2,1)} %copy-done.5, ...), custom_call_target="tpu_custom_call" | custom-call | flops 78643200 | bytes 7864320 | tf_op jit(solution)/shard_map/pallas_call | solution.py:661
  84.0 7.5 %shard_map.292 = bf16[16,48,1536]{2,1,0:T(8,128)(2,1)} custom-call(s32[17]{0:T(128)} %pad_add_fusion.2.meta_ref, bf16[768,1024]{1,0:T(8,128)(2,1)} %get-tuple-element.117.turned_ref, bf16[1024,3072]{1,0:T(8,128)(2,1)} %get-tuple-element.116.rhs_ref), custom_call_target="tpu_custom_call" | custom-call | flops 2415919104 | bytes 8257536 | tf_op jit(solution)/shard_map/pallas_call | solution.py:147
  92.3 8.0 %shard_map.293 = f32[16,48,1536]{2,1,0:T(8,128)} custom-call(s32[17]{0:T(128)} %pad_add_fusion.1.meta_ref, bf16[768,1024]{1,0:T(8,128)(2,1)} %get-tuple-element.117.turned_ref, bf16[1024,3072]{1,0:T(8,128)(2,1)} %get-tuple-element.116.rhs_ref), custom_call_target="tpu_custom_call" | custom-call | flops 2415919104 | bytes 8257536 | tf_op jit(solution)/shard_map/pallas_call | solution.py:147
  100.3 3.9 %add_convert_fusion.1 = bf16[8,48,1536]{2,1,0:T(8,128)(2,1)} fusion(f32[16,48,1536]{2,1,0:T(8,128)} %shard_map.293, bf16[16,48,1536]{2,1,0:T(8,128)(2,1)S(1)} %collective-permute-done.5), kind=kLoop, calls=%fused_computation.2 | loop fusion | flops 1769472 | bytes 4718592 | tf_op jit(solution)/shard_map/convert_element_type | solution.py:295
  106.0 22.5 %shard_map.294 = (bf16[1024,3072]{1,0:T(8,128)(2,1)}, f32[1024,768]{1,0:T(8,128)}, bf16[1024,768]{1,0:T(8,128)(2,1)}, bf16[1024,768]{1,0:T(8,128)(2,1)}, f32[8,3072]{1,0:T(8,128)}, /*index=5*/f32[8,768]{1,0:T(8,128)}) custom-call(f32[1024,768]{1,0:T(8,128)} %get-tuple-element.121.mid_ref, bf16[1024,3072]{1,0:T(8,128)(2,1)} %get-tuple-element.122.slope_ref, ...), custom_call_target="tpu_custom_call" | custom-call | flops 10871635968 | bytes 34603008 | tf_op jit(solution)/shard_map/pallas_call | solution.py:730
  130.6 9.3 %shard_map.295 = bf16[16,48,1920]{2,1,0:T(8,128)(2,1)} custom-call(s32[17]{0:T(128)} %pad_add_fusion.2.meta_ref, bf16[768,1024]{1,0:T(8,128)(2,1)} %get-tuple-element.134.turned_ref, bf16[1024,3072]{1,0:T(8,128)(2,1)} %get-tuple-element.142.rhs_ref, bf16[768,1024]{1,0:T(8,128)(2,1)} %get-tuple-element.137.refs_0_, bf16[1024,768]{1,0:T(8,128)(2,1)} %get-tuple-element.138.refs_1_), custom_call_target="tpu_custom_call" | custom-call | flops 3019898880 | bytes 9928704 | tf_op jit(solution)/shard_map/pallas_call | solution.py:147
  145.1 9.7 %shard_map.296 = f32[16,48,1920]{2,1,0:T(8,128)} custom-call(s32[17]{0:T(128)} %pad_add_fusion.1.meta_ref, bf16[768,1024]{1,0:T(8,128)(2,1)} %get-tuple-element.134.turned_ref, bf16[1024,3072]{1,0:T(8,128)(2,1)} %get-tuple-element.142.rhs_ref, bf16[768,1024]{1,0:T(8,128)(2,1)} %get-tuple-element.137.refs_0_, bf16[1024,768]{1,0:T(8,128)(2,1)} %get-tuple-element.138.refs_1_), custom_call_target="tpu_custom_call" | custom-call | flops 3019898880 | bytes 9928704 | tf_op jit(solution)/shard_map/pallas_call | solution.py:147
  156.6 3.2 add_convert_fusion
  161.9 14.3 %shard_map.297 = (bf16[1024,2304]{1,0:T(8,128)(2,1)}, f32[8,768]{1,0:T(8,128)}) custom-call(bf16[1024,2304]{1,0:T(8,128)(2,1)} %get-tuple-element.131.qkv_ref, bf16[1024,768]{1,0:T(8,128)(2,1)} %get-tuple-element.148.dctx_ref, s32[8,1,128]{2,1,0:T(1,128)} %bitcast.30), custom_call_target="tpu_custom_call" | custom-call | flops 704643072 | bytes 5505024 | tf_op jit(solution)/shard_map/pallas_call | solution.py:815
  176.2 3.3 collective-permute-done.11
  185.3 14.3 %shard_map.298 = (bf16[1024,2304]{1,0:T(8,128)(2,1)}, f32[8,768]{1,0:T(8,128)}) custom-call(bf16[1024,2304]{1,0:T(8,128)(2,1)} %get-tuple-element.131.qkv_ref, bf16[1024,768]{1,0:T(8,128)(2,1)} %get-tuple-element.148.dctx_ref, s32[8,1,128]{2,1,0:T(1,128)} %bitcast.31, ...), custom_call_target="tpu_custom_call", output_to_operand_aliasing={{0}: (3, {})} | custom-call | flops 704643072 | bytes 5505024 | tf_op jit(solution)/shard_map/pallas_call | solution.py:815
  205.1 7.0 %shard_map.299 = bf16[16,48,1280]{2,1,0:T(8,128)(2,1)} custom-call(s32[17]{0:T(128)} %pad_add_fusion.2.meta_ref, bf16[768,1024]{1,0:T(8,128)(2,1)} %get-tuple-element.167.turned_ref, bf16[1024,2304]{1,0:T(8,128)(2,1)} %get-tuple-element.185.rhs_ref, f32[8,768]{1,0:T(8,128)} %get-tuple-element.169.refs_0_.refs_1_, ...), custom_call_target="tpu_custom_call" | custom-call | flops 2013265920 | bytes 7143424 | tf_op jit(solution)/shard_map/pallas_call | solution.py:147
  212.1 8.8 %collective-permute-done.14 = bf16[2,48,1536]{2,1,0:T(8,128)(2,1)S(1)} collective-permute-done((bf16[2,48,1536]{2,1,0:T(8,128)(2,1)S(1)}, bf16[2,48,1536]{2,1,0:T(8,128)(2,1)S(1)}, u32[]{:S(2)}, u32[]{:S(2)}) %collective-permute-start.14) | collective-permute-done | bytes 294944 | tf_op jit(solution)/shard_map/ppermute | solution.py:38
  224.9 7.6 %shard_map.300 = f32[16,48,1280]{2,1,0:T(8,128)} custom-call(s32[17]{0:T(128)} %pad_add_fusion.1.meta_ref, bf16[768,1024]{1,0:T(8,128)(2,1)} %get-tuple-element.167.turned_ref, bf16[1024,2304]{1,0:T(8,128)(2,1)} %get-tuple-element.185.rhs_ref, f32[8,768]{1,0:T(8,128)} %get-tuple-element.169.refs_0_.refs_1_, f32[8,768]{1,0:T(8,128)} %get-tuple-element.169.refs_0_.refs_1_, ...), custom_call_target="tpu_custom_call" | custom-call | flops 2013265920 | bytes 7143424 | tf_op jit(solution)/shard_map/pallas_call | solution.py:147
  232.5 3.2 collective-permute-done.16
  243.6 3.9 %fusion.1 = f32[1024,768]{1,0:T(8,128)S(1)} fusion(bf16[1024,2304]{1,0:T(8,128)(2,1)S(1)} %bitcast.18, bf16[768,2304]{1,0:T(8,128)(2,1)S(1)} %copy-done.9), kind=kOutput, calls=%fused_computation.50 | convolution fusion | flops 3623878656 | bytes 11403264 | tf_op jit(solution)/shard_map/ne,de->nd/dot_general | solution.py:941
  250.0 17.1 %collective-permute-done.21 = bf16[8,48,1280]{2,1,0:T(8,128)(2,1)S(1)} collective-permute-done((bf16[8,48,1280]{2,1,0:T(8,128)(2,1)S(1)}, bf16[8,48,1280]{2,1,0:T(8,128)(2,1)S(1)}, u32[]{:S(2)}, u32[]{:S(2)}) %collective-permute-start.21) | collective-permute-done | bytes 983072 | tf_op jit(solution)/shard_map/ppermute | solution.py:38
  268.5 8.8 %collective-permute-done.22 = bf16[4,48,1280]{2,1,0:T(8,128)(2,1)S(1)} collective-permute-done((bf16[4,48,1280]{2,1,0:T(8,128)(2,1)S(1)}, bf16[4,48,1280]{2,1,0:T(8,128)(2,1)S(1)}, u32[]{:S(2)}, u32[]{:S(2)}) %collective-permute-start.22) | collective-permute-done | bytes 491552 | tf_op jit(solution)/shard_map/ppermute | solution.py:38
  281.5 12.7 %collective-permute-done.23 = bf16[2,48,1280]{2,1,0:T(8,128)(2,1)S(1)} collective-permute-done((bf16[2,48,1280]{2,1,0:T(8,128)(2,1)S(1)}, bf16[2,48,1280]{2,1,0:T(8,128)(2,1)S(1)}, u32[]{:S(2)}, u32[]{:S(2)}) %collective-permute-start.23) | collective-permute-done | bytes 245792 | tf_op jit(solution)/shard_map/ppermute | solution.py:38
  295.3 3.2 collective-permute-done.30
  301.8 6.2 %collective-permute-done.25 = bf16[1,48,1280]{2,1,0:T(8,128)(2,1)S(1)} collective-permute-done((bf16[1,48,1280]{2,1,0:T(8,128)(2,1)S(1)}, bf16[1,48,1280]{2,1,0:T(8,128)(2,1)S(1)}, u32[]{:S(2)}, u32[]{:S(2)}) %collective-permute-start.25) | collective-permute-done | bytes 122912 | tf_op jit(solution)/shard_map/ppermute | solution.py:38
  308.1 4.7 %collective-permute-done.31 = bf16[4,48,1920]{2,1,0:T(8,128)(2,1)S(1)} collective-permute-done((bf16[4,48,1920]{2,1,0:T(8,128)(2,1)S(1)}, bf16[4,48,1920]{2,1,0:T(8,128)(2,1)S(1)}, u32[]{:S(2)}, u32[]{:S(2)}) %collective-permute-start.31) | collective-permute-done | bytes 737312 | tf_op jit(solution)/shard_map/ppermute | solution.py:38
  319.9 6.5 %collective-permute-done.27 = bf16[4,48,1280]{2,1,0:T(8,128)(2,1)S(1)} collective-permute-done((bf16[4,48,1280]{2,1,0:T(8,128)(2,1)S(1)}, bf16[4,48,1280]{2,1,0:T(8,128)(2,1)S(1)}, u32[]{:S(2)}, u32[]{:S(2)}) %collective-permute-start.27) | collective-permute-done | bytes 491552 | tf_op jit(solution)/shard_map/ppermute | solution.py:38
  327.3 5.8 %collective-permute-done.32 = bf16[8,48,1920]{2,1,0:T(8,128)(2,1)S(1)} collective-permute-done((bf16[8,48,1920]{2,1,0:T(8,128)(2,1)S(1)}, bf16[8,48,1920]{2,1,0:T(8,128)(2,1)S(1)}, u32[]{:S(2)}, u32[]{:S(2)}) %collective-permute-start.32) | collective-permute-done | bytes 1474592 | tf_op jit(solution)/shard_map/ppermute | solution.py:38
  337.4 6.2 %collective-permute-done.28 = bf16[8,48,1280]{2,1,0:T(8,128)(2,1)S(1)} collective-permute-done((bf16[8,48,1280]{2,1,0:T(8,128)(2,1)S(1)}, bf16[8,48,1280]{2,1,0:T(8,128)(2,1)S(1)}, u32[]{:S(2)}, u32[]{:S(2)}) %collective-permute-start.28) | collective-permute-done | bytes 983072 | tf_op jit(solution)/shard_map/ppermute | solution.py:38
  345.4 10.6 %shard_map.303 = f32[3072,768]{1,0:T(8,128)} custom-call(s32[33]{0:T(128)} %pad_add_fusion.3.meta_ref, bf16[16,48,1536]{2,1,0:T(8,128)(2,1)} %copy-done.1, bf16[16,48,1536]{2,1,0:T(8,128)(2,1)} %collective-permute-done.34.theirs_ref), custom_call_target="tpu_custom_call" | custom-call | bytes 14155776 | tf_op jit(solution)/shard_map/pallas_call | solution.py:256
  356.0 6.1 %shard_map.301 = (f32[768,2304]{1,0:T(8,128)}, f32[768]{0:T(1024)}, f32[768]{0:T(1024)}, f32[768]{0:T(1024)}, f32[768]{0:T(1024)}, /*index=5*/f32[768]{0:T(1024)...) custom-call(s32[33]{0:T(128)} %pad_add_fusion.3.meta_ref, ...), custom_call_target="tpu_custom_call" | custom-call | bytes 11796480 | tf_op jit(solution)/shard_map/pallas_call | solution.py:221
  362.1 7.9 %shard_map.302 = (f32[768,3072]{1,0:T(8,128)}, f32[768,768]{1,0:T(8,128)}) custom-call(s32[33]{0:T(128)} %pad_add_fusion.3.meta_ref, bf16[16,48,1920]{2,1,0:T(8,128)(2,1)} %constant_dynamic-update-slice_fusion.5.mine_ref, bf16[16,48,1920]{2,1,0:T(8,128)(2,1)} %collective-permute-done.33.theirs_ref), custom_call_target="tpu_custom_call" | custom-call | bytes 17694720 | tf_op jit(solution)/shard_map/pallas_call | solution.py:221
  (135 shorter events, 81.5 us)
Async XLA Ops:
  44.2 6.0 %collective-permute-start = (bf16[64,768]{1,0:T(8,128)(2,1)}, bf16[64,768]{1,0:T(8,128)(2,1)S(1)}, u32[]{:S(2)}, u32[]{:S(2)}) collective-permute-start(bf16[64,768]{1,0:T(8,128)(2,1)} %get-tuple-element.112.pool_ref), channel_id=1, source_target_pairs={{0,16},{16,0},{1,17},{17,1},{2,18},{18,2},{3,19},{19,3},{4,20},{20... | collective-permute-start | bytes 294920 | tf_op jit(solution)/shard_map/ppermute | solution.py:329
  54.9 8.8 %collective-permute-start.2 = (bf16[2,64,768]{2,1,0:T(8,128)(2,1)S(1)}, bf16[2,64,768]{2,1,0:T(8,128)(2,1)S(1)}, u32[]{:S(2)}, u32[]{:S(2)}) collective-permute-start(bf16[2,64,768]{2,1,0:T(8,128)(2,1)S(1)} %pad_maximum_fusion.11), channel_id=1, source_target_pairs={{0,8},{1,5},{2,10},{3,7},{4,12},{5,1},{6,14},{7,3},{8,0},{9,13},{1... | collective-permute-start | bytes 589832 | tf_op jit(solution)/shard_map/ppermute | solution.py:38
  63.7 7.8 %collective-permute-start.3 = (bf16[4,64,768]{2,1,0:T(8,128)(2,1)S(1)}, bf16[4,64,768]{2,1,0:T(8,128)(2,1)S(1)}, u32[]{:S(2)}, u32[]{:S(2)}) collective-permute-start(bf16[4,64,768]{2,1,0:T(8,128)(2,1)S(1)} %pad_maximum_fusion.7), channel_id=1, source_target_pairs={{0,4},{1,3},{2,6},{3,1},{4,0},{5,7},{6,2},{7,5},{8,12},{9,11},{10,... | collective-permute-start | bytes 1179656 | tf_op jit(solution)/shard_map/ppermute | solution.py:38
  91.5 8.8 %collective-permute-start.5 = (bf16[16,48,1536]{2,1,0:T(8,128)(2,1)}, bf16[16,48,1536]{2,1,0:T(8,128)(2,1)S(1)}, u32[]{:S(2)}, u32[]{:S(2)}) collective-permute-start(bf16[16,48,1536]{2,1,0:T(8,128)(2,1)} %shard_map.292), channel_id=1, source_target_pairs={{0,1},{1,0},{2,3},{3,2},{4,5},{5,4},{6,7},{7,6},{8,9},{9,8},{10,11... | collective-permute-start | bytes 7077896 | tf_op jit(solution)/shard_map/ppermute | solution.py:42
  104.2 24.3 %collective-permute-start.6 = (bf16[8,48,1536]{2,1,0:T(8,128)(2,1)}, bf16[8,48,1536]{2,1,0:T(8,128)(2,1)}, u32[]{:S(2)}, u32[]{:S(2)}) collective-permute-start(bf16[8,48,1536]{2,1,0:T(8,128)(2,1)} %add_convert_fusion.1), channel_id=1, source_target_pairs={{0,16},{1,3},{2,18},{3,1},{4,20},{5,7},{6,22},{7,5},{8,24},{9,11},... | collective-permute-start | bytes 3538952 | tf_op jit(solution)/shard_map/ppermute | solution.py:38
  129.8 10.0 %collective-permute-start.7 = (bf16[4,48,1536]{2,1,0:T(8,128)(2,1)S(1)}, bf16[4,48,1536]{2,1,0:T(8,128)(2,1)S(1)}, u32[]{:S(2)}, u32[]{:S(2)}) collective-permute-start(bf16[4,48,1536]{2,1,0:T(8,128)(2,1)S(1)} %add_convert_fusion.4), channel_id=1, source_target_pairs={{0,4},{1,17},{2,6},{3,19},{4,0},{5,21},{6,2},{7,23},{8,12},{9,25},... | collective-permute-start | bytes 1769480 | tf_op jit(solution)/shard_map/ppermute | solution.py:38
  141.7 13.1 %collective-permute-start.9 = (bf16[16,48,1920]{2,1,0:T(8,128)(2,1)}, bf16[16,48,1920]{2,1,0:T(8,128)(2,1)S(1)}, u32[]{:S(2)}, u32[]{:S(2)}) collective-permute-start(bf16[16,48,1920]{2,1,0:T(8,128)(2,1)} %shard_map.295), channel_id=1, source_target_pairs={{0,1},{1,0},{2,3},{3,2},{4,5},{5,4},{6,7},{7,6},{8,9},{9,8},{10,11... | collective-permute-start | bytes 8847368 | tf_op jit(solution)/shard_map/ppermute | solution.py:42
  142.2 12.6 %collective-permute-start.8 = (bf16[2,48,1536]{2,1,0:T(8,128)(2,1)}, bf16[2,48,1536]{2,1,0:T(8,128)(2,1)}, u32[]{:S(2)}, u32[]{:S(2)}) collective-permute-start(bf16[2,48,1536]{2,1,0:T(8,128)(2,1)} %add_convert_fusion.7), channel_id=1, source_target_pairs={{0,8},{1,5},{2,10},{3,7},{4,12},{5,1},{6,14},{7,3},{8,0},{9,13},{1... | collective-permute-start | bytes 884744 | tf_op jit(solution)/shard_map/ppermute | solution.py:38
  159.8 19.7 %collective-permute-start.11 = (bf16[8,48,1920]{2,1,0:T(8,128)(2,1)}, bf16[8,48,1920]{2,1,0:T(8,128)(2,1)}, u32[]{:S(2)}, u32[]{:S(2)}) collective-permute-start(bf16[8,48,1920]{2,1,0:T(8,128)(2,1)} %add_convert_fusion), channel_id=1, source_target_pairs={{0,16},{1,3},{2,18},{3,1},{4,20},{5,7},{6,22},{7,5},{8,24},{9,11},... | collective-permute-start | bytes 4423688 | tf_op jit(solution)/shard_map/ppermute | solution.py:38
  160.4 15.8 %collective-permute-start.10 = (bf16[1,48,1536]{2,1,0:T(8,128)(2,1)}, bf16[1,48,1536]{2,1,0:T(8,128)(2,1)}, u32[]{:S(2)}, u32[]{:S(2)}) collective-permute-start(bf16[1,48,1536]{2,1,0:T(8,128)(2,1)} %add_convert_fusion.12), channel_id=1, source_target_pairs={{0,2},{1,9},{2,0},{3,11},{4,6},{5,13},{6,4},{7,15},{8,10},{9,1},{1... | collective-permute-start | bytes 442376 | tf_op jit(solution)/shard_map/ppermute | solution.py:38
  183.2 16.4 %collective-permute-start.13 = (bf16[4,48,1920]{2,1,0:T(8,128)(2,1)S(1)}, bf16[4,48,1920]{2,1,0:T(8,128)(2,1)S(1)}, u32[]{:S(2)}, u32[]{:S(2)}) collective-permute-start(bf16[4,48,1920]{2,1,0:T(8,128)(2,1)S(1)} %add_convert_fusion.3), channel_id=1, source_target_pairs={{0,4},{1,17},{2,6},{3,19},{4,0},{5,21},{6,2},{7,23},{8,12},{9,25},... | collective-permute-start | bytes 2211848 | tf_op jit(solution)/shard_map/ppermute | solution.py:38
  184.4 15.2 %collective-permute-start.12 = (bf16[1,48,1536]{2,1,0:T(8,128)(2,1)}, bf16[1,48,1536]{2,1,0:T(8,128)(2,1)S(1)}, u32[]{:S(2)}, u32[]{:S(2)}) collective-permute-start(bf16[1,48,1536]{2,1,0:T(8,128)(2,1)} %add_convert_fusion.11), channel_id=1, source_target_pairs={{0,2},{1,9},{2,0},{3,11},{4,6},{5,13},{6,4},{7,15},{8,10},{9,1},{1... | collective-permute-start | bytes 442376 | tf_op jit(solution)/shard_map/ppermute | solution.py:38
  202.1 18.8 %collective-permute-start.15 = (bf16[2,48,1920]{2,1,0:T(8,128)(2,1)S(1)}, bf16[2,48,1920]{2,1,0:T(8,128)(2,1)S(1)}, u32[]{:S(2)}, u32[]{:S(2)}) collective-permute-start(bf16[2,48,1920]{2,1,0:T(8,128)(2,1)S(1)} %add_convert_fusion.6), channel_id=1, source_target_pairs={{0,8},{1,5},{2,10},{3,7},{4,12},{5,1},{6,14},{7,3},{8,0},{9,13},{1... | collective-permute-start | bytes 1105928 | tf_op jit(solution)/shard_map/ppermute | solution.py:38
  203.6 17.3 %collective-permute-start.14 = (bf16[2,48,1536]{2,1,0:T(8,128)(2,1)S(1)}, bf16[2,48,1536]{2,1,0:T(8,128)(2,1)S(1)}, u32[]{:S(2)}, u32[]{:S(2)}) collective-permute-start(bf16[2,48,1536]{2,1,0:T(8,128)(2,1)S(1)} %pad_maximum_fusion.9), channel_id=1, source_target_pairs={{0,8},{1,5},{2,10},{3,7},{4,12},{5,1},{6,14},{7,3},{8,0},{9,13},{1... | collective-permute-start | bytes 884744 | tf_op jit(solution)/shard_map/ppermute | solution.py:38
  223.7 12.0 %collective-permute-start.18 = (bf16[16,48,1280]{2,1,0:T(8,128)(2,1)}, bf16[16,48,1280]{2,1,0:T(8,128)(2,1)}, u32[]{:S(2)}, u32[]{:S(2)}) collective-permute-start(bf16[16,48,1280]{2,1,0:T(8,128)(2,1)} %shard_map.299), channel_id=1, source_target_pairs={{0,1},{1,0},{2,3},{3,2},{4,5},{5,4},{6,7},{7,6},{8,9},{9,8},{10,11... | collective-permute-start | bytes 5898248 | tf_op jit(solution)/shard_map/ppermute | solution.py:42
  223.7 12.0 %collective-permute-start.16 = (bf16[4,48,1536]{2,1,0:T(8,128)(2,1)S(1)}, bf16[4,48,1536]{2,1,0:T(8,128)(2,1)}, u32[]{:S(2)}, u32[]{:S(2)}) collective-permute-start(bf16[4,48,1536]{2,1,0:T(8,128)(2,1)S(1)} %pad_maximum_fusion.5), channel_id=1, source_target_pairs={{0,4},{1,17},{2,6},{3,19},{4,0},{5,21},{6,2},{7,23},{8,12},{9,25},... | collective-permute-start | bytes 1769480 | tf_op jit(solution)/shard_map/ppermute | solution.py:38
  223.7 8.8 %collective-permute-start.17 = (bf16[1,48,1920]{2,1,0:T(8,128)(2,1)}, bf16[1,48,1920]{2,1,0:T(8,128)(2,1)}, u32[]{:S(2)}, u32[]{:S(2)}) collective-permute-start(bf16[1,48,1920]{2,1,0:T(8,128)(2,1)} %add_convert_fusion.10), channel_id=1, source_target_pairs={{0,2},{1,9},{2,0},{3,11},{4,6},{5,13},{6,4},{7,15},{8,10},{9,1},{1... | collective-permute-start | bytes 552968 | tf_op jit(solution)/shard_map/ppermute | solution.py:38
  240.4 26.8 %collective-permute-start.19 = (bf16[8,48,1536]{2,1,0:T(8,128)(2,1)S(1)}, bf16[8,48,1536]{2,1,0:T(8,128)(2,1)S(1)}, u32[]{:S(2)}, u32[]{:S(2)}) collective-permute-start(bf16[8,48,1536]{2,1,0:T(8,128)(2,1)S(1)} %pad_maximum_fusion.1), channel_id=1, source_target_pairs={{0,16},{1,3},{2,18},{3,1},{4,20},{5,7},{6,22},{7,5},{8,24},{9,11},... | collective-permute-start | bytes 3538952 | tf_op jit(solution)/shard_map/ppermute | solution.py:38
  241.0 26.2 %collective-permute-start.21 = (bf16[8,48,1280]{2,1,0:T(8,128)(2,1)S(1)}, bf16[8,48,1280]{2,1,0:T(8,128)(2,1)S(1)}, u32[]{:S(2)}, u32[]{:S(2)}) collective-permute-start(bf16[8,48,1280]{2,1,0:T(8,128)(2,1)S(1)} %add_convert_fusion.2), channel_id=1, source_target_pairs={{0,16},{1,3},{2,18},{3,1},{4,20},{5,7},{6,22},{7,5},{8,24},{9,11},... | collective-permute-start | bytes 2949128 | tf_op jit(solution)/shard_map/ppermute | solution.py:38
  242.5 7.6 %collective-permute-start.20 = (bf16[1,48,1920]{2,1,0:T(8,128)(2,1)S(1)}, bf16[1,48,1920]{2,1,0:T(8,128)(2,1)S(1)}, u32[]{:S(2)}, u32[]{:S(2)}) collective-permute-start(bf16[1,48,1920]{2,1,0:T(8,128)(2,1)S(1)} %add_convert_fusion.9), channel_id=1, source_target_pairs={{0,2},{1,9},{2,0},{3,11},{4,6},{5,13},{6,4},{7,15},{8,10},{9,1},{1... | collective-permute-start | bytes 552968 | tf_op jit(solution)/shard_map/ppermute | solution.py:38
  268.4 8.9 %collective-permute-start.22 = (bf16[4,48,1280]{2,1,0:T(8,128)(2,1)S(1)}, bf16[4,48,1280]{2,1,0:T(8,128)(2,1)S(1)}, u32[]{:S(2)}, u32[]{:S(2)}) collective-permute-start(bf16[4,48,1280]{2,1,0:T(8,128)(2,1)S(1)} %add_convert_fusion.5), channel_id=1, source_target_pairs={{0,4},{1,17},{2,6},{3,19},{4,0},{5,21},{6,2},{7,23},{8,12},{9,25},... | collective-permute-start | bytes 1474568 | tf_op jit(solution)/shard_map/ppermute | solution.py:38
  278.4 15.8 %collective-permute-start.23 = (bf16[2,48,1280]{2,1,0:T(8,128)(2,1)S(1)}, bf16[2,48,1280]{2,1,0:T(8,128)(2,1)S(1)}, u32[]{:S(2)}, u32[]{:S(2)}) collective-permute-start(bf16[2,48,1280]{2,1,0:T(8,128)(2,1)S(1)} %add_convert_fusion.8), channel_id=1, source_target_pairs={{0,8},{1,5},{2,10},{3,7},{4,12},{5,1},{6,14},{7,3},{8,0},{9,13},{1... | collective-permute-start | bytes 737288 | tf_op jit(solution)/shard_map/ppermute | solution.py:38
  278.5 20.0 %collective-permute-start.30 = (bf16[2,48,1920]{2,1,0:T(8,128)(2,1)S(1)}, bf16[2,48,1920]{2,1,0:T(8,128)(2,1)S(1)}, u32[]{:S(2)}, u32[]{:S(2)}) collective-permute-start(bf16[2,48,1920]{2,1,0:T(8,128)(2,1)S(1)} %pad_maximum_fusion.8), channel_id=1, source_target_pairs={{0,8},{1,5},{2,10},{3,7},{4,12},{5,1},{6,14},{7,3},{8,0},{9,13},{1... | collective-permute-start | bytes 1105928 | tf_op jit(solution)/shard_map/ppermute | solution.py:38
  298.5 14.2 %collective-permute-start.31 = (bf16[4,48,1920]{2,1,0:T(8,128)(2,1)S(1)}, bf16[4,48,1920]{2,1,0:T(8,128)(2,1)S(1)}, u32[]{:S(2)}, u32[]{:S(2)}) collective-permute-start(bf16[4,48,1920]{2,1,0:T(8,128)(2,1)S(1)} %pad_maximum_fusion.4), channel_id=1, source_target_pairs={{0,4},{1,17},{2,6},{3,19},{4,0},{5,21},{6,2},{7,23},{8,12},{9,25},... | collective-permute-start | bytes 2211848 | tf_op jit(solution)/shard_map/ppermute | solution.py:38
  301.8 6.2 %collective-permute-start.25 = (bf16[1,48,1280]{2,1,0:T(8,128)(2,1)S(1)}, bf16[1,48,1280]{2,1,0:T(8,128)(2,1)S(1)}, u32[]{:S(2)}, u32[]{:S(2)}) collective-permute-start(bf16[1,48,1280]{2,1,0:T(8,128)(2,1)S(1)} %get-tuple-element.208), channel_id=1, source_target_pairs={{0,2},{1,9},{2,0},{3,11},{4,6},{5,13},{6,4},{7,15},{8,10},{9,1},{1... | collective-permute-start | bytes 368648 | tf_op jit(solution)/shard_map/ppermute | solution.py:38
  308.0 9.5 %collective-permute-start.26 = (bf16[2,48,1280]{2,1,0:T(8,128)(2,1)S(1)}, bf16[2,48,1280]{2,1,0:T(8,128)(2,1)S(1)}, u32[]{:S(2)}, u32[]{:S(2)}) collective-permute-start(bf16[2,48,1280]{2,1,0:T(8,128)(2,1)S(1)} %pad_maximum_fusion.10), channel_id=1, source_target_pairs={{0,8},{1,5},{2,10},{3,7},{4,12},{5,1},{6,14},{7,3},{8,0},{9,13},{1... | collective-permute-start | bytes 737288 | tf_op jit(solution)/shard_map/ppermute | solution.py:38
  312.9 20.2 %collective-permute-start.32 = (bf16[8,48,1920]{2,1,0:T(8,128)(2,1)S(1)}, bf16[8,48,1920]{2,1,0:T(8,128)(2,1)S(1)}, u32[]{:S(2)}, u32[]{:S(2)}) collective-permute-start(bf16[8,48,1920]{2,1,0:T(8,128)(2,1)S(1)} %pad_maximum_fusion), channel_id=1, source_target_pairs={{0,16},{1,3},{2,18},{3,1},{4,20},{5,7},{6,22},{7,5},{8,24},{9,11},... | collective-permute-start | bytes 4423688 | tf_op jit(solution)/shard_map/ppermute | solution.py:38
  317.5 8.9 %collective-permute-start.27 = (bf16[4,48,1280]{2,1,0:T(8,128)(2,1)S(1)}, bf16[4,48,1280]{2,1,0:T(8,128)(2,1)S(1)}, u32[]{:S(2)}, u32[]{:S(2)}) collective-permute-start(bf16[4,48,1280]{2,1,0:T(8,128)(2,1)S(1)} %pad_maximum_fusion.6), channel_id=1, source_target_pairs={{0,4},{1,17},{2,6},{3,19},{4,0},{5,21},{6,2},{7,23},{8,12},{9,25},... | collective-permute-start | bytes 1474568 | tf_op jit(solution)/shard_map/ppermute | solution.py:38
  326.5 17.1 %collective-permute-start.28 = (bf16[8,48,1280]{2,1,0:T(8,128)(2,1)S(1)}, bf16[8,48,1280]{2,1,0:T(8,128)(2,1)S(1)}, u32[]{:S(2)}, u32[]{:S(2)}) collective-permute-start(bf16[8,48,1280]{2,1,0:T(8,128)(2,1)S(1)} %pad_maximum_fusion.2), channel_id=1, source_target_pairs={{0,16},{1,3},{2,18},{3,1},{4,20},{5,7},{6,22},{7,5},{8,24},{9,11},... | collective-permute-start | bytes 2949128 | tf_op jit(solution)/shard_map/ppermute | solution.py:38
  334.4 27.8 %collective-permute-start.33 = (bf16[16,48,1920]{2,1,0:T(8,128)(2,1)}, bf16[16,48,1920]{2,1,0:T(8,128)(2,1)}, u32[]{:S(2)}, u32[]{:S(2)}) collective-permute-start(bf16[16,48,1920]{2,1,0:T(8,128)(2,1)} %constant_dynamic-update-slice_fusion.5.mine_ref), channel_id=1, source_target_pairs={{0,1},{1,0},{2,3},{3,2},{4,5},{5,4},{6,7},{7,6},{8,9},{9,8},{10,11... | collective-permute-start | bytes 8847368 | tf_op jit(solution)/shard_map/ppermute | solution.py:42
  334.5 10.9 %collective-permute-start.34 = (bf16[16,48,1536]{2,1,0:T(8,128)(2,1)S(1)}, bf16[16,48,1536]{2,1,0:T(8,128)(2,1)}, u32[]{:S(2)}, u32[]{:S(2)}) collective-permute-start(bf16[16,48,1536]{2,1,0:T(8,128)(2,1)S(1)} %constant_dynamic-update-slice_fusion.10.mine_ref), channel_id=1, source_target_pairs={{0,1},{1,0},{2,3},{3,2},{4,5},{5,4},{6,7},{7,6},{8,9},{9,8},{10,11... | collective-permute-start | bytes 7077896 | tf_op jit(solution)/shard_map/ppermute | solution.py:42
  344.6 11.4 %collective-permute-start.29 = (bf16[16,48,1280]{2,1,0:T(8,128)(2,1)}, bf16[16,48,1280]{2,1,0:T(8,128)(2,1)}, u32[]{:S(2)}, u32[]{:S(2)}) collective-permute-start(bf16[16,48,1280]{2,1,0:T(8,128)(2,1)} %constant_dynamic-update-slice_fusion.mine_ref), channel_id=1, source_target_pairs={{0,1},{1,0},{2,3},{3,2},{4,5},{5,4},{6,7},{7,6},{8,9},{9,8},{10,11... | collective-permute-start | bytes 5898248 | tf_op jit(solution)/shard_map/ppermute | solution.py:42
  (17 other events, 231.3 us)
